TPU v7x, 32 devices: a whole 2x2x4 slice. The times are simulated.
32 devices in a mesh: member: 4 (over x, core), space: 8 (over z, y).
Axes of the slice: x: 2, y: 2, z: 4, core: 2. Of those that a mesh axis runs over, the one named last changes fastest.
Arguments:
- spectra: float32 [16, 12, 320, 641], P('member', None, 'space'), may hold values from -6 to 6
- legendre: bfloat16 [320, 641, 384], P('space'), as said below
- sin_lat: float32 [384], replicated, may hold values from 0 to 1, as said below
- gravity: float32 [2, 2], replicated, may hold values from 0.1 to 2, as said below
- stability: float32 [2, 2], replicated, may hold values from 0.1 to 2, as said below
- clones: int32 [2, 2], replicated, may hold values from 0 to 15, as said below
Outputs:
- new_state: float32 [16, 12, 320, 641], P('member', None, 'space')
Inputs may be any that keep to these rules, and one draw needn't show every extreme that they name: `clones`: column 0 holds 2 distinct killed trajectories, column 1 for each a survivor; no survivor is killed, and a survivor may be copied onto several killed trajectories. legendre[p, j, l] is the associated Legendre function of the (m, n) of position (p, j), normalized so that its square integrates to one over -1 to 1, at mu = sin_lat[l]. `sin_lat`: decreasing from the pole towards the equator. `gravity`: diagonal entries 1 to 2, off-diagonal entries 0.1 to 0.6. `stability`: diagonal entries 1 to 2, off-diagonal entries 0.1 to 0.6.
All inputs are finite; a program needn't handle non-finite values.
Results may differ from a plain program's by a relative error of at most 0.0016.
Values may be sent and summed in bfloat16 or wider, within the bound.
No kernel may reach another device: no remote copies, remote signals or barrier semaphores. Data moves between devices by JAX's collectives and lax.ppermute only.
A program may use at most 192 MiB of HBM per device.

v0:
```python
import math

import jax
import jax.numpy as jnp
from jax import lax
from jax.sharding import PartitionSpec as P

NLON = 1280


time_step = 0.25
wave_scale = 16.0
diffusion = 0.02


def from_root(value, axis, root):
    mine = lax.axis_index(axis) == root
    return lax.psum(jnp.where(mine, value, jnp.zeros_like(value)), axis)


def pair_layout(pair_index, row_length, truncation):
    column = jnp.arange(row_length, dtype=jnp.int32)[None, :]
    lower_pair = pair_index[:, None]
    leading = column < truncation - lower_pair
    wave_order = jnp.where(leading, lower_pair, truncation - 1 - lower_pair)
    offset = jnp.where(leading, column, column - (truncation - lower_pair))
    parity = (1 - 2 * (offset % 2)).astype(jnp.float32)
    return (leading.astype(jnp.float32), parity, wave_order + offset)


def fourier_table(pair_count, truncation, longitudes):
    halves = jnp.arange(2, dtype=jnp.int32)[:, None]
    pair_all = jnp.arange(pair_count, dtype=jnp.int32)[None, :]
    wave_order = jnp.where(halves == 0, pair_all, truncation - 1 - pair_all)
    column = jnp.arange(longitudes, dtype=jnp.int32)
    phase = wave_order[:, :, None] * column[None, None, :] % longitudes
    angle = phase.astype(jnp.float32) * (2.0 * math.pi / longitudes)
    return jnp.stack([jnp.cos(angle), -jnp.sin(angle)]).astype(jnp.bfloat16)


def latitude_terms(sin_lat, first_row, count):
    mirrored = jnp.concatenate([sin_lat, -sin_lat])
    local_sine = lax.dynamic_slice_in_dim(mirrored, first_row, count)
    weights = math.pi * jnp.sqrt(1.0 - local_sine * local_sine) / mirrored.shape[0]
    return (2.0 * local_sine, weights)


def tendencies(physical_grid_samples, coriolis):
    local_spin_spectrum = physical_grid_samples[:, 0:2]
    spreading_rate_spectrum = physical_grid_samples[:, 2:4]
    thermal_spectrum = physical_grid_samples[:, 4:6]
    planetary_spin_spectrum = local_spin_spectrum + coriolis[:, None]
    average_heat_level = 0.5 * (thermal_spectrum[:, 0:1] + thermal_spectrum[:, 1:2])
    return jnp.concatenate(
        [
            -planetary_spin_spectrum * spreading_rate_spectrum,
            planetary_spin_spectrum * local_spin_spectrum
            - 0.5 * spreading_rate_spectrum * spreading_rate_spectrum,
            -(thermal_spectrum + average_heat_level) * spreading_rate_spectrum,
        ],
        axis=1,
    )


def semi_implicit(spectra, tendency, degree, gravity, stability):
    trajectory_count, comp_count, pair_count, row_length = spectra.shape
    truncation = row_length - 1
    shaped = spectra.reshape(trajectory_count, comp_count // 2, 2, pair_count, row_length)
    forcing = tendency.reshape(trajectory_count, comp_count // 2, 2, pair_count, row_length)
    eigen_value = (
        wave_scale * (degree * (degree + 1)).astype(jnp.float32) / float(truncation * truncation)
    )
    damping = 1.0 / (1.0 + diffusion * eigen_value * eigen_value)
    coupling = time_step * time_step * eigen_value
    product = jnp.dot(gravity, stability, precision=lax.Precision.HIGHEST)
    new_zeta = damping * (shaped[:, 0:2] + time_step * forcing[:, 0:2])
    t_star = shaped[:, 4:6] + time_step * forcing[:, 4:6]
    d_star = shaped[:, 2:4] + time_step * forcing[:, 2:4]
    right_one = d_star[:, 0] + time_step * eigen_value * (
        gravity[0, 0] * t_star[:, 0] + gravity[0, 1] * t_star[:, 1]
    )
    right_two = d_star[:, 1] + time_step * eigen_value * (
        gravity[1, 0] * t_star[:, 0] + gravity[1, 1] * t_star[:, 1]
    )
    diag_one = 1.0 + coupling * product[0, 0]
    diag_two = 1.0 + coupling * product[1, 1]
    cross_one = coupling * product[0, 1]
    cross_two = coupling * product[1, 0]
    determ = diag_one * diag_two - cross_one * cross_two
    div_one = (diag_two * right_one - cross_one * right_two) / determ
    div_two = (diag_one * right_two - cross_two * right_one) / determ
    temp_one = damping * (
        t_star[:, 0] - time_step * (stability[0, 0] * div_one + stability[0, 1] * div_two)
    )
    temp_two = damping * (
        t_star[:, 1] - time_step * (stability[1, 0] * div_one + stability[1, 1] * div_two)
    )
    new_div = damping * jnp.stack([div_one, div_two], axis=1)
    new_temp = jnp.stack([temp_one, temp_two], axis=1)
    result = jnp.concatenate([new_zeta, new_div, new_temp], axis=1)
    return result.reshape(spectra.shape)


def advance(spectra, legendre, sin_lat, gravity, stability):
    trajectory_count, comp_count, pair_local, row_length = spectra.shape
    space_count = lax.axis_size("space")
    position = lax.axis_index("space")
    truncation = row_length - 1
    half_lat = legendre.shape[2]
    lat_count = 2 * half_lat
    lat_local = lat_count // space_count
    pair_total = pair_local * space_count
    pair_index = position * pair_local + jnp.arange(pair_local, dtype=jnp.int32)
    leading, parity, degree = pair_layout(pair_index, row_length, truncation)
    halves = jnp.stack([leading, 1.0 - leading])
    mirror_sign = jnp.stack([jnp.ones_like(parity), parity])
    factor = (halves[:, None] * mirror_sign[None, :]).astype(jnp.bfloat16)
    inputs = spectra.astype(jnp.bfloat16)[:, :, None, None] * factor[None, None]
    fourier = jnp.einsum("tchspj,pjl->tchpsl", inputs, legendre, preferred_element_type=jnp.float32)
    fourier = fourier.reshape(trajectory_count, comp_count, 2, pair_local, lat_count).astype(
        jnp.bfloat16
    )
    zonal_table = fourier_table(pair_total, truncation, NLON)
    coriolis, weights = latitude_terms(sin_lat, position * lat_local, lat_local)
    banded = lax.all_to_all(fourier, "space", split_axis=4, concat_axis=3, tiled=True)
    grid_banded = banded
    count_here = grid_banded.shape[0]
    grid_banded = grid_banded.reshape(count_here, comp_count // 2, 2, 2, pair_total, lat_local)
    physical_grid_samples = jnp.einsum(
        "tfrhpl,rhpk->tflk", grid_banded, zonal_table, preferred_element_type=jnp.float32
    ) * (1.0 / truncation)
    forcing = tendencies(physical_grid_samples, coriolis).astype(jnp.bfloat16)
    weighted = (
        jnp.einsum("tflk,rhpk->tfrhpl", forcing, zonal_table, preferred_element_type=jnp.float32)
        * weights
    )
    returned = lax.all_to_all(
        weighted.astype(jnp.bfloat16).reshape(count_here, comp_count, 2, pair_total, lat_local),
        "space",
        split_axis=3,
        concat_axis=4,
        tiled=True,
    )
    returned = returned.reshape(trajectory_count, comp_count, 2, pair_local, 2, half_lat).astype(
        jnp.float32
    )
    legendre_wide = legendre.astype(jnp.float32)
    projected = jnp.einsum(
        "tchpsl,pjl->tchspj", returned, legendre_wide, precision=lax.Precision.HIGHEST
    )
    first_part = projected[:, :, 0, 0] + parity * projected[:, :, 0, 1]
    second_part = projected[:, :, 1, 0] + parity * projected[:, :, 1, 1]
    tendency = leading * first_part + (1.0 - leading) * second_part
    return semi_implicit(spectra, tendency, degree, gravity, stability)


def copy_clones(field_values, clones):
    resident_rows = field_values.shape[0]
    ensemble_slot = lax.axis_index("member")
    row_numbers = jnp.arange(resident_rows, dtype=jnp.int32)

    def visit(entry, updated):
        removed_members = clones[entry, 0]
        sending_member = clones[entry, 1]
        owning_member = sending_member // resident_rows
        surviving_member = lax.dynamic_index_in_dim(
            field_values, sending_member % resident_rows, 0, keepdims=False
        )
        received_rows = from_root(surviving_member, "member", owning_member)
        is_mine = removed_members // resident_rows == ensemble_slot
        selected = jnp.logical_and(row_numbers == removed_members % resident_rows, is_mine)
        return jnp.where(selected[:, None, None, None], received_rows[None], updated)

    return lax.fori_loop(0, clones.shape[0], visit, field_values)


def shards(spectra, legendre, sin_lat, gravity, stability, clones):
    advanced_states = advance(spectra, legendre, sin_lat, gravity, stability)
    return copy_clones(advanced_states, clones)


def solution(mesh):
    placed = (P("member", None, "space", None), P("space", None, None), P(), P(), P(), P())
    return jax.shard_map(
        shards,
        mesh=mesh,
        in_specs=placed,
        out_specs=P("member", None, "space", None),
        check_vma=False,
    )
```

profile of v0, /device:TPU:0, one launch (start us, length us, event | category | flops | bytes accessed | tf_op | source)
XLA Modules:
  0.0 810.3 jit_solution(4045247310415176663)
XLA Ops:
  7.5 3.0 convert_element_type.116
  13.8 18.7 %convert_bitcast_fusion = bf16[4,12,2,40,2,384]{5,1,4,2,0,3:T(8,128)(2,1)} fusion(bf16[40,641,384,1,1,1]{2,0,1,5,4,3:T(8,128)(2,1)} %bitcast.86, bf16[2,2,40,641]{3,1,0,2:T(2,128)(2,1)S(1)} %multiply_convert_fusion.1, bf16[4,12,40,641]{3,1,0,2:T(8,128)(2,1)} %copy.44), kind=kOutput, calls=%fused_computation.17 | convolution fusion | flops 3788643840 | bytes 28256320 | tf_op jit(solution)/shard_map/tchspj,pjl->tchpsl/dot_general | solution.py:119
  32.4 40.7 %copy.72 = bf16[4,12,2,40,2,384]{3,2,1,0,5,4:T(2,128)(2,1)} copy(bf16[4,12,2,40,2,384]{5,1,4,2,0,3:T(8,128)(2,1)} %convert_bitcast_fusion) | data formatting | bytes 11796480 | tf_op jit(solution)/shard_map/convert_element_type | solution.py:120
  73.1 31.3 %reshape.951 = bf16[8,2,184320]{2,1,0:T(2,128)(2,1)} reshape(bf16[768,4,12,2,40]{4,3,2,1,0:T(2,128)(2,1)} %bitcast.70) | data formatting | bytes 11796480
  104.4 7.8 all-to-all-start
  112.4 15.0 %cosine_convert_fusion = (bf16[1,2,320,1280]{3,2,0,1:T(8,128)(2,1)S(1)}, bf16[1,2,320,1280]{3,2,0,1:T(8,128)(2,1)S(1)}) fusion(s32[2,320]{1,0:T(2,128)S(1)} %iota_select_fusion), kind=kLoop, calls=%fused_computation.45 | loop fusion | flops 9830400 | bytes 3279360 | tf_op jit(solution)/shard_map/convert.3
  127.4 114.5 %all-to-all-done = bf16[8,2,184320]{2,1,0:T(2,128)(2,1)} async-done(((bf16[8,2,184320]{2,1,0:T(2,128)(2,1)}), bf16[8,2,184320]{2,1,0:T(2,128)(2,1)}, u32[]{:S(2)}, u32[]{:S(2)}) %all-to-all-start) | async-done | bytes 5898272 | tf_op jit(solution)/shard_map/all_to_all | solution.py:125
  241.9 32.7 %reshape.952 = bf16[768,4,12,2,40]{4,3,2,1,0:T(2,128)(2,1)} reshape(bf16[8,2,184320]{2,1,0:T(2,128)(2,1)} %all-to-all-done) | data formatting | bytes 11796480
  274.6 40.8 %copy.48 = bf16[4,12,2,40,8,96]{5,3,4,2,1,0:T(8,128)(2,1)} copy(bf16[4,12,2,40,8,96]{3,2,1,0,5,4:T(2,128)(2,1)} %bitcast.71) | data formatting | bytes 11796480 | tf_op jit(solution)/shard_map/all_to_all | solution.py:125
  315.4 10.4 %bitcast_multiply_fusion = f32[4,6,96,1280]{3,2,1,0:T(8,128)S(1)} fusion(bf16[4,6,2,2,320,96]{5,4,3,2,1,0:T(8,128)(2,1)} %bitcast.79, bf16[1,2,320,1280]{3,2,0,1:T(8,128)(2,1)S(1)} %get-tuple-element.229, bf16[1,2,320,1280]{3,2,0,1:T(8,128)(2,1)S(1)} %get-tuple-element.228), kind=kOutput, calls=%fused_computation.13 | convolution fusion | flops 7554334720 | bytes 20971520 | tf_op jit(solution)/shard_map/tfrhpl,rhpk->tflk/dot_general | solution.py:129
  326.0 2.8 fusion.27
  328.8 10.9 %fusion.17 = bf16[4,6,2,2,320,96]{4,5,1,0,3,2:T(8,128)(2,1)S(1)} fusion(f32[96]{0:T(128)S(1)} %get-tuple-element.227, bf16[4,2,96,1280]{3,2,1,0:T(8,128)(2,1)} %get-tuple-element.223, bf16[4,2,96,1280]{3,2,1,0:T(8,128)(2,1)S(1)} %get-tuple-element.219, bf16[4,2,96,1280]{3,2,1,0:T(8,128)(2,1)S(1)} %get-tuple-element.218, ...), kind=kOutput, calls=%fused_computation.20 | convolution fusion | flops 7574978560 | bytes 15073664 | tf_op jit(solution)/shard_map/tflk,rhpk->tfrhpl/dot_general | solution.py:134
  339.7 4.3 copy.51
  344.0 32.6 %copy.52 = bf16[4,12,2,320,96]{4,2,1,0,3:T(2,128)(2,1)} copy(bf16[4,12,2,320,96]{3,4,2,1,0:T(8,128)(2,1)} %bitcast.80) | data formatting | bytes 11796480 | tf_op jit(solution)/shard_map/reshape | solution.py:138
  376.6 5.1 all-to-all-start.1
  386.6 166.1 %all-to-all-done.1 = bf16[4,12,2,320,96]{4,2,1,0,3:T(2,128)(2,1)} async-done(((bf16[4,12,2,320,96]{4,2,1,0,3:T(2,128)(2,1)}), bf16[4,12,2,320,96]{4,2,1,0,3:T(2,128)(2,1)}, u32[]{:S(2)}, u32[]{:S(2)}) %all-to-all-start.1) | async-done | bytes 5898272 | tf_op jit(solution)/shard_map/all_to_all | solution.py:137
  552.7 6.3 copy.53
  559.0 5.6 copy.54
  564.6 16.9 %reshape.943 = bf16[4,12,2,40,2,384]{5,4,3,2,1,0:T(2,128)(2,1)} reshape(bf16[4,12,2,40,8,96]{5,4,3,2,1,0:T(8,128)(2,1)} %copy.54) | data formatting | bytes 11796480 | tf_op jit(solution)/shard_map/reshape | solution.py:144
  581.5 35.2 %fusion.7 = f32[4,12,2,2,40,641]{5,1,3,2,0,4:T(8,128)} fusion(bf16[40,641,384,1,1,1]{2,0,1,5,4,3:T(8,128)(2,1)} %bitcast.87, bf16[4,12,2,40,2,384]{5,4,3,2,1,0:T(2,128)(2,1)} %reshape.943), kind=kOutput, calls=%fused_computation.12 | convolution fusion | flops 3780771840 | bytes 45281280 | tf_op jit(solution)/shard_map/tchpsl,pjl->tchspj/dot_general | solution.py:148
  616.7 22.6 %fusion.59 = (f32[4,12,1,1,40,641]{5,1,3,2,0,4:T(8,128)}, f32[4,12,1,1,40,641]{5,1,3,2,0,4:T(8,128)}, f32[4,12,1,1,40,641]{5,1,3,2,0,4:T(8,128)}, f32[4,12,1,1,40,641]{5,1,3,2,0,4:T(8,128)}) fusion(f32[4,12,2,2,40,641]{5,1,3,2,0,4:T(8,128)} %fusion.7), kind=kLoop, calls=%fused_computation.109 | loop fusion | bytes 39383040 | tf_op jit(solution)/shard_map/slice | solution.py:151
  639.3 9.3 %copy.57 = f32[4,12,1,1,40,641]{5,4,1,0,3,2:T(8,128)} copy(f32[4,12,1,1,40,641]{5,1,3,2,0,4:T(8,128)} %get-tuple-element.217) | data formatting | bytes 9845760 | tf_op jit(solution)/shard_map/slice | solution.py:151
  648.7 5.9 copy.58
  654.6 6.0 copy.59
  660.6 6.2 copy.60
  666.8 13.1 %multiply_add_fusion = f32[4,6,2,40,641]{4,3,2,1,0:T(8,128)} fusion(f32[4,6,2,40,641]{4,3,2,1,0:T(8,128)} %bitcast.83, f32[4,6,2,40,641]{4,3,2,1,0:T(8,128)} %bitcast.84, f32[4,6,2,40,641]{4,3,2,1,0:T(8,128)} %bitcast.81, f32[4,6,2,40,641]{4,3,2,1,0:T(8,128)} %bitcast.82, f32[40,641]{1,0:T(8,128)S(1)} %get-tuple-element.249, f32[40,641]{1,0:T(8,128)S(1)} %fusion.49, ...), kind=kLoop, calls=%fused_computation.27 | loop fusion | flops 8615040 | bytes 24922080 | tf_op jit(solution)/shard_map/add | solution.py:153
  679.9 5.6 fusion.42
  696.5 106.6 %while.17 = (s32[]{:T(128)}, f32[4,12,40,641]{3,2,1,0:T(8,128)}, s32[2,2]{1,0:T(2,128)S(1)}, s32[]{:T(128)}, f32[4,12,40,641]{3,2,1,0:T(8,128)}, /*index=5*/s32[...) while((s32[]{:T(128)}, f32[4,12,40,641]{3,2,1,0:T(8,128)}, ...), condition=%wide.region_2.3_spmd.clone, body=%wide.region_0.2_spmd.clone.sunk | while | flops 1846136 | bytes 21410572 | solution.py:174
  705.0 37.9 %all-reduce.3.cloned.1.call-done = f32[12,40,641]{2,1,0:T(8,128)} async-done(((f32[12,40,641]{2,1,0:T(8,128)}), f32[12,40,641]{2,1,0:T(8,128)}) %all-reduce.3.cloned.1.call-update) | async-done | bytes 1230736 | tf_op jit(solution)/shard_map/while/body/eval_jaxpr/psum | solution.py:18
  742.9 6.3 broadcast_select_fusion.2
  757.8 39.0 %all-reduce.3.cloned.1.call-done = f32[12,40,641]{2,1,0:T(8,128)} async-done(((f32[12,40,641]{2,1,0:T(8,128)}), f32[12,40,641]{2,1,0:T(8,128)}) %all-reduce.3.cloned.1.call-update) | async-done | bytes 1230736 | tf_op jit(solution)/shard_map/while/body/eval_jaxpr/psum | solution.py:18
  796.7 6.3 broadcast_select_fusion.2
  (61 shorter events, 24.6 us)
Async XLA Ops:
  104.4 7.8 copy-start.3
  104.4 137.5 %all-to-all-start = ((bf16[8,2,184320]{2,1,0:T(2,128)(2,1)}), bf16[8,2,184320]{2,1,0:T(2,128)(2,1)}, u32[]{:S(2)}, u32[]{:S(2)}) async-start(bf16[8,2,184320]{2,1,0:T(2,128)(2,1)} %reshape.951), calls=%async_computation | async-start | bytes 11796480 | tf_op jit(solution)/shard_map/all_to_all | solution.py:125
  376.6 5.1 copy-start.4
  376.6 5.1 copy-start.5
  376.6 176.1 %all-to-all-start.1 = ((bf16[4,12,2,320,96]{4,2,1,0,3:T(2,128)(2,1)}), bf16[4,12,2,320,96]{4,2,1,0,3:T(2,128)(2,1)}, u32[]{:S(2)}, u32[]{:S(2)}) async-start(bf16[4,12,2,320,96]{4,2,1,0,3:T(2,128)(2,1)} %copy.52), calls=%async_computation.1 | async-start | bytes 15728640 | tf_op jit(solution)/shard_map/all_to_all | solution.py:137
  639.3 9.4 %copy-start.1 = (f32[4,12,1,1,40,641]{5,1,3,2,0,4:T(8,128)S(1)}, f32[4,12,1,1,40,641]{5,1,3,2,0,4:T(8,128)}, u32[]{:S(2)}) copy-start(f32[4,12,1,1,40,641]{5,1,3,2,0,4:T(8,128)} %get-tuple-element.214) | copy-start | bytes 14768644
  639.3 15.3 %slice-start.2 = ((s8[7864320]{0:T(1024)(128)(4,1)}), s8[4194304]{0:T(1024)(128)(4,1)S(1)}, s32[]{:S(2)}) async-start(s8[7864320]{0:T(1024)(128)(4,1)} %bitcast.76), calls=%async_computation.5 | async-start | bytes 8388608
  648.7 5.9 slice-start.3
  648.7 11.9 %slice-start = ((s8[7864320]{0:T(1024)(128)(4,1)}), s8[4194304]{0:T(1024)(128)(4,1)S(1)}, s32[]{:S(2)}) async-start(s8[7864320]{0:T(1024)(128)(4,1)} %bitcast.74), calls=%async_computation.3 | async-start | bytes 8388608
  654.6 6.0 slice-start.1
  692.2 4.3 copy-start
  692.2 4.3 copy-start.2
  696.5 46.4 %all-reduce.3.cloned.1.call-start = ((), (), s32[]{:S(2)}) async-start(), calls=%async_computation.2 | async-start | bytes 2949120 | tf_op jit(solution)/shard_map/while/body/eval_jaxpr/psum | solution.py:18
  749.3 47.5 %all-reduce.3.cloned.1.call-start = ((), (), s32[]{:S(2)}) async-start(), calls=%async_computation.2 | async-start | bytes 2949120 | tf_op jit(solution)/shard_map/while/body/eval_jaxpr/psum | solution.py:18
Sparse Core Ops, SparseCore 0:
  702.4 40.4 all-reduce.2
  755.2 41.5 all-reduce.2
where the time goes:
time: 822 us; the launch traced here: 810 us
  waiting for transfers between devices  358 us (44%)
  local copies, waits for them, and re-layouts  271 us (33%)
  matrix products  75.2 us (9%)
  other arithmetic  66.3 us (8%)
  between operations  16.6 us (2%)
  starting transfers between devices  12.9 us (2%)
  loops' own time  10.5 us (1%)
    all_to_all x1, waiting for transfers between devices, advance(): lax.all_to_all(weighted.astype(jnp.bfloat16).reshape(count_here, comp_cou...  166 us
    all_to_all x1, waiting for transfers between devices, advance(): lax.all_to_all(fourier, 'space', split_axis=4, concat_axis=3, tiled=True)  115 us
    psum x2, waiting for transfers between devices, from_root(): return lax.psum(jnp.where(mine, value, jnp.zeros_like(value)), axis)  76.9 us
    unnamed x23, local copies, waits for them, and re-layouts  68.3 us
    all_to_all x1, local copies, waits for them, and re-layouts, advance(): lax.all_to_all(fourier, 'space', split_axis=4, concat_axis=3, tiled=True)  40.8 us
    convert_element_type x1, local copies, waits for them, and re-layouts, advance(): fourier.reshape(trajectory_count, comp_count, 2, pair_local, lat_count)  40.7 us
    slice x3, local copies, waits for them, and re-layouts, advance(): first_part = projected[:, :, 0, 0] + parity * projected[:, :, 0, 1]  37.9 us
    dot_general x1, matrix products, advance(): jnp.einsum('tchpsl,pjl->tchspj', returned, legendre_wide, precision=lax.P...  35.2 us
  transfers between devices with their start and end apart: 4, of which 4 were waited for; matrix products, arithmetic and copies ran while one was open for 2% of the time, Pallas kernels for 0%

commit v1 on v0

v1 whole, which is shorter than its diff:
```python
import functools
import math

import jax
import jax.numpy as jnp
from jax import lax
from jax.experimental import pallas as pl
from jax.experimental.pallas import tpu as pltpu
from jax.sharding import PartitionSpec as P

LANES = 128
SUB = 8
LONGITUDES_PER_WAVE = 2

time_step = 0.25
wave_scale = 16.0
diffusion = 0.02


def layout_terms(first_pair, count, lane0, lanes, truncation):
    pair = first_pair + lax.broadcasted_iota(jnp.int32, (count, lanes), 0)
    column = lane0 + lax.broadcasted_iota(jnp.int32, (count, lanes), 1)
    leading = column < truncation - pair
    offset = jnp.where(leading, column, column - (truncation - pair))
    order = jnp.where(leading, pair, truncation - 1 - pair)
    return leading, (offset & 1) == 1, order + offset


def load_legendre(leg_ref, wide, row_length):
    block = leg_ref.shape[1]
    tiles = leg_ref.shape[2] // LANES
    for k in range(tiles):
        wide[k, : row_length * block, :] = (
            leg_ref[:, :, k * LANES : (k + 1) * LANES]
            .astype(jnp.float32)
            .reshape(row_length * block, LANES)
        )


def clear_tail(wide, row_length, block):
    for k in range(wide.shape[0]):
        wide[k, row_length * block :, :] = jnp.zeros(
            (wide.shape[1] - row_length * block, LANES), jnp.float32
        )


def forward_kernel(where_ref, spec_ref, leg_ref, out_ref, wide, xs, res, *, truncation, pairs):
    step = pl.program_id(0)
    row_length = truncation + 1
    trajectories, comps, block, _ = spec_ref.shape
    rows = trajectories * comps
    tiles = xs.shape[0]
    padded = tiles * LANES

    @pl.when(step == 0)
    def _():
        clear_tail(wide, row_length, block)

    load_legendre(leg_ref, wide, row_length)
    for k in range(tiles):
        width = min(LANES, row_length - k * LANES)
        piece = spec_ref[:, :, :, k * LANES : k * LANES + width].reshape(rows * block, width)
        if width < LANES:
            xs[k] = jnp.zeros((rows * block, LANES), jnp.float32)
            xs[k, :, :width] = piece
        else:
            xs[k] = piece

    first_pair = where_ref[0] + step * block

    def one(q, carry):
        x = jnp.concatenate(
            [xs[k, pl.ds(q, rows, stride=block), :] for k in range(tiles)], axis=1
        )
        leading, odd, _ = layout_terms(first_pair + q, 1, 0, padded, truncation)
        lead = jnp.where(leading, x, 0.0)
        trail = jnp.where(leading, 0.0, x)
        lhs = jnp.concatenate(
            [lead, trail, jnp.where(odd, -lead, lead), jnp.where(odd, -trail, trail)], axis=0
        ).astype(jnp.bfloat16)
        rhs = wide[0, pl.ds(q, padded, stride=block), :].astype(jnp.bfloat16)
        got = jnp.dot(lhs, rhs, preferred_element_type=jnp.float32)
        res[pl.ds(step * block + q, 4 * rows, stride=pairs), :] = got
        return carry

    lax.fori_loop(0, block, one, 0)

    @pl.when(step == pl.num_programs(0) - 1)
    def _():
        for t in range(trajectories):
            for s in range(2):
                for f in range(comps // 2):
                    parts = []
                    for r in range(2):
                        for h in range(2):
                            row = ((s * 2 + h) * rows + t * comps + 2 * f + r) * pairs
                            parts.append(res[row : row + pairs, :])
                    out_ref[t * 2 + s, f] = jnp.concatenate(parts, axis=0).astype(jnp.bfloat16)


def grid_kernel(cor_ref, weight_ref, in_ref, syn_ref, ana_ref, out_ref, modes, force, *, scale):
    sources, fields, rows, lanes = in_ref.shape
    longitudes = syn_ref.shape[0]
    for d in range(sources):
        for f in range(fields):
            modes[d * rows : (d + 1) * rows, f * lanes : (f + 1) * lanes] = in_ref[d, f]
    cor = cor_ref[...]
    weight = weight_ref[...]
    span = 128

    def synth(b, carry):
        at = pl.multiple_of(b * span, span)
        g = (
            jnp.dot(syn_ref[pl.ds(at, span), :], modes[...], preferred_element_type=jnp.float32)
            * scale
        )
        field = [g[:, f * lanes : (f + 1) * lanes] for f in range(fields)]
        mean = 0.5 * (field[4] + field[5])
        out = [None] * fields
        for a in range(2):
            spin = field[a] + cor
            div = field[2 + a]
            out[a] = -spin * div
            out[2 + a] = spin * field[a] - 0.5 * div * div
            out[4 + a] = -(field[4 + a] + mean) * div
        for f in range(fields):
            force[pl.ds(at, span), f * lanes : (f + 1) * lanes] = out[f].astype(jnp.bfloat16)
        return carry

    lax.fori_loop(0, longitudes // span, synth, 0)

    def analyse(d, carry):
        at = pl.multiple_of(d * rows, 16)
        w = jnp.dot(ana_ref[pl.ds(at, rows), :], force[...], preferred_element_type=jnp.float32)
        for f in range(fields):
            out_ref[d, f] = (w[:, f * lanes : (f + 1) * lanes] * weight).astype(jnp.bfloat16)
        return carry

    lax.fori_loop(0, sources, analyse, 0)


def semi_implicit_slabs(old, tend, degree, gm, hm, truncation):
    eig = wave_scale * (degree * (degree + 1)).astype(jnp.float32) / float(truncation * truncation)
    damping = 1.0 / (1.0 + diffusion * eig * eig)
    coupling = time_step * time_step * eig
    pm = [[gm[a][0] * hm[0][b] + gm[a][1] * hm[1][b] for b in range(2)] for a in range(2)]
    diag_one = 1.0 + coupling * pm[0][0]
    diag_two = 1.0 + coupling * pm[1][1]
    cross_one = coupling * pm[0][1]
    cross_two = coupling * pm[1][0]
    inverse = 1.0 / (diag_one * diag_two - cross_one * cross_two)
    out = [None] * 12
    for r in range(2):
        star = [old[c * 2 + r] + time_step * tend[c * 2 + r] for c in range(6)]
        right = [
            star[2 + a] + time_step * eig * (gm[a][0] * star[4] + gm[a][1] * star[5])
            for a in range(2)
        ]
        div = [
            (diag_two * right[0] - cross_one * right[1]) * inverse,
            (diag_one * right[1] - cross_two * right[0]) * inverse,
        ]
        for a in range(2):
            out[a * 2 + r] = damping * star[a]
            out[(2 + a) * 2 + r] = damping * div[a]
            out[(4 + a) * 2 + r] = damping * (
                star[4 + a] - time_step * (hm[a][0] * div[0] + hm[a][1] * div[1])
            )
    return out


def inverse_kernel(where_ref, gravity_ref, stability_ref, *refs, truncation, pairs, chunks, last):
    w_refs, refs = refs[:chunks], refs[chunks:]
    leg_refs, refs = refs[:chunks], refs[chunks:]
    if last:
        part_ref, spec_ref, out_ref, wide, ws, ten = refs
    else:
        out_ref, wide, ws, ten = refs
    step = pl.program_id(0)
    row_length = truncation + 1
    trajectories, comps, block, _ = out_ref.shape
    rows = trajectories * comps
    tiles = ten.shape[0]
    padded = tiles * LANES

    @pl.when(step == 0)
    def _():
        clear_tail(wide, row_length, block)
        for k in range(chunks):
            for t in range(trajectories):
                for s in range(2):
                    for f in range(comps // 2):
                        got = w_refs[k][t * 2 + s, f].astype(jnp.float32)
                        for r in range(2):
                            for h in range(2):
                                row = ((s * 2 + h) * rows + t * comps + 2 * f + r) * pairs
                                at = (r * 2 + h) * pairs
                                ws[k, row : row + pairs, :] = got[at : at + pairs, :]

    for k in range(chunks):
        wide[k, : row_length * block, :] = (
            leg_refs[k][...].astype(jnp.float32).reshape(row_length * block, LANES)
        )
    first_pair = where_ref[0] + step * block

    def one(q, carry):
        got = None
        for k in range(chunks):
            lhs = ws[k, pl.ds(step * block + q, 4 * rows, stride=pairs), :].astype(jnp.bfloat16)
            rhs = wide[k, pl.ds(q, padded, stride=block), :].astype(jnp.bfloat16)
            term = lax.dot_general(
                lhs, rhs, (((1,), (1,)), ((), ())), preferred_element_type=jnp.float32
            )
            got = term if got is None else got + term
        leading, odd, _ = layout_terms(first_pair + q, 1, 0, padded, truncation)
        north = jnp.where(leading, got[:rows], got[rows : 2 * rows])
        south = jnp.where(leading, got[2 * rows : 3 * rows], got[3 * rows :])
        total = north + jnp.where(odd, -south, south)
        for k in range(tiles):
            ten[k, pl.ds(q, rows, stride=block), :] = total[:, k * LANES : (k + 1) * LANES]
        return carry

    lax.fori_loop(0, block, one, 0)

    if last:
        gm = [[gravity_ref[a, b] for b in range(2)] for a in range(2)]
        hm = [[stability_ref[a, b] for b in range(2)] for a in range(2)]
    for k in range(tiles):
        width = min(LANES, row_length - k * LANES)
        lanes = slice(k * LANES, k * LANES + width)
        if last:
            _, _, degree = layout_terms(first_pair, block, k * LANES, width, truncation)

        def body(t, carry):
            tend = []
            for c in range(comps):
                at = pl.multiple_of((t * comps + c) * block, SUB)
                value = ten[k, pl.ds(at, block), :][:, :width]
                tend.append(value)
            if last:
                tend = [tend[c] + part_ref[t, c, :, lanes] for c in range(comps)]
                old = [spec_ref[t, c, :, lanes] for c in range(comps)]
                tend = semi_implicit_slabs(old, tend, degree, gm, hm, truncation)
            for c in range(comps):
                out_ref[t, c, :, lanes] = tend[c]
            return carry

        lax.fori_loop(0, trajectories, body, 0)


def fourier_tables(pair_count, groups, truncation, longitudes):
    index = jnp.arange(pair_count * 4, dtype=jnp.int32)
    local = pair_count // groups
    group = index // (4 * local)
    part = index // (2 * local) % 2
    half = index // local % 2
    pair = group * local + index % local
    order = jnp.where(half == 0, pair, truncation - 1 - pair)
    phase = order[:, None] * jnp.arange(longitudes, dtype=jnp.int32)[None, :] % longitudes
    angle = phase.astype(jnp.float32) * (2.0 * math.pi / longitudes)
    return jnp.where(part[:, None] == 0, jnp.cos(angle), -jnp.sin(angle)).astype(jnp.bfloat16)


def cloned_rows(spectra, clones):
    local = spectra.shape[0]
    members = lax.axis_size("member")
    got = []
    for i in range(clones.shape[0]):
        source = clones[i, 1] // local
        target = clones[i, 0] // local
        row = lax.dynamic_index_in_dim(spectra, clones[i, 1] % local, 0, keepdims=False)

        def move(a, b):
            if a == b:
                return lambda v: v
            return lambda v: lax.ppermute(v, "member", [(a, b)])

        branches = [move(a, b) for a in range(members) for b in range(members)]
        got.append(lax.switch(source * members + target, branches, row))
    return got


def replace_rows(spectra, rows, clones):
    local = spectra.shape[0]
    me = lax.axis_index("member")
    index = jnp.arange(local, dtype=jnp.int32)
    for i, row in enumerate(rows):
        mine = jnp.logical_and(clones[i, 0] // local == me, index == clones[i, 0] % local)
        spectra = jnp.where(mine[:, None, None, None], row[None], spectra)
    return spectra


def shards(spectra, legendre, sin_lat, gravity, stability, clones):
    trajectories, comps, pairs, row_length = spectra.shape
    truncation = row_length - 1
    half_lat = legendre.shape[2]
    longitudes = LONGITUDES_PER_WAVE * truncation
    space = lax.axis_size("space")
    position = lax.axis_index("space")
    fields = comps // 2
    split = space // (2 * trajectories)
    lane_count = LANES // split
    chunk_count = half_lat // LANES
    padded_pairs = -(-pairs // SUB) * SUB
    steps = padded_pairs // SUB
    tiles = -(-row_length // LANES)
    extra = padded_pairs - pairs
    rows = trajectories * comps

    state = replace_rows(spectra, cloned_rows(spectra, clones), clones)
    columns = jnp.transpose(legendre, (1, 0, 2))
    if extra:
        state = jnp.pad(state, ((0, 0), (0, 0), (0, extra), (0, 0)))
        columns = jnp.pad(columns, ((0, 0), (0, extra), (0, 0)))
    where = (position * pairs).astype(jnp.int32).reshape(1)

    smem = pl.BlockSpec(memory_space=pltpu.SMEM)
    state_spec = pl.BlockSpec((trajectories, comps, SUB, row_length), lambda i: (0, 0, i, 0))
    wire_shape = (2 * trajectories, fields, 4 * padded_pairs, LANES)
    wire_spec = pl.BlockSpec(wire_shape, lambda i: (0, 0, 0, 0))

    def leg_spec(k):
        return pl.BlockSpec((row_length, SUB, LANES), lambda i: (0, i, k))

    limit = 60 * 1024 * 1024

    def forward(k):
        return pl.pallas_call(
            functools.partial(forward_kernel, truncation=truncation, pairs=padded_pairs),
            out_shape=jax.ShapeDtypeStruct(wire_shape, jnp.bfloat16),
            grid=(steps,),
            in_specs=[smem, state_spec, leg_spec(k)],
            out_specs=wire_spec,
            scratch_shapes=[
                pltpu.VMEM((1, tiles * LANES * SUB, LANES), jnp.float32),
                pltpu.VMEM((tiles, rows * SUB, LANES), jnp.float32),
                pltpu.VMEM((4 * rows * padded_pairs, LANES), jnp.float32),
            ],
            compiler_params=pltpu.CompilerParams(vmem_limit_bytes=limit),
            cost_estimate=pl.CostEstimate(
                flops=8 * rows * padded_pairs * row_length * LANES,
                bytes_accessed=16 * 1024 * 1024,
                transcendentals=0,
            ),
            name="forward",
        )(where, state, columns)

    def to_wire(x):
        if extra:
            x = x.reshape(2 * trajectories, fields, 4, padded_pairs, LANES)[:, :, :, :pairs]
            x = x.reshape(2 * trajectories, fields, 4 * pairs, LANES)
        if split > 1:
            x = x.reshape(2 * trajectories, fields, 4 * pairs, split, lane_count)
            x = jnp.transpose(x, (0, 3, 1, 2, 4)).reshape(space, fields, 4 * pairs, lane_count)
        return x

    def from_wire(x):
        if split > 1:
            x = x.reshape(2 * trajectories, split, fields, 4 * pairs, lane_count)
            x = jnp.transpose(x, (0, 2, 3, 1, 4))
            x = x.reshape(2 * trajectories, fields, 4 * pairs, LANES)
        if extra:
            x = x.reshape(2 * trajectories, fields, 4, pairs, LANES)
            x = jnp.pad(x, ((0, 0), (0, 0), (0, 0), (0, extra), (0, 0)))
            x = x.reshape(wire_shape)
        return x

    def exchange(x):
        return lax.all_to_all(x, "space", split_axis=0, concat_axis=0, tiled=True)

    analysis = fourier_tables(pairs * space, space, truncation, longitudes)
    synthesis = analysis.T
    south = position // split % 2
    hemisphere = jnp.where(south == 0, sin_lat, -sin_lat)
    weights_all = math.pi * jnp.sqrt(1.0 - hemisphere * hemisphere) / (2 * half_lat)
    vmem = pl.BlockSpec(memory_space=pltpu.VMEM)
    modes = 4 * pairs * space

    def grid(k, x):
        first = k * LANES + position % split * lane_count
        mu = lax.dynamic_slice_in_dim(hemisphere, first, lane_count)
        weight = lax.dynamic_slice_in_dim(weights_all, first, lane_count)
        if split > 1:
            short = LANES - lane_count
            mu = jnp.pad(mu, (0, short))
            weight = jnp.pad(weight, (0, short))
            x = jnp.pad(x, ((0, 0), (0, 0), (0, 0), (0, short)))
        out = pl.pallas_call(
            functools.partial(grid_kernel, scale=1.0 / truncation),
            out_shape=jax.ShapeDtypeStruct(x.shape, jnp.bfloat16),
            in_specs=[vmem] * 5,
            out_specs=vmem,
            scratch_shapes=[
                pltpu.VMEM((modes, fields * LANES), jnp.bfloat16),
                pltpu.VMEM((longitudes, fields * LANES), jnp.bfloat16),
            ],
            compiler_params=pltpu.CompilerParams(vmem_limit_bytes=limit),
            cost_estimate=pl.CostEstimate(
                flops=4 * modes * longitudes * fields * LANES,
                bytes_accessed=12 * 1024 * 1024,
                transcendentals=0,
            ),
            name="grid",
        )((2.0 * mu)[None], weight[None], x, synthesis, analysis)
        return out[..., :lane_count] if split > 1 else out

    def inverse(ws, first, last, part):
        chunks = len(ws)
        extra_in = [part, state] if last else []
        return pl.pallas_call(
            functools.partial(
                inverse_kernel, truncation=truncation, pairs=padded_pairs, chunks=chunks, last=last
            ),
            out_shape=jax.ShapeDtypeStruct(state.shape, jnp.float32),
            grid=(steps,),
            in_specs=[smem] * 3
            + [wire_spec] * chunks
            + [leg_spec(first + k) for k in range(chunks)]
            + [state_spec] * len(extra_in),
            out_specs=state_spec,
            scratch_shapes=[
                pltpu.VMEM((chunks, tiles * LANES * SUB, LANES), jnp.float32),
                pltpu.VMEM((chunks, 4 * rows * padded_pairs, LANES), jnp.float32),
                pltpu.VMEM((tiles, rows * SUB, LANES), jnp.float32),
            ],
            compiler_params=pltpu.CompilerParams(vmem_limit_bytes=limit),
            cost_estimate=pl.CostEstimate(
                flops=8 * rows * padded_pairs * row_length * LANES * chunks,
                bytes_accessed=20 * 1024 * 1024,
                transcendentals=0,
            ),
            name="inverse",
        )(where, gravity, stability, *ws, *([columns] * chunks), *extra_in)

    sent = [exchange(to_wire(forward(k))) for k in range(chunk_count)]
    back = [from_wire(exchange(grid(k, x))) for k, x in enumerate(sent)]
    part = inverse(back[:-1], 0, False, None)
    out = inverse(back[-1:], chunk_count - 1, True, part)
    return out[:, :, :pairs] if extra else out


def solution(mesh):
    placed = (P("member", None, "space", None), P("space", None, None), P(), P(), P(), P())
    return jax.shard_map(
        shards,
        mesh=mesh,
        in_specs=placed,
        out_specs=P("member", None, "space", None),
        check_vma=False,
    )
```

time: 822 us -> 409 us (0.50)
  local copies, waits for them, and re-layouts: 271 us -> 8.91 us
  waiting for transfers between devices: 358 us -> 146 us
  Pallas kernels: 0 us -> 142 us
  matrix products: 75.2 us -> 0 us
  starting transfers between devices: 12.9 us -> 30.7 us
  loops' own time: 10.5 us -> 0.14 us
    all_to_all x2 -> x6, waiting for transfers between devices: 281 us -> 110 us  [exchange(): return lax.all_to_all(x, 'space', split_axis=0, concat_axis=0, tiled=True)]
    pallas_call x0 -> x8, Pallas kernels: none -> 142 us  [the longest x3 52.3 us: forward(): pl.pallas_call(functools.partial(forward_kernel, truncation=truncation, p...]
    psum x2 -> x0, waiting for transfers between devices: 76.9 us -> none  [from_root(): return lax.psum(jnp.where(mine, value, jnp.zeros_like(value)), axis)]
    dot_general x5 -> x0, matrix products: 75.2 us -> none  [the longest x1 35.2 us: advance(): jnp.einsum('tchpsl,pjl->tchspj', returned, legendre_wide, precision=lax.P...]
    unnamed x23 -> x10, local copies, waits for them, and re-layouts: 68.3 us -> 5.26 us
    convert_element_type x6 -> x1, other arithmetic: 4.13 us -> 57 us  [fourier_tables(): jnp.where(part[:, None] == 0, jnp.cos(angle), -jnp.sin(angle))]
    all_to_all x3 -> x0, local copies, waits for them, and re-layouts: 52.6 us -> none  [the longest x1 40.8 us: advance(): lax.all_to_all(fourier, 'space', split_axis=4, concat_axis=3, tiled=True)]
    slice x8 -> x1, local copies, waits for them, and re-layouts: 51.9 us -> 1.44 us  [replace_rows(): clones[i, 0] // local == me]
  transfers between devices with their start and end apart: 4 -> 8, of which waited for: 4 -> 6; matrix products, arithmetic and copies ran while one was open for 2% -> 14% of each run, Pallas kernels for 0% -> 26%
where the time goes in v1:
time: 409 us; the launch traced here: 402 us
  waiting for transfers between devices  146 us (36%)
  Pallas kernels  142 us (35%)
  other arithmetic  63.6 us (16%)
  starting transfers between devices  30.7 us (8%)
  between operations  10 us (2%)
  local copies, waits for them, and re-layouts  8.91 us (2%)
    all_to_all x6, waiting for transfers between devices, exchange(): return lax.all_to_all(x, 'space', split_axis=0, concat_axis=0, tiled=True)  110 us
    convert_element_type x1, other arithmetic, fourier_tables(): jnp.where(part[:, None] == 0, jnp.cos(angle), -jnp.sin(angle))  57 us
    pallas_call x3, Pallas kernels, forward(): pl.pallas_call(functools.partial(forward_kernel, truncation=truncation, p...  52.3 us
    pallas_call x2, Pallas kernels, inverse(): pl.pallas_call(functools.partial(inverse_kernel, truncation=truncation, p...  47.6 us
    pallas_call x3, Pallas kernels, grid(): pl.pallas_call(functools.partial(grid_kernel, scale=1.0 / truncation), ou...  42.1 us
    ppermute x2, waiting for transfers between devices, move(): return lambda v: lax.ppermute(v, 'member', [(a, b)])  36.3 us
    all_to_all x6, starting transfers between devices, exchange(): return lax.all_to_all(x, 'space', split_axis=0, concat_axis=0, tiled=True)  28.6 us
  transfers between devices with their start and end apart: 8, of which 6 were waited for; matrix products, arithmetic and copies ran while one was open for 14% of the time, Pallas kernels for 26%

profile of v1, /device:TPU:0, one launch (start us, length us, event | category | flops | bytes accessed | tf_op | source)
XLA Modules:
  0.0 401.6 jit_solution(4974247474277215027)
XLA Ops:
  0.0 1.4 fusion.27
  11.4 2.0 dynamic-slice_bitcast_fusion.1
  13.4 0.9 conditional.2
  13.4 0.8 collective-permute-start.10
  14.3 37.7 %conditional.3 = (f32[12,40,641]{2,1,0:T(8,128)S(1)}) conditional(s32[]{:T(128)} %clamp.7, f32[12,40,641]{2,1,0:T(8,128)S(1)} %get-tuple-element.74, f32[12,40,641]{2,1,0:T(8,128)S(1)} %get-tuple-element.74, f32[12,40,641]{2,1,0:T(8,128)S(1)} %get-tuple-element.74, f32[12,40,641]{2,1,0:T(8,128)S(1)} %get-tuple-element.74, ...), branch_computations={%region_16.17_spmd, %region_17.18_spmd, %region_18.19_spmd, %regio... | conditional | bytes 7384368 | solution.py:279
  14.4 1.3 collective-permute-start.21
  15.7 36.3 %collective-permute-done.21 = f32[12,40,641]{2,1,0:T(8,128)S(1)} collective-permute-done((f32[12,40,641]{2,1,0:T(8,128)S(1)}, f32[12,40,641]{2,1,0:T(8,128)S(1)}, u32[]{:S(2)}, u32[]{:S(2)}) %collective-permute-start.21) | collective-permute-done | bytes 1230752 | tf_op jit(solution)/shard_map/cond/branch_12_fun/ppermute | solution.py:276
  52.1 5.9 %select_select_fusion.spec_ref.refs_3_ = f32[4,12,40,641]{3,2,1,0:T(8,128)} fusion(f32[4,12,40,641]{3,2,1,0:T(8,128)} %param.38, f32[12,40,641]{2,1,0:T(8,128)S(1)} %get-tuple-element.93, f32[12,40,641]{2,1,0:T(8,128)S(1)} %get-tuple-element.92, pred[4]{0:T(512)(128)(4,1)S(1)} %get-tuple-element.90, pred[4]{0:T(512)(128)(4,1)S(1)} %get-tuple-element.91), kind=kLoop, calls=%fused_computation.16 | loop fusion | flops 2461440 | bytes 12307208 | tf_op jit(solution)/shard_map/jit(_where)/select_n | solution.py:289
  58.0 17.4 %forward.5 = bf16[8,6,160,128]{3,2,1,0:T(8,128)(2,1)} custom-call(s32[1]{0:T(128)} %bitcast.where_ref, f32[4,12,40,641]{3,2,1,0:T(8,128)} %select_select_fusion.spec_ref.refs_3_, bf16[641,40,384]{2,1,0:T(8,128)(2,1)} %bitcast.22), custom_call_target="tpu_custom_call" | custom-call | flops 1260257280 | bytes 16777216 | tf_op jit(solution)/shard_map/forward/pallas_call | solution.py:328
  75.4 6.6 %all-to-all-start.4 = ((bf16[8,6,160,128]{3,2,1,0:T(8,128)(2,1)}), bf16[8,6,160,128]{3,2,1,0:T(8,128)(2,1)S(1)}, u32[]{:S(2)}, u32[]{:S(2)}) async-start(bf16[8,6,160,128]{3,2,1,0:T(8,128)(2,1)} %forward.5), calls=%async_computation.4 | async-start | bytes 3932160 | tf_op jit(solution)/shard_map/all_to_all | solution.py:369
  82.1 17.4 %forward.4 = bf16[8,6,160,128]{3,2,1,0:T(8,128)(2,1)} custom-call(s32[1]{0:T(128)} %bitcast.where_ref, f32[4,12,40,641]{3,2,1,0:T(8,128)} %select_select_fusion.spec_ref.refs_3_, bf16[641,40,384]{2,1,0:T(8,128)(2,1)} %bitcast.23), custom_call_target="tpu_custom_call" | custom-call | flops 1260257280 | bytes 16777216 | tf_op jit(solution)/shard_map/forward/pallas_call | solution.py:328
  99.5 11.5 %all-to-all-done.4.in_ref = bf16[8,6,160,128]{3,2,1,0:T(8,128)(2,1)S(1)} async-done(((bf16[8,6,160,128]{3,2,1,0:T(8,128)(2,1)}), bf16[8,6,160,128]{3,2,1,0:T(8,128)(2,1)S(1)}, u32[]{:S(2)}, u32[]{:S(2)}) %all-to-all-start.4) | async-done | bytes 1966112 | tf_op jit(solution)/shard_map/all_to_all | solution.py:369
  110.9 1.3 copy-done.2
  112.2 4.5 %all-to-all-start.2 = ((bf16[8,6,160,128]{3,2,1,0:T(8,128)(2,1)}), bf16[8,6,160,128]{3,2,1,0:T(8,128)(2,1)}, u32[]{:S(2)}, u32[]{:S(2)}) async-start(bf16[8,6,160,128]{3,2,1,0:T(8,128)(2,1)} %forward.4), calls=%async_computation.2 | async-start | bytes 3932160 | tf_op jit(solution)/shard_map/all_to_all | solution.py:369
  116.8 17.5 %forward.3 = bf16[8,6,160,128]{3,2,1,0:T(8,128)(2,1)} custom-call(s32[1]{0:T(128)} %bitcast.where_ref, f32[4,12,40,641]{3,2,1,0:T(8,128)} %select_select_fusion.spec_ref.refs_3_, bf16[641,40,384]{2,1,0:T(8,128)(2,1)} %bitcast.24), custom_call_target="tpu_custom_call" | custom-call | flops 1260257280 | bytes 16777216 | tf_op jit(solution)/shard_map/forward/pallas_call | solution.py:328
  134.9 20.0 %all-to-all-done.2.in_ref = bf16[8,6,160,128]{3,2,1,0:T(8,128)(2,1)} async-done(((bf16[8,6,160,128]{3,2,1,0:T(8,128)(2,1)}), bf16[8,6,160,128]{3,2,1,0:T(8,128)(2,1)}, u32[]{:S(2)}, u32[]{:S(2)}) %all-to-all-start.2) | async-done | bytes 1966112 | tf_op jit(solution)/shard_map/all_to_all | solution.py:369
  154.9 3.6 all-to-all-start
  158.5 57.0 %select_convert_fusion = (bf16[1280,1280]{1,0:T(8,128)(2,1)}, bf16[1280,1280]{1,0:T(8,128)(2,1)}) fusion(s32[1280]{0:T(1024)S(1)} %subtract_select_fusion, pred[1280]{0:T(1024)(128)(4,1)S(1)} %fusion.19), kind=kLoop, calls=%fused_computation.6 | loop fusion | flops 39321600 | bytes 6560000 | tf_op jit(solution)/shard_map/convert_element_type | solution.py:261
  215.5 14.0 %grid.4 = bf16[8,6,160,128]{3,2,1,0:T(8,128)(2,1)} custom-call(f32[1,128]{1,0:T(1,128)} %get-tuple-element.88.cor_ref, f32[1,128]{1,0:T(1,128)} %get-tuple-element.78.weight_ref, bf16[8,6,160,128]{3,2,1,0:T(8,128)(2,1)} %all-to-all-done.2.in_ref, bf16[1280,1280]{1,0:T(8,128)(2,1)} %get-tuple-element.76.syn_ref, bf16[1280,1280]{1,0:T(8,128)(2,1)} %get-tuple-element.75.ana_ref), custom_call_target="tpu_custom_call" | custom-call | flops 5033164800 | bytes 12582912 | tf_op jit(solution)/shard_map/grid/pallas_call | solution.py:388
  229.6 1.4 copy-done.3
  231.0 5.9 %all-to-all-start.3 = ((bf16[8,6,160,128]{3,2,1,0:T(8,128)(2,1)}), bf16[8,6,160,128]{3,2,1,0:T(8,128)(2,1)S(1)}, u32[]{:S(2)}, u32[]{:S(2)}) async-start(bf16[8,6,160,128]{3,2,1,0:T(8,128)(2,1)} %grid.4), calls=%async_computation.3 | async-start | bytes 3932160 | tf_op jit(solution)/shard_map/all_to_all | solution.py:369
  236.9 14.0 %grid.5 = bf16[8,6,160,128]{3,2,1,0:T(8,128)(2,1)} custom-call(f32[1,128]{1,0:T(1,128)} %get-tuple-element.89.cor_ref, f32[1,128]{1,0:T(1,128)} %get-tuple-element.77.weight_ref, bf16[8,6,160,128]{3,2,1,0:T(8,128)(2,1)} %copy-done.2, bf16[1280,1280]{1,0:T(8,128)(2,1)} %get-tuple-element.76.syn_ref, bf16[1280,1280]{1,0:T(8,128)(2,1)} %get-tuple-element.75.ana_ref), custom_call_target="tpu_custom_call" | custom-call | flops 5033164800 | bytes 12582912 | tf_op jit(solution)/shard_map/grid/pallas_call | solution.py:388
  250.9 28.4 %all-to-all-done.3.refs_0_ = bf16[8,6,160,128]{3,2,1,0:T(8,128)(2,1)S(1)} async-done(((bf16[8,6,160,128]{3,2,1,0:T(8,128)(2,1)}), bf16[8,6,160,128]{3,2,1,0:T(8,128)(2,1)S(1)}, u32[]{:S(2)}, u32[]{:S(2)}) %all-to-all-start.3) | async-done | bytes 1966112 | tf_op jit(solution)/shard_map/all_to_all | solution.py:369
  279.4 1.3 copy-done
  280.7 4.3 %all-to-all-start.5 = ((bf16[8,6,160,128]{3,2,1,0:T(8,128)(2,1)}), bf16[8,6,160,128]{3,2,1,0:T(8,128)(2,1)}, u32[]{:S(2)}, u32[]{:S(2)}) async-start(bf16[8,6,160,128]{3,2,1,0:T(8,128)(2,1)} %grid.5), calls=%async_computation.5 | async-start | bytes 3932160 | tf_op jit(solution)/shard_map/all_to_all | solution.py:369
  285.0 14.1 %grid.3 = bf16[8,6,160,128]{3,2,1,0:T(8,128)(2,1)} custom-call(f32[1,128]{1,0:T(1,128)} %get-tuple-element.87.cor_ref, f32[1,128]{1,0:T(1,128)} %get-tuple-element.79.weight_ref, bf16[8,6,160,128]{3,2,1,0:T(8,128)(2,1)} %copy-done.3, bf16[1280,1280]{1,0:T(8,128)(2,1)} %get-tuple-element.76.syn_ref, bf16[1280,1280]{1,0:T(8,128)(2,1)} %get-tuple-element.75.ana_ref), custom_call_target="tpu_custom_call" | custom-call | flops 5033164800 | bytes 12582912 | tf_op jit(solution)/shard_map/grid/pallas_call | solution.py:388
  299.1 30.7 %all-to-all-done.5.refs_1_ = bf16[8,6,160,128]{3,2,1,0:T(8,128)(2,1)} async-done(((bf16[8,6,160,128]{3,2,1,0:T(8,128)(2,1)}), bf16[8,6,160,128]{3,2,1,0:T(8,128)(2,1)}, u32[]{:S(2)}, u32[]{:S(2)}) %all-to-all-start.5) | async-done | bytes 1966112 | tf_op jit(solution)/shard_map/all_to_all | solution.py:369
  329.8 3.6 all-to-all-start.1
  333.4 26.4 %inverse.2.refs_2_ = f32[4,12,40,641]{3,2,1,0:T(8,128)} custom-call(s32[1]{0:T(128)} %bitcast.where_ref, f32[2,2]{1,0:T(2,128)} %gravity_ref.3, f32[2,2]{1,0:T(2,128)} %stability_ref.3, bf16[8,6,160,128]{3,2,1,0:T(8,128)(2,1)} %copy-done, bf16[8,6,160,128]{3,2,1,0:T(8,128)(2,1)} %all-to-all-done.5.refs_1_, bf16[641,40,384]{2,1,0:T(8,128)(2,1)} %bitcast.25, ...), custom_call_target="tpu_custom_call" | custom-call | flops 2520514560 | bytes 20971520 | tf_op jit(solution)/shard_map/inverse/pallas_call | solution.py:410
  359.8 19.2 %all-to-all-done.1.refs_0_ = bf16[8,6,160,128]{3,2,1,0:T(8,128)(2,1)S(1)} async-done(((bf16[8,6,160,128]{3,2,1,0:T(8,128)(2,1)}), bf16[8,6,160,128]{3,2,1,0:T(8,128)(2,1)S(1)}, u32[]{:S(2)}, u32[]{:S(2)}) %all-to-all-start.1) | async-done | bytes 1966112 | tf_op jit(solution)/shard_map/all_to_all | solution.py:369
  379.0 1.3 copy-done.1
  380.3 21.2 %inverse.3 = f32[4,12,40,641]{3,2,1,0:T(8,128)} custom-call(s32[1]{0:T(128)} %bitcast.where_ref, f32[2,2]{1,0:T(2,128)} %gravity_ref.3, f32[2,2]{1,0:T(2,128)} %stability_ref.3, bf16[8,6,160,128]{3,2,1,0:T(8,128)(2,1)} %copy-done.1, bf16[641,40,384]{2,1,0:T(8,128)(2,1)} %bitcast.27, f32[4,12,40,641]{3,2,1,0:T(8,128)} %inverse.2.refs_2_, ...), custom_call_target="tpu_custom_call" | custom-call | flops 1260257280 | bytes 20971520 | tf_op jit(solution)/shard_map/inverse/pallas_call | solution.py:410
  (15 shorter events, 0.9 us)
Async XLA Ops:
  13.4 0.8 collective-permute-start.10
  14.4 37.6 %collective-permute-start.21 = (f32[12,40,641]{2,1,0:T(8,128)S(1)}, f32[12,40,641]{2,1,0:T(8,128)S(1)}, u32[]{:S(2)}, u32[]{:S(2)}) collective-permute-start(f32[12,40,641]{2,1,0:T(8,128)S(1)} %param.28), channel_id=1, source_target_pairs={{24,0},{25,1},{26,2},{27,3},{28,4},{29,5},{30,6},{31,7}} | collective-permute-start | bytes 3692168 | tf_op jit(solution)/shard_map/cond/branch_12_fun/ppermute | solution.py:276
  75.4 35.5 %all-to-all-start.4 = ((bf16[8,6,160,128]{3,2,1,0:T(8,128)(2,1)}), bf16[8,6,160,128]{3,2,1,0:T(8,128)(2,1)S(1)}, u32[]{:S(2)}, u32[]{:S(2)}) async-start(bf16[8,6,160,128]{3,2,1,0:T(8,128)(2,1)} %forward.5), calls=%async_computation.4 | async-start | bytes 3932160 | tf_op jit(solution)/shard_map/all_to_all | solution.py:369
  110.9 1.3 copy-start.2
  112.2 42.7 %all-to-all-start.2 = ((bf16[8,6,160,128]{3,2,1,0:T(8,128)(2,1)}), bf16[8,6,160,128]{3,2,1,0:T(8,128)(2,1)}, u32[]{:S(2)}, u32[]{:S(2)}) async-start(bf16[8,6,160,128]{3,2,1,0:T(8,128)(2,1)} %forward.4), calls=%async_computation.2 | async-start | bytes 3932160 | tf_op jit(solution)/shard_map/all_to_all | solution.py:369
  116.8 17.5 %copy-start.4 = (f32[384]{0:T(512)S(1)}, f32[384]{0:T(512)}, u32[]{:S(2)}) copy-start(f32[384]{0:T(512)} %param.40) | copy-start | bytes 4612
  154.9 74.7 %all-to-all-start = ((bf16[8,6,160,128]{3,2,1,0:T(8,128)(2,1)}), bf16[8,6,160,128]{3,2,1,0:T(8,128)(2,1)S(1)}, u32[]{:S(2)}, u32[]{:S(2)}) async-start(bf16[8,6,160,128]{3,2,1,0:T(8,128)(2,1)} %forward.3), calls=%async_computation | async-start | bytes 3932160 | tf_op jit(solution)/shard_map/all_to_all | solution.py:369
  229.6 1.4 copy-start.3
  231.0 48.4 %all-to-all-start.3 = ((bf16[8,6,160,128]{3,2,1,0:T(8,128)(2,1)}), bf16[8,6,160,128]{3,2,1,0:T(8,128)(2,1)S(1)}, u32[]{:S(2)}, u32[]{:S(2)}) async-start(bf16[8,6,160,128]{3,2,1,0:T(8,128)(2,1)} %grid.4), calls=%async_computation.3 | async-start | bytes 3932160 | tf_op jit(solution)/shard_map/all_to_all | solution.py:369
  279.4 1.3 copy-start
  280.7 49.1 %all-to-all-start.5 = ((bf16[8,6,160,128]{3,2,1,0:T(8,128)(2,1)}), bf16[8,6,160,128]{3,2,1,0:T(8,128)(2,1)}, u32[]{:S(2)}, u32[]{:S(2)}) async-start(bf16[8,6,160,128]{3,2,1,0:T(8,128)(2,1)} %grid.5), calls=%async_computation.5 | async-start | bytes 3932160 | tf_op jit(solution)/shard_map/all_to_all | solution.py:369
  329.8 49.2 %all-to-all-start.1 = ((bf16[8,6,160,128]{3,2,1,0:T(8,128)(2,1)}), bf16[8,6,160,128]{3,2,1,0:T(8,128)(2,1)S(1)}, u32[]{:S(2)}, u32[]{:S(2)}) async-start(bf16[8,6,160,128]{3,2,1,0:T(8,128)(2,1)} %grid.3), calls=%async_computation.1 | async-start | bytes 3932160 | tf_op jit(solution)/shard_map/all_to_all | solution.py:369
  379.0 1.3 copy-start.1

commit v2 on v1

--- a/solution.py
+++ b/solution.py
@@ -26,25 +26,7 @@
     return leading, (offset & 1) == 1, order + offset
 
 
-def load_legendre(leg_ref, wide, row_length):
-    block = leg_ref.shape[1]
-    tiles = leg_ref.shape[2] // LANES
-    for k in range(tiles):
-        wide[k, : row_length * block, :] = (
-            leg_ref[:, :, k * LANES : (k + 1) * LANES]
-            .astype(jnp.float32)
-            .reshape(row_length * block, LANES)
-        )
-
-
-def clear_tail(wide, row_length, block):
-    for k in range(wide.shape[0]):
-        wide[k, row_length * block :, :] = jnp.zeros(
-            (wide.shape[1] - row_length * block, LANES), jnp.float32
-        )
-
-
-def forward_kernel(where_ref, spec_ref, leg_ref, out_ref, wide, xs, res, *, truncation, pairs):
+def forward_kernel(where_ref, spec_ref, fresh_ref, leg_ref, out_ref, xs, res, *, truncation, pairs):
     step = pl.program_id(0)
     row_length = truncation + 1
     trajectories, comps, block, _ = spec_ref.shape
@@ -52,19 +34,23 @@
     tiles = xs.shape[0]
     padded = tiles * LANES
 
-    @pl.when(step == 0)
-    def _():
-        clear_tail(wide, row_length, block)
-
-    load_legendre(leg_ref, wide, row_length)
     for k in range(tiles):
         width = min(LANES, row_length - k * LANES)
-        piece = spec_ref[:, :, :, k * LANES : k * LANES + width].reshape(rows * block, width)
+        lanes = slice(k * LANES, k * LANES + width)
         if width < LANES:
             xs[k] = jnp.zeros((rows * block, LANES), jnp.float32)
-            xs[k, :, :width] = piece
-        else:
-            xs[k] = piece
+        xs[k, :, :width] = spec_ref[:, :, :, lanes].reshape(rows * block, width)
+
+    for i in range(fresh_ref.shape[0]):
+        slot = where_ref[1 + i]
+
+        @pl.when(slot >= 0)
+        def _():
+            at = pl.multiple_of(slot * comps * block, SUB)
+            for k in range(tiles):
+                width = min(LANES, row_length - k * LANES)
+                fresh = fresh_ref[i, :, :, k * LANES : k * LANES + width].astype(jnp.float32)
+                xs[k, pl.ds(at, comps * block), :width] = fresh.reshape(comps * block, width)
 
     first_pair = where_ref[0] + step * block
 
@@ -78,8 +64,7 @@
         lhs = jnp.concatenate(
             [lead, trail, jnp.where(odd, -lead, lead), jnp.where(odd, -trail, trail)], axis=0
         ).astype(jnp.bfloat16)
-        rhs = wide[0, pl.ds(q, padded, stride=block), :].astype(jnp.bfloat16)
-        got = jnp.dot(lhs, rhs, preferred_element_type=jnp.float32)
+        got = jnp.dot(lhs, leg_ref[q], preferred_element_type=jnp.float32)
         res[pl.ds(step * block + q, 4 * rows, stride=pairs), :] = got
         return carry
 
@@ -173,9 +158,9 @@
     w_refs, refs = refs[:chunks], refs[chunks:]
     leg_refs, refs = refs[:chunks], refs[chunks:]
     if last:
-        part_ref, spec_ref, out_ref, wide, ws, ten = refs
+        part_ref, spec_ref, fresh_ref, out_ref, ws, ten = refs
     else:
-        out_ref, wide, ws, ten = refs
+        out_ref, ws, ten = refs
     step = pl.program_id(0)
     row_length = truncation + 1
     trajectories, comps, block, _ = out_ref.shape
@@ -185,7 +170,6 @@
 
     @pl.when(step == 0)
     def _():
-        clear_tail(wide, row_length, block)
         for k in range(chunks):
             for t in range(trajectories):
                 for s in range(2):
@@ -197,19 +181,14 @@
                                 at = (r * 2 + h) * pairs
                                 ws[k, row : row + pairs, :] = got[at : at + pairs, :]
 
-    for k in range(chunks):
-        wide[k, : row_length * block, :] = (
-            leg_refs[k][...].astype(jnp.float32).reshape(row_length * block, LANES)
-        )
     first_pair = where_ref[0] + step * block
 
     def one(q, carry):
         got = None
         for k in range(chunks):
             lhs = ws[k, pl.ds(step * block + q, 4 * rows, stride=pairs), :].astype(jnp.bfloat16)
-            rhs = wide[k, pl.ds(q, padded, stride=block), :].astype(jnp.bfloat16)
             term = lax.dot_general(
-                lhs, rhs, (((1,), (1,)), ((), ())), preferred_element_type=jnp.float32
+                lhs, leg_refs[k][q], (((1,), (1,)), ((), ())), preferred_element_type=jnp.float32
             )
             got = term if got is None else got + term
         leading, odd, _ = layout_terms(first_pair + q, 1, 0, padded, truncation)
@@ -240,6 +219,9 @@
             if last:
                 tend = [tend[c] + part_ref[t, c, :, lanes] for c in range(comps)]
                 old = [spec_ref[t, c, :, lanes] for c in range(comps)]
+                for i in range(fresh_ref.shape[0]):
+                    mine = where_ref[1 + i] == t
+                    old = [jnp.where(mine, fresh_ref[i, c, :, lanes], old[c]) for c in range(comps)]
                 tend = semi_implicit_slabs(old, tend, degree, gm, hm, truncation)
             for c in range(comps):
                 out_ref[t, c, :, lanes] = tend[c]
@@ -256,38 +238,33 @@
     half = index // local % 2
     pair = group * local + index % local
     order = jnp.where(half == 0, pair, truncation - 1 - pair)
-    phase = order[:, None] * jnp.arange(longitudes, dtype=jnp.int32)[None, :] % longitudes
+    quarter = part * (longitudes // 4)
+    column = jnp.arange(longitudes, dtype=jnp.int32)[None, :]
+    phase = (order[:, None] * column + quarter[:, None]) % longitudes
     angle = phase.astype(jnp.float32) * (2.0 * math.pi / longitudes)
-    return jnp.where(part[:, None] == 0, jnp.cos(angle), -jnp.sin(angle)).astype(jnp.bfloat16)
-
-
-def cloned_rows(spectra, clones):
-    local = spectra.shape[0]
+    return jnp.cos(angle).astype(jnp.bfloat16)
+
+
+def clone_routes(clones, local):
     members = lax.axis_size("member")
-    got = []
-    for i in range(clones.shape[0]):
-        source = clones[i, 1] // local
-        target = clones[i, 0] // local
-        row = lax.dynamic_index_in_dim(spectra, clones[i, 1] % local, 0, keepdims=False)
-
-        def move(a, b):
-            if a == b:
-                return lambda v: v
-            return lambda v: lax.ppermute(v, "member", [(a, b)])
-
-        branches = [move(a, b) for a in range(members) for b in range(members)]
-        got.append(lax.switch(source * members + target, branches, row))
-    return got
-
-
-def replace_rows(spectra, rows, clones):
-    local = spectra.shape[0]
-    me = lax.axis_index("member")
-    index = jnp.arange(local, dtype=jnp.int32)
-    for i, row in enumerate(rows):
-        mine = jnp.logical_and(clones[i, 0] // local == me, index == clones[i, 0] % local)
-        spectra = jnp.where(mine[:, None, None, None], row[None], spectra)
-    return spectra
+    me = lax.axis_index("member").astype(jnp.int32)
+    owner = lax.div(clones, jnp.full_like(clones, local))
+    index = clones - owner * local
+    route = owner[:, 1] * members + owner[:, 0]
+    slot = jnp.where(owner[:, 0] == me, index[:, 0], -1)
+    return index[:, 1], route, slot
+
+
+def send_clone(row, route):
+    members = lax.axis_size("member")
+
+    def move(a, b):
+        if a == b:
+            return lambda v: v
+        return lambda v: lax.ppermute(v, "member", [(a, b)])
+
+    branches = [move(a, b) for a in range(members) for b in range(members)]
+    return lax.switch(route, branches, row)
 
 
 def shards(spectra, legendre, sin_lat, gravity, stability, clones):
@@ -307,20 +284,34 @@
     extra = padded_pairs - pairs
     rows = trajectories * comps
 
-    state = replace_rows(spectra, cloned_rows(spectra, clones), clones)
-    columns = jnp.transpose(legendre, (1, 0, 2))
+    survivor, route, slot = clone_routes(clones, trajectories)
+    count = clones.shape[0]
+    living = [
+        lax.dynamic_index_in_dim(spectra, survivor[i], 0, keepdims=False) for i in range(count)
+    ]
+    fresh_narrow = jnp.stack(
+        [send_clone(living[i].astype(jnp.bfloat16), route[i]) for i in range(count)]
+    )
+    state = spectra
     if extra:
         state = jnp.pad(state, ((0, 0), (0, 0), (0, extra), (0, 0)))
-        columns = jnp.pad(columns, ((0, 0), (0, extra), (0, 0)))
-    where = (position * pairs).astype(jnp.int32).reshape(1)
+        fresh_narrow = jnp.pad(fresh_narrow, ((0, 0), (0, 0), (0, extra), (0, 0)))
+    where = jnp.concatenate([(position * pairs).astype(jnp.int32).reshape(1), slot])
+    columns = [
+        jnp.pad(
+            legendre[:, :, k * LANES : (k + 1) * LANES],
+            ((0, extra), (0, tiles * LANES - row_length), (0, 0)),
+        )
+        for k in range(chunk_count)
+    ]
 
     smem = pl.BlockSpec(memory_space=pltpu.SMEM)
     state_spec = pl.BlockSpec((trajectories, comps, SUB, row_length), lambda i: (0, 0, i, 0))
     wire_shape = (2 * trajectories, fields, 4 * padded_pairs, LANES)
     wire_spec = pl.BlockSpec(wire_shape, lambda i: (0, 0, 0, 0))
 
-    def leg_spec(k):
-        return pl.BlockSpec((row_length, SUB, LANES), lambda i: (0, i, k))
+    fresh_spec = pl.BlockSpec((count, comps, SUB, row_length), lambda i: (0, 0, i, 0))
+    leg_spec = pl.BlockSpec((SUB, tiles * LANES, LANES), lambda i: (i, 0, 0))
 
     limit = 60 * 1024 * 1024
 
@@ -329,10 +320,9 @@
             functools.partial(forward_kernel, truncation=truncation, pairs=padded_pairs),
             out_shape=jax.ShapeDtypeStruct(wire_shape, jnp.bfloat16),
             grid=(steps,),
-            in_specs=[smem, state_spec, leg_spec(k)],
+            in_specs=[smem, state_spec, fresh_spec, leg_spec],
             out_specs=wire_spec,
             scratch_shapes=[
-                pltpu.VMEM((1, tiles * LANES * SUB, LANES), jnp.float32),
                 pltpu.VMEM((tiles, rows * SUB, LANES), jnp.float32),
                 pltpu.VMEM((4 * rows * padded_pairs, LANES), jnp.float32),
             ],
@@ -343,7 +333,7 @@
                 transcendentals=0,
             ),
             name="forward",
-        )(where, state, columns)
+        )(where, state, fresh_narrow, columns[k])
 
     def to_wire(x):
         if extra:
@@ -368,7 +358,9 @@
     def exchange(x):
         return lax.all_to_all(x, "space", split_axis=0, concat_axis=0, tiled=True)
 
-    analysis = fourier_tables(pairs * space, space, truncation, longitudes)
+    analysis = lax.optimization_barrier(
+        fourier_tables(pairs * space, space, truncation, longitudes)
+    )
     synthesis = analysis.T
     south = position // split % 2
     hemisphere = jnp.where(south == 0, sin_lat, -sin_lat)
@@ -406,7 +398,7 @@
 
     def inverse(ws, first, last, part):
         chunks = len(ws)
-        extra_in = [part, state] if last else []
+        extra_in = [part, state, fresh] if last else []
         return pl.pallas_call(
             functools.partial(
                 inverse_kernel, truncation=truncation, pairs=padded_pairs, chunks=chunks, last=last
@@ -415,11 +407,10 @@
             grid=(steps,),
             in_specs=[smem] * 3
             + [wire_spec] * chunks
-            + [leg_spec(first + k) for k in range(chunks)]
-            + [state_spec] * len(extra_in),
+            + [leg_spec] * chunks
+            + [state_spec, state_spec, fresh_spec][: len(extra_in)],
             out_specs=state_spec,
             scratch_shapes=[
-                pltpu.VMEM((chunks, tiles * LANES * SUB, LANES), jnp.float32),
                 pltpu.VMEM((chunks, 4 * rows * padded_pairs, LANES), jnp.float32),
                 pltpu.VMEM((tiles, rows * SUB, LANES), jnp.float32),
             ],
@@ -430,9 +421,14 @@
                 transcendentals=0,
             ),
             name="inverse",
-        )(where, gravity, stability, *ws, *([columns] * chunks), *extra_in)
-
-    sent = [exchange(to_wire(forward(k))) for k in range(chunk_count)]
+        )(where, gravity, stability, *ws, *columns[first : first + chunks], *extra_in)
+
+    made = [forward(k) for k in range(chunk_count)]
+    wide, _ = lax.optimization_barrier((living, made[1]))
+    fresh = jnp.stack([send_clone(wide[i], route[i]) for i in range(count)])
+    if extra:
+        fresh = jnp.pad(fresh, ((0, 0), (0, 0), (0, extra), (0, 0)))
+    sent = [exchange(to_wire(x)) for x in made]
     back = [from_wire(exchange(grid(k, x))) for k, x in enumerate(sent)]
     part = inverse(back[:-1], 0, False, None)
     out = inverse(back[-1:], chunk_count - 1, True, part)

time: 409 us -> 407 us (level)
  the two profiles are of different devices: /device:TPU:0 before, /device:TPU:1 now
where the time goes in v2:
time: 407 us; the launch traced here: 406 us
  waiting for transfers between devices  159 us (39%)
  Pallas kernels  121 us (30%)
  local copies, waits for them, and re-layouts  48.8 us (12%)
  other arithmetic  36.3 us (9%)
  starting transfers between devices  36 us (9%)
  between operations  5.19 us (1%)
    all_to_all x6, waiting for transfers between devices, exchange(): return lax.all_to_all(x, 'space', split_axis=0, concat_axis=0, tiled=True)  104 us
    ppermute x4, waiting for transfers between devices, move(): return lambda v: lax.ppermute(v, 'member', [(a, b)])  55.2 us
    pallas_call x3, Pallas kernels, grid(): pl.pallas_call(functools.partial(grid_kernel, scale=1.0 / truncation), ou...  42.1 us
    pallas_call x3, Pallas kernels, forward(): pl.pallas_call(functools.partial(forward_kernel, truncation=truncation, p...  40.3 us
    pallas_call x2, Pallas kernels, inverse(): pl.pallas_call(functools.partial(inverse_kernel, truncation=truncation, p...  38.5 us
    all_to_all x6, starting transfers between devices, exchange(): return lax.all_to_all(x, 'space', split_axis=0, concat_axis=0, tiled=True)  30 us
    convert_element_type x1, other arithmetic, fourier_tables(): return jnp.cos(angle).astype(jnp.bfloat16)  27.9 us
    pad x3, local copies, waits for them, and re-layouts, shards(): jnp.pad(legendre[:, :, k * LANES:(k + 1) * LANES], ((0, extra), (0, tiles...  15.5 us
  transfers between devices with their start and end apart: 10, of which 6 were waited for; matrix products, arithmetic and copies ran while one was open for 13% of the time, Pallas kernels for 22%

profile of v2, /device:TPU:1, one launch (start us, length us, event | category | flops | bytes accessed | tf_op | source)
XLA Modules:
  0.0 406.5 jit_solution(5198707180468466464)
XLA Ops:
  5.9 13.4 %fusion.26 = (bf16[40,641,128]{2,0,1:T(8,128)(2,1)S(1)}, bf16[40,641,128]{2,0,1:T(8,128)(2,1)}, bf16[40,641,128]{2,0,1:T(8,128)(2,1)}) fusion(bf16[40,641,384]{2,0,1:T(8,128)(2,1)} %param.71), kind=kLoop, calls=%fused_computation.71 | loop fusion | bytes 39383040 | tf_op jit(solution)/shard_map/slice | solution.py:302
  19.3 3.6 copy.15
  28.6 20.5 %conditional.5 = (bf16[1,12,40,641]{3,2,1,0:T(8,128)(2,1)}) conditional(s32[]{:T(128)} %bitcast.38, f32[12,40,641]{2,1,0:T(8,128)S(1)} %get-tuple-element.206, f32[12,40,641]{2,1,0:T(8,128)S(1)} %get-tuple-element.206, f32[12,40,641]{2,1,0:T(8,128)S(1)} %get-tuple-element.206, ...), branch_computations={%region_16.17_spmd, %region_17.18_spmd, %region_18.19_spmd, %regio... | conditional | flops 307680 | bytes 4307568 | solution.py:267
  29.9 19.1 %collective-permute-done.22 = bf16[12,40,641]{2,1,0:T(8,128)(2,1)} collective-permute-done((bf16[12,40,641]{2,1,0:T(8,128)(2,1)S(1)}, bf16[12,40,641]{2,1,0:T(8,128)(2,1)}, u32[]{:S(2)}, u32[]{:S(2)}) %collective-permute-start.22) | collective-permute-done | bytes 615392 | tf_op jit(solution)/shard_map/cond/branch_13_fun/ppermute | solution.py:264
  51.6 7.1 %pad.12.leg_ref.refs_3_ = bf16[40,768,128]{2,1,0:T(8,128)(2,1)} pad(bf16[40,641,128]{2,1,0:T(8,128)(2,1)} %copy.15, bf16[]{:T(256)} %constant.138.clone.1), padding=0_0x0_127x0_0 | pad | bytes 14428162 | tf_op jit(solution)/shard_map/jit(_pad)/pad | solution.py:301
  58.8 13.4 %forward.5 = bf16[8,6,160,128]{3,2,1,0:T(8,128)(2,1)} custom-call(s32[3]{0:T(128)} %pad_add_fusion.where_ref, f32[4,12,40,641]{3,2,1,0:T(8,128)} %refs_3_.1, bf16[2,12,40,641]{3,2,1,0:T(8,128)(2,1)} %pad_maximum_fusion.1.fresh_ref, bf16[40,768,128]{2,1,0:T(8,128)(2,1)} %pad.12.leg_ref.refs_3_), custom_call_target="tpu_custom_call" | custom-call | flops 1260257280 | bytes 16777216 | tf_op jit(solution)/shard_map/forward/pallas_call | solution.py:319
  72.2 7.0 %all-to-all-start.4 = ((bf16[8,6,160,128]{3,2,1,0:T(8,128)(2,1)}), bf16[8,6,160,128]{3,2,1,0:T(8,128)(2,1)}, u32[]{:S(2)}, u32[]{:S(2)}) async-start(bf16[8,6,160,128]{3,2,1,0:T(8,128)(2,1)} %forward.5), calls=%async_computation.4 | async-start | bytes 3932160 | tf_op jit(solution)/shard_map/all_to_all | solution.py:359
  79.2 3.7 copy.14
  82.9 4.2 %pad.11.leg_ref.refs_2_ = bf16[40,768,128]{2,1,0:T(8,128)(2,1)} pad(bf16[40,641,128]{2,1,0:T(8,128)(2,1)S(1)} %copy.14, bf16[]{:T(256)} %constant.138.clone.1), padding=0_0x0_127x0_0 | pad | bytes 14428162 | tf_op jit(solution)/shard_map/jit(_pad)/pad | solution.py:301
  87.1 13.4 %forward.4 = bf16[8,6,160,128]{3,2,1,0:T(8,128)(2,1)} custom-call(s32[3]{0:T(128)} %pad_add_fusion.where_ref, f32[4,12,40,641]{3,2,1,0:T(8,128)} %refs_3_.1, bf16[2,12,40,641]{3,2,1,0:T(8,128)(2,1)} %pad_maximum_fusion.1.fresh_ref, bf16[40,768,128]{2,1,0:T(8,128)(2,1)} %pad.11.leg_ref.refs_2_), custom_call_target="tpu_custom_call" | custom-call | flops 1260257280 | bytes 16777216 | tf_op jit(solution)/shard_map/forward/pallas_call | solution.py:319
  100.5 18.3 %all-to-all-done.4.in_ref = bf16[8,6,160,128]{3,2,1,0:T(8,128)(2,1)} async-done(((bf16[8,6,160,128]{3,2,1,0:T(8,128)(2,1)}), bf16[8,6,160,128]{3,2,1,0:T(8,128)(2,1)}, u32[]{:S(2)}, u32[]{:S(2)}) %all-to-all-start.4) | async-done | bytes 1966112 | tf_op jit(solution)/shard_map/all_to_all | solution.py:359
  118.8 4.5 %all-to-all-start.2 = ((bf16[8,6,160,128]{3,2,1,0:T(8,128)(2,1)}), bf16[8,6,160,128]{3,2,1,0:T(8,128)(2,1)}, u32[]{:S(2)}, u32[]{:S(2)}) async-start(bf16[8,6,160,128]{3,2,1,0:T(8,128)(2,1)} %forward.4), calls=%async_computation.2 | async-start | bytes 3932160 | tf_op jit(solution)/shard_map/all_to_all | solution.py:359
  123.3 3.7 copy.13
  127.0 4.2 %pad.10.leg_ref.refs_1_ = bf16[40,768,128]{2,1,0:T(8,128)(2,1)} pad(bf16[40,641,128]{2,1,0:T(8,128)(2,1)S(1)} %copy.13, bf16[]{:T(256)} %constant.138.clone.1), padding=0_0x0_127x0_0 | pad | bytes 14428162 | tf_op jit(solution)/shard_map/jit(_pad)/pad | solution.py:301
  131.2 13.4 %forward.3 = bf16[8,6,160,128]{3,2,1,0:T(8,128)(2,1)} custom-call(s32[3]{0:T(128)} %pad_add_fusion.where_ref, f32[4,12,40,641]{3,2,1,0:T(8,128)} %refs_3_.1, bf16[2,12,40,641]{3,2,1,0:T(8,128)(2,1)} %pad_maximum_fusion.1.fresh_ref, bf16[40,768,128]{2,1,0:T(8,128)(2,1)} %pad.10.leg_ref.refs_1_), custom_call_target="tpu_custom_call" | custom-call | flops 1260257280 | bytes 16777216 | tf_op jit(solution)/shard_map/forward/pallas_call | solution.py:319
  144.6 23.4 %all-to-all-done.2.in_ref = bf16[8,6,160,128]{3,2,1,0:T(8,128)(2,1)} async-done(((bf16[8,6,160,128]{3,2,1,0:T(8,128)(2,1)}), bf16[8,6,160,128]{3,2,1,0:T(8,128)(2,1)}, u32[]{:S(2)}, u32[]{:S(2)}) %all-to-all-start.2) | async-done | bytes 1966112 | tf_op jit(solution)/shard_map/all_to_all | solution.py:359
  168.1 4.3 %all-to-all-start = ((bf16[8,6,160,128]{3,2,1,0:T(8,128)(2,1)}), bf16[8,6,160,128]{3,2,1,0:T(8,128)(2,1)}, u32[]{:S(2)}, u32[]{:S(2)}) async-start(bf16[8,6,160,128]{3,2,1,0:T(8,128)(2,1)} %forward.3), calls=%async_computation | async-start | bytes 3932160 | tf_op jit(solution)/shard_map/all_to_all | solution.py:359
  172.4 27.9 %fusion.3.ana_ref = bf16[1280,1280]{1,0:T(8,128)(2,1)} fusion(s32[1280]{0:T(1024)S(1)} %get-tuple-element.236, s32[1280]{0:T(1024)S(1)} %get-tuple-element.235), kind=kLoop, calls=%fused_computation.12 | loop fusion | flops 18022400 | bytes 3287040 | tf_op jit(solution)/shard_map/convert_element_type | solution.py:245
  200.3 5.6 %copy.8.syn_ref = bf16[1280,1280]{1,0:T(8,128)(2,1)} copy(bf16[1280,1280]{0,1:T(8,128)(2,1)} %bitcast.64) | data formatting | bytes 6553600 | tf_op jit(solution)/shard_map/transpose | solution.py:364
  206.6 14.0 %grid.5 = bf16[8,6,160,128]{3,2,1,0:T(8,128)(2,1)} custom-call(f32[1,128]{1,0:T(1,128)} %get-tuple-element.234.cor_ref, f32[1,128]{1,0:T(1,128)} %get-tuple-element.218.weight_ref, bf16[8,6,160,128]{3,2,1,0:T(8,128)(2,1)} %all-to-all-done.4.in_ref, bf16[1280,1280]{1,0:T(8,128)(2,1)} %copy.8.syn_ref, bf16[1280,1280]{1,0:T(8,128)(2,1)} %fusion.3.ana_ref), custom_call_target="tpu_custom_call" | custom-call | flops 5033164800 | bytes 12582912 | tf_op jit(solution)/shard_map/grid/pallas_call | solution.py:380
  220.6 5.3 %all-to-all-start.5 = ((bf16[8,6,160,128]{3,2,1,0:T(8,128)(2,1)}), bf16[8,6,160,128]{3,2,1,0:T(8,128)(2,1)}, u32[]{:S(2)}, u32[]{:S(2)}) async-start(bf16[8,6,160,128]{3,2,1,0:T(8,128)(2,1)} %grid.5), calls=%async_computation.5 | async-start | bytes 3932160 | tf_op jit(solution)/shard_map/all_to_all | solution.py:359
  225.9 14.0 %grid.4 = bf16[8,6,160,128]{3,2,1,0:T(8,128)(2,1)} custom-call(f32[1,128]{1,0:T(1,128)} %get-tuple-element.233.cor_ref, f32[1,128]{1,0:T(1,128)} %get-tuple-element.219.weight_ref, bf16[8,6,160,128]{3,2,1,0:T(8,128)(2,1)} %all-to-all-done.2.in_ref, bf16[1280,1280]{1,0:T(8,128)(2,1)} %copy.8.syn_ref, bf16[1280,1280]{1,0:T(8,128)(2,1)} %fusion.3.ana_ref), custom_call_target="tpu_custom_call" | custom-call | flops 5033164800 | bytes 12582912 | tf_op jit(solution)/shard_map/grid/pallas_call | solution.py:380
  240.0 31.6 %all-to-all-done.5.refs_1_ = bf16[8,6,160,128]{3,2,1,0:T(8,128)(2,1)} async-done(((bf16[8,6,160,128]{3,2,1,0:T(8,128)(2,1)}), bf16[8,6,160,128]{3,2,1,0:T(8,128)(2,1)}, u32[]{:S(2)}, u32[]{:S(2)}) %all-to-all-start.5) | async-done | bytes 1966112 | tf_op jit(solution)/shard_map/all_to_all | solution.py:359
  271.6 4.3 %all-to-all-start.3 = ((bf16[8,6,160,128]{3,2,1,0:T(8,128)(2,1)}), bf16[8,6,160,128]{3,2,1,0:T(8,128)(2,1)}, u32[]{:S(2)}, u32[]{:S(2)}) async-start(bf16[8,6,160,128]{3,2,1,0:T(8,128)(2,1)} %grid.4), calls=%async_computation.3 | async-start | bytes 3932160 | tf_op jit(solution)/shard_map/all_to_all | solution.py:359
  275.9 14.0 %grid.3 = bf16[8,6,160,128]{3,2,1,0:T(8,128)(2,1)} custom-call(f32[1,128]{1,0:T(1,128)} %get-tuple-element.232.cor_ref, f32[1,128]{1,0:T(1,128)} %get-tuple-element.220.weight_ref, bf16[8,6,160,128]{3,2,1,0:T(8,128)(2,1)} %all-to-all-done.in_ref, bf16[1280,1280]{1,0:T(8,128)(2,1)} %copy.8.syn_ref, bf16[1280,1280]{1,0:T(8,128)(2,1)} %fusion.3.ana_ref), custom_call_target="tpu_custom_call" | custom-call | flops 5033164800 | bytes 12582912 | tf_op jit(solution)/shard_map/grid/pallas_call | solution.py:380
  289.9 30.7 %all-to-all-done.3.refs_0_ = bf16[8,6,160,128]{3,2,1,0:T(8,128)(2,1)} async-done(((bf16[8,6,160,128]{3,2,1,0:T(8,128)(2,1)}), bf16[8,6,160,128]{3,2,1,0:T(8,128)(2,1)}, u32[]{:S(2)}, u32[]{:S(2)}) %all-to-all-start.3) | async-done | bytes 1966112 | tf_op jit(solution)/shard_map/all_to_all | solution.py:359
  320.6 4.5 %all-to-all-start.1 = ((bf16[8,6,160,128]{3,2,1,0:T(8,128)(2,1)}), bf16[8,6,160,128]{3,2,1,0:T(8,128)(2,1)}, u32[]{:S(2)}, u32[]{:S(2)}) async-start(bf16[8,6,160,128]{3,2,1,0:T(8,128)(2,1)} %grid.3), calls=%async_computation.1 | async-start | bytes 3932160 | tf_op jit(solution)/shard_map/all_to_all | solution.py:359
  327.0 37.4 %conditional.7 = (f32[12,40,641]{2,1,0:T(8,128)}) conditional(s32[]{:T(128)} %bitcast.38, f32[12,40,641]{2,1,0:T(8,128)S(1)} %get-tuple-element.206, f32[12,40,641]{2,1,0:T(8,128)S(1)} %get-tuple-element.206, f32[12,40,641]{2,1,0:T(8,128)S(1)} %get-tuple-element.206, ...), branch_computations={%region_48.49_spmd, %region_49.50_spmd, %region_50.51_spmd, %regio... | conditional | bytes 4922928 | solution.py:267
  328.3 36.1 %collective-permute-done.46 = f32[12,40,641]{2,1,0:T(8,128)} collective-permute-done((f32[12,40,641]{2,1,0:T(8,128)S(1)}, f32[12,40,641]{2,1,0:T(8,128)}, u32[]{:S(2)}, u32[]{:S(2)}) %collective-permute-start.46) | collective-permute-done | bytes 1230752 | tf_op jit(solution)/shard_map/cond/branch_13_fun/ppermute | solution.py:264
  364.3 3.6 pad_maximum_fusion.refs_4_
  368.0 19.4 %inverse.2.refs_2_ = f32[4,12,40,641]{3,2,1,0:T(8,128)} custom-call(s32[3]{0:T(128)} %pad_add_fusion.where_ref, f32[2,2]{1,0:T(2,128)} %gravity_ref.3, f32[2,2]{1,0:T(2,128)} %stability_ref.3, bf16[8,6,160,128]{3,2,1,0:T(8,128)(2,1)} %all-to-all-done.3.refs_0_, bf16[8,6,160,128]{3,2,1,0:T(8,128)(2,1)} %all-to-all-done.5.refs_1_, ...), custom_call_target="tpu_custom_call" | custom-call | flops 2520514560 | bytes 20971520 | tf_op jit(solution)/shard_map/inverse/pallas_call | solution.py:402
  387.4 19.1 %inverse.3 = f32[4,12,40,641]{3,2,1,0:T(8,128)} custom-call(s32[3]{0:T(128)} %pad_add_fusion.where_ref, f32[2,2]{1,0:T(2,128)} %gravity_ref.3, f32[2,2]{1,0:T(2,128)} %stability_ref.3, bf16[8,6,160,128]{3,2,1,0:T(8,128)(2,1)} %all-to-all-done.1.refs_0_, bf16[40,768,128]{2,1,0:T(8,128)(2,1)} %pad.10.leg_ref.refs_1_, f32[4,12,40,641]{3,2,1,0:T(8,128)} %inverse.2.refs_2_, ...), custom_call_target="tpu_custom_call" | custom-call | flops 1260257280 | bytes 20971520 | tf_op jit(solution)/shard_map/inverse/pallas_call | solution.py:402
  (24 shorter events, 17.7 us)
Async XLA Ops:
  27.0 1.6 collective-permute-start.9
  28.6 20.4 %collective-permute-start.22 = (bf16[12,40,641]{2,1,0:T(8,128)(2,1)S(1)}, bf16[12,40,641]{2,1,0:T(8,128)(2,1)}, u32[]{:S(2)}, u32[]{:S(2)}) collective-permute-start(bf16[12,40,641]{2,1,0:T(8,128)(2,1)S(1)} %convert_element_type.167), channel_id=1, source_target_pairs={{24,8},{25,9},{26,10},{27,11},{28,12},{29,13},{30,14},{31,15}} | collective-permute-start | bytes 1846088 | tf_op jit(solution)/shard_map/cond/branch_13_fun/ppermute | solution.py:264
  72.2 46.6 %all-to-all-start.4 = ((bf16[8,6,160,128]{3,2,1,0:T(8,128)(2,1)}), bf16[8,6,160,128]{3,2,1,0:T(8,128)(2,1)}, u32[]{:S(2)}, u32[]{:S(2)}) async-start(bf16[8,6,160,128]{3,2,1,0:T(8,128)(2,1)} %forward.5), calls=%async_computation.4 | async-start | bytes 3932160 | tf_op jit(solution)/shard_map/all_to_all | solution.py:359
  118.8 49.2 %all-to-all-start.2 = ((bf16[8,6,160,128]{3,2,1,0:T(8,128)(2,1)}), bf16[8,6,160,128]{3,2,1,0:T(8,128)(2,1)}, u32[]{:S(2)}, u32[]{:S(2)}) async-start(bf16[8,6,160,128]{3,2,1,0:T(8,128)(2,1)} %forward.4), calls=%async_computation.2 | async-start | bytes 3932160 | tf_op jit(solution)/shard_map/all_to_all | solution.py:359
  168.1 52.5 %all-to-all-start = ((bf16[8,6,160,128]{3,2,1,0:T(8,128)(2,1)}), bf16[8,6,160,128]{3,2,1,0:T(8,128)(2,1)}, u32[]{:S(2)}, u32[]{:S(2)}) async-start(bf16[8,6,160,128]{3,2,1,0:T(8,128)(2,1)} %forward.3), calls=%async_computation | async-start | bytes 3932160 | tf_op jit(solution)/shard_map/all_to_all | solution.py:359
  200.3 5.6 %copy-start = (f32[384]{0:T(512)S(1)}, f32[384]{0:T(512)}, u32[]{:S(2)}) copy-start(f32[384]{0:T(512)} %param.72) | copy-start | bytes 4612
  220.6 51.0 %all-to-all-start.5 = ((bf16[8,6,160,128]{3,2,1,0:T(8,128)(2,1)}), bf16[8,6,160,128]{3,2,1,0:T(8,128)(2,1)}, u32[]{:S(2)}, u32[]{:S(2)}) async-start(bf16[8,6,160,128]{3,2,1,0:T(8,128)(2,1)} %grid.5), calls=%async_computation.5 | async-start | bytes 3932160 | tf_op jit(solution)/shard_map/all_to_all | solution.py:359
  271.6 49.1 %all-to-all-start.3 = ((bf16[8,6,160,128]{3,2,1,0:T(8,128)(2,1)}), bf16[8,6,160,128]{3,2,1,0:T(8,128)(2,1)}, u32[]{:S(2)}, u32[]{:S(2)}) async-start(bf16[8,6,160,128]{3,2,1,0:T(8,128)(2,1)} %grid.4), calls=%async_computation.3 | async-start | bytes 3932160 | tf_op jit(solution)/shard_map/all_to_all | solution.py:359
  320.6 66.8 %all-to-all-start.1 = ((bf16[8,6,160,128]{3,2,1,0:T(8,128)(2,1)}), bf16[8,6,160,128]{3,2,1,0:T(8,128)(2,1)}, u32[]{:S(2)}, u32[]{:S(2)}) async-start(bf16[8,6,160,128]{3,2,1,0:T(8,128)(2,1)} %grid.3), calls=%async_computation.1 | async-start | bytes 3932160 | tf_op jit(solution)/shard_map/all_to_all | solution.py:359
  325.1 1.9 collective-permute-start.33
  327.0 37.4 %collective-permute-start.46 = (f32[12,40,641]{2,1,0:T(8,128)S(1)}, f32[12,40,641]{2,1,0:T(8,128)}, u32[]{:S(2)}, u32[]{:S(2)}) collective-permute-start(f32[12,40,641]{2,1,0:T(8,128)S(1)} %param.61), channel_id=1, source_target_pairs={{24,8},{25,9},{26,10},{27,11},{28,12},{29,13},{30,14},{31,15}} | collective-permute-start | bytes 3692168 | tf_op jit(solution)/shard_map/cond/branch_13_fun/ppermute | solution.py:264

commit v3 on v2

--- a/solution.py
+++ b/solution.py
@@ -8,8 +8,11 @@
 from jax.experimental.pallas import tpu as pltpu
 from jax.sharding import PartitionSpec as P
 
+
 LANES = 128
 SUB = 8
+UNROLL_FORWARD = 2
+UNROLL_INVERSE = 4
 LONGITUDES_PER_WAVE = 2
 
 time_step = 0.25
@@ -26,14 +29,29 @@
     return leading, (offset & 1) == 1, order + offset
 
 
-def forward_kernel(where_ref, spec_ref, fresh_ref, leg_ref, out_ref, xs, res, *, truncation, pairs):
+def forward_kernel(where_ref, spec_ref, fresh_ref, leg_ref, *refs, truncation, pairs, keep):
     step = pl.program_id(0)
     row_length = truncation + 1
     trajectories, comps, block, _ = spec_ref.shape
     rows = trajectories * comps
+    slots = 2 * trajectories
+    out_refs, refs = refs[:slots], refs[slots:]
+    if keep:
+        keep_ref, refs = refs[0], refs[1:]
+    wide, xs, res = refs
     tiles = xs.shape[0]
     padded = tiles * LANES
-
+    count = fresh_ref.shape[0]
+
+    @pl.when(step == 0)
+    def _():
+        wide[row_length * block :, :] = jnp.zeros(
+            (wide.shape[0] - row_length * block, LANES), jnp.float32
+        )
+
+    wide[: row_length * block, :] = (
+        leg_ref[...].astype(jnp.float32).reshape(row_length * block, LANES)
+    )
     for k in range(tiles):
         width = min(LANES, row_length - k * LANES)
         lanes = slice(k * LANES, k * LANES + width)
@@ -41,7 +59,7 @@
             xs[k] = jnp.zeros((rows * block, LANES), jnp.float32)
         xs[k, :, :width] = spec_ref[:, :, :, lanes].reshape(rows * block, width)
 
-    for i in range(fresh_ref.shape[0]):
+    for i in range(count):
         slot = where_ref[1 + i]
 
         @pl.when(slot >= 0)
@@ -64,31 +82,38 @@
         lhs = jnp.concatenate(
             [lead, trail, jnp.where(odd, -lead, lead), jnp.where(odd, -trail, trail)], axis=0
         ).astype(jnp.bfloat16)
-        got = jnp.dot(lhs, leg_ref[q], preferred_element_type=jnp.float32)
+        rhs = wide[pl.ds(q, padded, stride=block), :].astype(jnp.bfloat16)
+        if keep:
+            keep_ref[q] = rhs
+        got = jnp.dot(lhs, rhs, preferred_element_type=jnp.float32)
         res[pl.ds(step * block + q, 4 * rows, stride=pairs), :] = got
         return carry
 
-    lax.fori_loop(0, block, one, 0)
+    lax.fori_loop(0, block, one, 0, unroll=UNROLL_FORWARD)
 
     @pl.when(step == pl.num_programs(0) - 1)
     def _():
-        for t in range(trajectories):
-            for s in range(2):
-                for f in range(comps // 2):
-                    parts = []
-                    for r in range(2):
-                        for h in range(2):
-                            row = ((s * 2 + h) * rows + t * comps + 2 * f + r) * pairs
-                            parts.append(res[row : row + pairs, :])
-                    out_ref[t * 2 + s, f] = jnp.concatenate(parts, axis=0).astype(jnp.bfloat16)
-
-
-def grid_kernel(cor_ref, weight_ref, in_ref, syn_ref, ana_ref, out_ref, modes, force, *, scale):
-    sources, fields, rows, lanes = in_ref.shape
+        for n in range(slots):
+            place = where_ref[1 + count + n]
+            t, s = lax.div(place, 2), lax.rem(place, 2)
+            base = pl.multiple_of((s * (2 * rows) + t * comps) * pairs, SUB)
+            for f in range(comps // 2):
+                parts = []
+                for r in range(2):
+                    for h in range(2):
+                        parts.append(res[pl.ds(base + (h * rows + 2 * f + r) * pairs, pairs), :])
+                out_refs[n][f] = jnp.concatenate(parts, axis=0).astype(jnp.bfloat16)
+
+
+def grid_kernel(order_ref, cor_ref, weight_ref, syn_ref, ana_ref, *refs, scale):
+    sources = order_ref.shape[0]
+    in_refs, out_refs, (modes, force) = refs[:sources], refs[sources:-2], refs[-2:]
+    fields, rows, lanes = in_refs[0].shape
     longitudes = syn_ref.shape[0]
-    for d in range(sources):
+    for n in range(sources):
+        at = pl.multiple_of(order_ref[n] * rows, 16)
         for f in range(fields):
-            modes[d * rows : (d + 1) * rows, f * lanes : (f + 1) * lanes] = in_ref[d, f]
+            modes[pl.ds(at, rows), f * lanes : (f + 1) * lanes] = in_refs[n][f]
     cor = cor_ref[...]
     weight = weight_ref[...]
     span = 128
@@ -118,10 +143,15 @@
         at = pl.multiple_of(d * rows, 16)
         w = jnp.dot(ana_ref[pl.ds(at, rows), :], force[...], preferred_element_type=jnp.float32)
         for f in range(fields):
-            out_ref[d, f] = (w[:, f * lanes : (f + 1) * lanes] * weight).astype(jnp.bfloat16)
+            lane = slice(f * lanes, (f + 1) * lanes)
+            modes[pl.ds(at, rows), lane] = (w[:, lane] * weight).astype(jnp.bfloat16)
         return carry
 
     lax.fori_loop(0, sources, analyse, 0)
+    for n in range(sources):
+        at = pl.multiple_of(order_ref[n] * rows, 16)
+        for f in range(fields):
+            out_refs[n][f] = modes[pl.ds(at, rows), f * lanes : (f + 1) * lanes]
 
 
 def semi_implicit_slabs(old, tend, degree, gm, hm, truncation):
@@ -154,41 +184,61 @@
     return out
 
 
-def inverse_kernel(where_ref, gravity_ref, stability_ref, *refs, truncation, pairs, chunks, last):
-    w_refs, refs = refs[:chunks], refs[chunks:]
+def inverse_kernel(
+    where_ref, gravity_ref, stability_ref, *refs, truncation, pairs, chunks, last, slots
+):
+    w_refs, refs = refs[: chunks * slots], refs[chunks * slots :]
     leg_refs, refs = refs[:chunks], refs[chunks:]
     if last:
         part_ref, spec_ref, fresh_ref, out_ref, ws, ten = refs
     else:
-        out_ref, ws, ten = refs
+        out_ref, ws, ten, wide = refs
     step = pl.program_id(0)
     row_length = truncation + 1
     trajectories, comps, block, _ = out_ref.shape
     rows = trajectories * comps
     tiles = ten.shape[0]
     padded = tiles * LANES
+    count = where_ref.shape[0] - 1 - slots
 
     @pl.when(step == 0)
     def _():
+        if not last:
+            for k in range(chunks):
+                wide[k, row_length * block :, :] = jnp.zeros(
+                    (wide.shape[1] - row_length * block, LANES), jnp.float32
+                )
         for k in range(chunks):
-            for t in range(trajectories):
-                for s in range(2):
-                    for f in range(comps // 2):
-                        got = w_refs[k][t * 2 + s, f].astype(jnp.float32)
-                        for r in range(2):
-                            for h in range(2):
-                                row = ((s * 2 + h) * rows + t * comps + 2 * f + r) * pairs
-                                at = (r * 2 + h) * pairs
-                                ws[k, row : row + pairs, :] = got[at : at + pairs, :]
-
+            for n in range(slots):
+                place = where_ref[1 + count + n]
+                t, s = lax.div(place, 2), lax.rem(place, 2)
+                base = pl.multiple_of((s * (2 * rows) + t * comps) * pairs, SUB)
+                for f in range(comps // 2):
+                    got = w_refs[k * slots + n][f].astype(jnp.float32)
+                    for r in range(2):
+                        for h in range(2):
+                            at = (r * 2 + h) * pairs
+                            ws[k, pl.ds(base + (h * rows + 2 * f + r) * pairs, pairs), :] = got[
+                                at : at + pairs, :
+                            ]
+
+    if not last:
+        for k in range(chunks):
+            wide[k, : row_length * block, :] = (
+                leg_refs[k][...].astype(jnp.float32).reshape(row_length * block, LANES)
+            )
     first_pair = where_ref[0] + step * block
 
     def one(q, carry):
         got = None
         for k in range(chunks):
             lhs = ws[k, pl.ds(step * block + q, 4 * rows, stride=pairs), :].astype(jnp.bfloat16)
+            if last:
+                rhs = leg_refs[k][q]
+            else:
+                rhs = wide[k, pl.ds(q, padded, stride=block), :].astype(jnp.bfloat16)
             term = lax.dot_general(
-                lhs, leg_refs[k][q], (((1,), (1,)), ((), ())), preferred_element_type=jnp.float32
+                lhs, rhs, (((1,), (1,)), ((), ())), preferred_element_type=jnp.float32
             )
             got = term if got is None else got + term
         leading, odd, _ = layout_terms(first_pair + q, 1, 0, padded, truncation)
@@ -199,7 +249,7 @@
             ten[k, pl.ds(q, rows, stride=block), :] = total[:, k * LANES : (k + 1) * LANES]
         return carry
 
-    lax.fori_loop(0, block, one, 0)
+    lax.fori_loop(0, block, one, 0, unroll=UNROLL_INVERSE)
 
     if last:
         gm = [[gravity_ref[a, b] for b in range(2)] for a in range(2)]
@@ -239,10 +289,13 @@
     pair = group * local + index % local
     order = jnp.where(half == 0, pair, truncation - 1 - pair)
     quarter = part * (longitudes // 4)
-    column = jnp.arange(longitudes, dtype=jnp.int32)[None, :]
+    half_turn = longitudes // 2
+    column = jnp.arange(half_turn, dtype=jnp.int32)[None, :]
     phase = (order[:, None] * column + quarter[:, None]) % longitudes
     angle = phase.astype(jnp.float32) * (2.0 * math.pi / longitudes)
-    return jnp.cos(angle).astype(jnp.bfloat16)
+    first = jnp.cos(angle)
+    second = jnp.where(order[:, None] % 2 == 0, first, -first)
+    return jnp.concatenate([first, second], axis=1).astype(jnp.bfloat16)
 
 
 def clone_routes(clones, local):
@@ -296,67 +349,91 @@
     if extra:
         state = jnp.pad(state, ((0, 0), (0, 0), (0, extra), (0, 0)))
         fresh_narrow = jnp.pad(fresh_narrow, ((0, 0), (0, 0), (0, extra), (0, 0)))
-    where = jnp.concatenate([(position * pairs).astype(jnp.int32).reshape(1), slot])
-    columns = [
-        jnp.pad(
-            legendre[:, :, k * LANES : (k + 1) * LANES],
-            ((0, extra), (0, tiles * LANES - row_length), (0, 0)),
-        )
-        for k in range(chunk_count)
-    ]
+    slots = 2 * trajectories
+    direct = split == 1
+    if direct:
+        order = jnp.bitwise_xor(position.astype(jnp.int32), jnp.arange(space, dtype=jnp.int32))
+        slot_order = order
+    else:
+        order = jnp.arange(space, dtype=jnp.int32)
+        slot_order = jnp.arange(slots, dtype=jnp.int32)
+    where = jnp.concatenate([(position * pairs).astype(jnp.int32).reshape(1), slot, slot_order])
+    columns = jnp.transpose(legendre, (1, 0, 2))
+    if extra:
+        columns = jnp.pad(columns, ((0, 0), (0, extra), (0, 0)))
 
     smem = pl.BlockSpec(memory_space=pltpu.SMEM)
     state_spec = pl.BlockSpec((trajectories, comps, SUB, row_length), lambda i: (0, 0, i, 0))
-    wire_shape = (2 * trajectories, fields, 4 * padded_pairs, LANES)
-    wire_spec = pl.BlockSpec(wire_shape, lambda i: (0, 0, 0, 0))
-
     fresh_spec = pl.BlockSpec((count, comps, SUB, row_length), lambda i: (0, 0, i, 0))
-    leg_spec = pl.BlockSpec((SUB, tiles * LANES, LANES), lambda i: (i, 0, 0))
-
-    limit = 60 * 1024 * 1024
-
-    def forward(k):
+    kept_spec = pl.BlockSpec((SUB, tiles * LANES, LANES), lambda i: (i, 0, 0))
+    part_shape = (fields, 4 * padded_pairs, LANES)
+    part_spec = pl.BlockSpec(part_shape, lambda i: (0, 0, 0))
+
+    def leg_spec(k):
+        return pl.BlockSpec((row_length, SUB, LANES), lambda i: (0, i, k))
+
+    mib = 1024 * 1024
+
+    def forward(k, where):
+        keep = k == chunk_count - 1
+        kept_shape = jax.ShapeDtypeStruct((padded_pairs, tiles * LANES, LANES), jnp.bfloat16)
         return pl.pallas_call(
-            functools.partial(forward_kernel, truncation=truncation, pairs=padded_pairs),
-            out_shape=jax.ShapeDtypeStruct(wire_shape, jnp.bfloat16),
+            functools.partial(
+                forward_kernel, truncation=truncation, pairs=padded_pairs, keep=keep
+            ),
+            out_shape=[jax.ShapeDtypeStruct(part_shape, jnp.bfloat16)] * slots
+            + [kept_shape] * keep,
             grid=(steps,),
-            in_specs=[smem, state_spec, fresh_spec, leg_spec],
-            out_specs=wire_spec,
+            in_specs=[smem, state_spec, fresh_spec, leg_spec(k)],
+            out_specs=[part_spec] * slots + [kept_spec] * keep,
             scratch_shapes=[
+                pltpu.VMEM((tiles * LANES * SUB, LANES), jnp.float32),
                 pltpu.VMEM((tiles, rows * SUB, LANES), jnp.float32),
                 pltpu.VMEM((4 * rows * padded_pairs, LANES), jnp.float32),
             ],
-            compiler_params=pltpu.CompilerParams(vmem_limit_bytes=limit),
+            compiler_params=pltpu.CompilerParams(vmem_limit_bytes=60 * mib),
             cost_estimate=pl.CostEstimate(
                 flops=8 * rows * padded_pairs * row_length * LANES,
                 bytes_accessed=16 * 1024 * 1024,
                 transcendentals=0,
             ),
             name="forward",
-        )(where, state, fresh_narrow, columns[k])
+        )(where, state, fresh_narrow, columns)
 
     def to_wire(x):
         if extra:
-            x = x.reshape(2 * trajectories, fields, 4, padded_pairs, LANES)[:, :, :, :pairs]
-            x = x.reshape(2 * trajectories, fields, 4 * pairs, LANES)
-        if split > 1:
-            x = x.reshape(2 * trajectories, fields, 4 * pairs, split, lane_count)
-            x = jnp.transpose(x, (0, 3, 1, 2, 4)).reshape(space, fields, 4 * pairs, lane_count)
-        return x
+            x = x.reshape(slots, fields, 4, padded_pairs, LANES)[:, :, :, :pairs]
+        x = x.reshape(slots, fields, 4 * pairs, split, lane_count)
+        return jnp.transpose(x, (0, 3, 1, 2, 4)).reshape(space, fields, 4 * pairs, lane_count)
 
     def from_wire(x):
-        if split > 1:
-            x = x.reshape(2 * trajectories, split, fields, 4 * pairs, lane_count)
-            x = jnp.transpose(x, (0, 2, 3, 1, 4))
-            x = x.reshape(2 * trajectories, fields, 4 * pairs, LANES)
+        x = x.reshape(slots, split, fields, 4, pairs, lane_count)
+        x = jnp.transpose(x, (0, 2, 3, 4, 1, 5)).reshape(slots, fields, 4, pairs, LANES)
         if extra:
-            x = x.reshape(2 * trajectories, fields, 4, pairs, LANES)
             x = jnp.pad(x, ((0, 0), (0, 0), (0, 0), (0, extra), (0, 0)))
-            x = x.reshape(wire_shape)
-        return x
+        return x.reshape((slots,) + part_shape)
 
     def exchange(x):
         return lax.all_to_all(x, "space", split_axis=0, concat_axis=0, tiled=True)
+
+    def swap(parts):
+        return [
+            lax.ppermute(x, "space", [(d, d ^ n) for d in range(space)]) if n else x
+            for n, x in enumerate(parts)
+        ]
+
+    def spread(parts):
+        if direct:
+            return swap(parts)
+        x = exchange(to_wire(jnp.stack(parts)))
+        x = jnp.pad(x, ((0, 0), (0, 0), (0, 0), (0, LANES - lane_count)))
+        return [x[d] for d in range(space)]
+
+    def collect(parts):
+        if direct:
+            return swap(parts)
+        x = from_wire(exchange(jnp.stack(parts)[..., :lane_count]))
+        return [x[n] for n in range(slots)]
 
     analysis = lax.optimization_barrier(
         fourier_tables(pairs * space, space, truncation, longitudes)
@@ -368,70 +445,90 @@
     vmem = pl.BlockSpec(memory_space=pltpu.VMEM)
     modes = 4 * pairs * space
 
-    def grid(k, x):
+    def grid(k, parts):
         first = k * LANES + position % split * lane_count
         mu = lax.dynamic_slice_in_dim(hemisphere, first, lane_count)
         weight = lax.dynamic_slice_in_dim(weights_all, first, lane_count)
-        if split > 1:
-            short = LANES - lane_count
+        short = LANES - lane_count
+        if short:
             mu = jnp.pad(mu, (0, short))
             weight = jnp.pad(weight, (0, short))
-            x = jnp.pad(x, ((0, 0), (0, 0), (0, 0), (0, short)))
-        out = pl.pallas_call(
+        return pl.pallas_call(
             functools.partial(grid_kernel, scale=1.0 / truncation),
-            out_shape=jax.ShapeDtypeStruct(x.shape, jnp.bfloat16),
-            in_specs=[vmem] * 5,
-            out_specs=vmem,
+            out_shape=[jax.ShapeDtypeStruct(x.shape, jnp.bfloat16) for x in parts],
+            in_specs=[smem] + [vmem] * (4 + space),
+            out_specs=[vmem] * space,
             scratch_shapes=[
                 pltpu.VMEM((modes, fields * LANES), jnp.bfloat16),
                 pltpu.VMEM((longitudes, fields * LANES), jnp.bfloat16),
             ],
-            compiler_params=pltpu.CompilerParams(vmem_limit_bytes=limit),
+            compiler_params=pltpu.CompilerParams(vmem_limit_bytes=60 * mib),
             cost_estimate=pl.CostEstimate(
                 flops=4 * modes * longitudes * fields * LANES,
                 bytes_accessed=12 * 1024 * 1024,
                 transcendentals=0,
             ),
             name="grid",
-        )((2.0 * mu)[None], weight[None], x, synthesis, analysis)
-        return out[..., :lane_count] if split > 1 else out
-
-    def inverse(ws, first, last, part):
+        )(order, (2.0 * mu)[None], weight[None], synthesis, analysis, *parts)
+
+    def inverse(ws, first, kept, part):
         chunks = len(ws)
+        last = kept is not None
         extra_in = [part, state, fresh] if last else []
+        wide_scratch = pltpu.VMEM((chunks, tiles * LANES * SUB, LANES), jnp.float32)
+        legs = [kept] if last else [columns] * chunks
         return pl.pallas_call(
             functools.partial(
-                inverse_kernel, truncation=truncation, pairs=padded_pairs, chunks=chunks, last=last
+                inverse_kernel,
+                truncation=truncation,
+                pairs=padded_pairs,
+                chunks=chunks,
+                last=last,
+                slots=slots,
             ),
             out_shape=jax.ShapeDtypeStruct(state.shape, jnp.float32),
             grid=(steps,),
             in_specs=[smem] * 3
-            + [wire_spec] * chunks
-            + [leg_spec] * chunks
+            + [part_spec] * (chunks * slots)
+            + ([kept_spec] if last else [leg_spec(first + k) for k in range(chunks)])
             + [state_spec, state_spec, fresh_spec][: len(extra_in)],
             out_specs=state_spec,
             scratch_shapes=[
                 pltpu.VMEM((chunks, 4 * rows * padded_pairs, LANES), jnp.float32),
                 pltpu.VMEM((tiles, rows * SUB, LANES), jnp.float32),
-            ],
-            compiler_params=pltpu.CompilerParams(vmem_limit_bytes=limit),
+            ]
+            + ([] if last else [wide_scratch]),
+            compiler_params=pltpu.CompilerParams(vmem_limit_bytes=60 * mib),
             cost_estimate=pl.CostEstimate(
                 flops=8 * rows * padded_pairs * row_length * LANES * chunks,
                 bytes_accessed=20 * 1024 * 1024,
                 transcendentals=0,
             ),
             name="inverse",
-        )(where, gravity, stability, *ws, *columns[first : first + chunks], *extra_in)
-
-    made = [forward(k) for k in range(chunk_count)]
-    wide, _ = lax.optimization_barrier((living, made[1]))
-    fresh = jnp.stack([send_clone(wide[i], route[i]) for i in range(count)])
-    if extra:
-        fresh = jnp.pad(fresh, ((0, 0), (0, 0), (0, extra), (0, 0)))
-    sent = [exchange(to_wire(x)) for x in made]
-    back = [from_wire(exchange(grid(k, x))) for k, x in enumerate(sent)]
-    part = inverse(back[:-1], 0, False, None)
-    out = inverse(back[-1:], chunk_count - 1, True, part)
+        )(where, gravity, stability, *[x for w in ws for x in w], *legs, *extra_in)
+
+    made, turn = [], where
+    for k in range(chunk_count):
+        made.append(list(forward(k, turn)))
+        turn, made[-1][0] = lax.optimization_barrier((where, made[-1][0]))
+    kept = made[-1][-1]
+    sent = []
+    for x in made:
+        sent.append(spread(x[:slots]))
+    back = []
+    for k in range(chunk_count):
+        parts = sent[k]
+        if k == 1:
+            parts, fresh = lax.optimization_barrier((parts, fresh))
+        got = grid(k, parts)
+        if k == 0:
+            wide, got = lax.optimization_barrier((living, got))
+            fresh = jnp.stack([send_clone(wide[i], route[i]) for i in range(count)])
+            if extra:
+                fresh = jnp.pad(fresh, ((0, 0), (0, 0), (0, extra), (0, 0)))
+        back.append(collect(got))
+    part = inverse(back[:-1], 0, None, None)
+    out = inverse(back[-1:], chunk_count - 1, kept, part)
     return out[:, :, :pairs] if extra else out
 
 

time: 407 us -> 382 us (0.939)
  the two profiles are of different devices: /device:TPU:1 before, /device:TPU:8 now
where the time goes in v3:
time: 382 us; the launch traced here: 381 us
  waiting for transfers between devices  147 us (38%)
  Pallas kernels  121 us (32%)
  starting transfers between devices  72.3 us (19%)
  other arithmetic  25.7 us (7%)
  local copies, waits for them, and re-layouts  9.95 us (3%)
  between operations  5.58 us (1%)
    ppermute x42, waiting for transfers between devices, swap(): lax.ppermute(x, 'space', [(d, d ^ n) for d in range(space)])  98.7 us
    ppermute x42, starting transfers between devices, swap(): lax.ppermute(x, 'space', [(d, d ^ n) for d in range(space)])  66.3 us
    ppermute x4, waiting for transfers between devices, move(): return lambda v: lax.ppermute(v, 'member', [(a, b)])  47.9 us
    pallas_call x3, Pallas kernels, grid(): pl.pallas_call(functools.partial(grid_kernel, scale=1.0 / truncation), ou...  43.1 us
    pallas_call x3, Pallas kernels, forward(): pl.pallas_call(functools.partial(forward_kernel, truncation=truncation, p...  42.4 us
    pallas_call x2, Pallas kernels, inverse(): pl.pallas_call(functools.partial(inverse_kernel, truncation=truncation, p...  35.6 us
    another operation x1, other arithmetic  15.2 us
  transfers between devices with their start and end apart: 46, of which 14 were waited for; matrix products, arithmetic and copies ran while one was open for 7% of the time, Pallas kernels for 24%

profile of v3, /device:TPU:8, one launch (start us, length us, event | category | flops | bytes accessed | tf_op | source)
XLA Modules:
  0.0 381.2 jit_solution(673085149264743574)
XLA Ops:
  10.9 20.6 %conditional.4 = (bf16[1,12,40,641]{3,2,1,0:T(8,128)(2,1)}) conditional(s32[]{:T(128)} %bitcast.36, f32[12,40,641]{2,1,0:T(8,128)S(1)} %get-tuple-element.330, f32[12,40,641]{2,1,0:T(8,128)S(1)} %get-tuple-element.330, f32[12,40,641]{2,1,0:T(8,128)S(1)} %get-tuple-element.330, ...), branch_computations={%region_0.1_spmd, %region_1.2_spmd, %region_2.3_spmd, %region_3.4_... | conditional | flops 307680 | bytes 4307568 | solution.py:320
  12.3 19.2 %collective-permute-done.9 = bf16[12,40,641]{2,1,0:T(8,128)(2,1)} collective-permute-done((bf16[12,40,641]{2,1,0:T(8,128)(2,1)S(1)}, bf16[12,40,641]{2,1,0:T(8,128)(2,1)}, u32[]{:S(2)}, u32[]{:S(2)}) %collective-permute-start.9) | collective-permute-done | bytes 615392 | tf_op jit(solution)/shard_map/cond/branch_12_fun/ppermute | solution.py:317
  34.7 13.8 %forward.3 = (bf16[6,160,128]{2,1,0:T(8,128)(2,1)}, bf16[6,160,128]{2,1,0:T(8,128)(2,1)}, bf16[6,160,128]{2,1,0:T(8,128)(2,1)}, bf16[6,160,128]{2,1,0:T(8,128)(2...) custom-call(s32[11]{0:T(128)} %pad_add_fusion.where_ref, ...), custom_call_target="tpu_custom_call" | custom-call | flops 1260257280 | bytes 16777216 | tf_op jit(solution)/shard_map/forward/pallas_call | solution.py:380
  55.9 15.2 %fusion.7 = (bf16[1280,640]{1,0:T(8,128)(2,1)S(1)}, bf16[1280,640]{1,0:T(8,128)(2,1)S(1)}) fusion(s32[1280]{0:T(1024)S(1)} %get-tuple-element.377, s32[1280]{0:T(1024)S(1)} %get-tuple-element.376, pred[1280]{0:T(1024)(128)(4,1)S(1)} %fusion.22), kind=kLoop, calls=%fused_computation.20 | loop fusion | flops 11468800 | bytes 3288320 | tf_op jit(solution)/shard_map/convert
  73.1 13.8 %forward.4 = (bf16[6,160,128]{2,1,0:T(8,128)(2,1)}, bf16[6,160,128]{2,1,0:T(8,128)(2,1)}, bf16[6,160,128]{2,1,0:T(8,128)(2,1)}, bf16[6,160,128]{2,1,0:T(8,128)(2...) custom-call(s32[11]{0:T(128)} %pad_add_fusion.where_ref, ...), custom_call_target="tpu_custom_call" | custom-call | flops 1260257280 | bytes 16777216 | tf_op jit(solution)/shard_map/forward/pallas_call | solution.py:380
  89.0 14.8 %forward.5 = (bf16[6,160,128]{2,1,0:T(8,128)(2,1)}, bf16[6,160,128]{2,1,0:T(8,128)(2,1)}, bf16[6,160,128]{2,1,0:T(8,128)(2,1)}, bf16[6,160,128]{2,1,0:T(8,128)(2...) custom-call(s32[11]{0:T(128)} %pad_add_fusion.where_ref, ...), custom_call_target="tpu_custom_call" | custom-call | flops 1260257280 | bytes 16777216 | tf_op jit(solution)/shard_map/forward/pallas_call | solution.py:380
  103.7 5.7 %copy.7.syn_ref = bf16[1280,1280]{1,0:T(8,128)(2,1)} copy(bf16[1280,1280]{0,1:T(8,128)(2,1)} %bitcast.70) | data formatting | bytes 6553600 | tf_op jit(solution)/shard_map/transpose | solution.py:441
  113.8 4.1 %collective-permute-start.51 = (bf16[6,160,128]{2,1,0:T(8,128)(2,1)}, bf16[6,160,128]{2,1,0:T(8,128)(2,1)}, u32[]{:S(2)}, u32[]{:S(2)}) collective-permute-start(bf16[6,160,128]{2,1,0:T(8,128)(2,1)} %get-tuple-element.285), channel_id=1, source_target_pairs={{0,4},{1,5},{2,6},{3,7},{4,0},{5,1},{6,2},{7,3},{8,12},{9,13},{10,... | collective-permute-start | bytes 737288 | tf_op jit(solution)/shard_map/ppermute | solution.py:421
  117.9 14.3 %grid.4 = (bf16[6,160,128]{2,1,0:T(8,128)(2,1)}, bf16[6,160,128]{2,1,0:T(8,128)(2,1)}, bf16[6,160,128]{2,1,0:T(8,128)(2,1)}, bf16[6,160,128]{2,1,0:T(8,128)(2,1)...) custom-call(s32[8]{0:T(128)} %copy-done.18, ...), custom_call_target="tpu_custom_call" | custom-call | flops 5033164800 | bytes 12582912 | tf_op jit(solution)/shard_map/grid/pallas_call | solution.py:456
  134.1 30.2 %conditional.6 = (f32[12,40,641]{2,1,0:T(8,128)}) conditional(s32[]{:T(128)} %bitcast.36, f32[12,40,641]{2,1,0:T(8,128)S(1)} %get-tuple-element.330, f32[12,40,641]{2,1,0:T(8,128)S(1)} %get-tuple-element.330, f32[12,40,641]{2,1,0:T(8,128)S(1)} %get-tuple-element.330, ...), branch_computations={%region_32.33_spmd, %region_33.34_spmd, %region_34.35_spmd, %regio... | conditional | bytes 4922928 | solution.py:320
  135.5 28.7 %collective-permute-done.33 = f32[12,40,641]{2,1,0:T(8,128)} collective-permute-done((f32[12,40,641]{2,1,0:T(8,128)S(1)}, f32[12,40,641]{2,1,0:T(8,128)}, u32[]{:S(2)}, u32[]{:S(2)}) %collective-permute-start.33) | collective-permute-done | bytes 1230752 | tf_op jit(solution)/shard_map/cond/branch_12_fun/ppermute | solution.py:317
  171.4 19.3 %collective-permute-done.52.refs_5_ = bf16[6,160,128]{2,1,0:T(8,128)(2,1)S(1)} collective-permute-done((bf16[6,160,128]{2,1,0:T(8,128)(2,1)}, bf16[6,160,128]{2,1,0:T(8,128)(2,1)S(1)}, u32[]{:S(2)}, u32[]{:S(2)}) %collective-permute-start.52) | collective-permute-done | bytes 245792 | tf_op jit(solution)/shard_map/ppermute | solution.py:421
  190.8 3.8 %collective-permute-start.78 = (bf16[6,160,128]{2,1,0:T(8,128)(2,1)S(1)}, bf16[6,160,128]{2,1,0:T(8,128)(2,1)S(1)}, u32[]{:S(2)}, u32[]{:S(2)}) collective-permute-start(bf16[6,160,128]{2,1,0:T(8,128)(2,1)S(1)} %copy-done.25), channel_id=1, source_target_pairs={{0,3},{1,2},{2,1},{3,0},{4,7},{5,6},{6,5},{7,4},{8,11},{9,10},{10,... | collective-permute-start | bytes 737288 | tf_op jit(solution)/shard_map/ppermute | solution.py:421
  194.6 2.9 collective-permute-done.53.refs_6_
  197.5 8.1 %collective-permute-done.54.refs_7_ = bf16[6,160,128]{2,1,0:T(8,128)(2,1)S(1)} collective-permute-done((bf16[6,160,128]{2,1,0:T(8,128)(2,1)}, bf16[6,160,128]{2,1,0:T(8,128)(2,1)S(1)}, u32[]{:S(2)}, u32[]{:S(2)}) %collective-permute-start.54) | collective-permute-done | bytes 245792 | tf_op jit(solution)/shard_map/ppermute | solution.py:421
  208.5 14.4 %grid.3 = (bf16[6,160,128]{2,1,0:T(8,128)(2,1)}, bf16[6,160,128]{2,1,0:T(8,128)(2,1)}, bf16[6,160,128]{2,1,0:T(8,128)(2,1)}, bf16[6,160,128]{2,1,0:T(8,128)(2,1)...) custom-call(s32[8]{0:T(128)} %copy-done.18, ...), custom_call_target="tpu_custom_call" | custom-call | flops 5033164800 | bytes 12582912 | tf_op jit(solution)/shard_map/grid/pallas_call | solution.py:456
  223.8 3.7 pad_maximum_fusion.1.refs_11_
  227.5 5.0 %collective-permute-start.56 = (bf16[6,160,128]{2,1,0:T(8,128)(2,1)S(1)}, bf16[6,160,128]{2,1,0:T(8,128)(2,1)S(1)}, u32[]{:S(2)}, u32[]{:S(2)}) collective-permute-start(bf16[6,160,128]{2,1,0:T(8,128)(2,1)S(1)} %copy-done.40), channel_id=1, source_target_pairs={{0,2},{1,3},{2,0},{3,1},{4,6},{5,7},{6,4},{7,5},{8,10},{9,11},{10,... | collective-permute-start | bytes 737288 | tf_op jit(solution)/shard_map/ppermute | solution.py:421
  236.2 2.9 collective-permute-start.72
  239.1 14.4 %grid.5 = (bf16[6,160,128]{2,1,0:T(8,128)(2,1)}, bf16[6,160,128]{2,1,0:T(8,128)(2,1)}, bf16[6,160,128]{2,1,0:T(8,128)(2,1)}, bf16[6,160,128]{2,1,0:T(8,128)(2,1)...) custom-call(s32[8]{0:T(128)} %copy-done.18, ...), custom_call_target="tpu_custom_call" | custom-call | flops 5033164800 | bytes 12582912 | tf_op jit(solution)/shard_map/grid/pallas_call | solution.py:456
  260.0 3.4 collective-permute-start.84
  263.4 14.4 %collective-permute-done.73.refs_5_ = bf16[6,160,128]{2,1,0:T(8,128)(2,1)S(1)} collective-permute-done((bf16[6,160,128]{2,1,0:T(8,128)(2,1)S(1)}, bf16[6,160,128]{2,1,0:T(8,128)(2,1)S(1)}, u32[]{:S(2)}, u32[]{:S(2)}) %collective-permute-start.73) | collective-permute-done | bytes 245792 | tf_op jit(solution)/shard_map/ppermute | solution.py:421
  277.8 4.0 %collective-permute-start.85 = (bf16[6,160,128]{2,1,0:T(8,128)(2,1)}, bf16[6,160,128]{2,1,0:T(8,128)(2,1)S(1)}, u32[]{:S(2)}, u32[]{:S(2)}) collective-permute-start(bf16[6,160,128]{2,1,0:T(8,128)(2,1)} %get-tuple-element.343), channel_id=1, source_target_pairs={{0,3},{1,2},{2,1},{3,0},{4,7},{5,6},{6,5},{7,4},{8,11},{9,10},{10,... | collective-permute-start | bytes 737288 | tf_op jit(solution)/shard_map/ppermute | solution.py:421
  281.8 10.7 %collective-permute-done.74.refs_6_ = bf16[6,160,128]{2,1,0:T(8,128)(2,1)S(1)} collective-permute-done((bf16[6,160,128]{2,1,0:T(8,128)(2,1)S(1)}, bf16[6,160,128]{2,1,0:T(8,128)(2,1)S(1)}, u32[]{:S(2)}, u32[]{:S(2)}) %collective-permute-start.74) | collective-permute-done | bytes 245792 | tf_op jit(solution)/shard_map/ppermute | solution.py:421
  292.6 12.0 %collective-permute-done.75.refs_7_ = bf16[6,160,128]{2,1,0:T(8,128)(2,1)S(1)} collective-permute-done((bf16[6,160,128]{2,1,0:T(8,128)(2,1)S(1)}, bf16[6,160,128]{2,1,0:T(8,128)(2,1)S(1)}, u32[]{:S(2)}, u32[]{:S(2)}) %collective-permute-start.75) | collective-permute-done | bytes 245792 | tf_op jit(solution)/shard_map/ppermute | solution.py:421
  306.1 5.0 %collective-permute-start.57 = (bf16[6,160,128]{2,1,0:T(8,128)(2,1)}, bf16[6,160,128]{2,1,0:T(8,128)(2,1)S(1)}, u32[]{:S(2)}, u32[]{:S(2)}) collective-permute-start(bf16[6,160,128]{2,1,0:T(8,128)(2,1)} %get-tuple-element.292), channel_id=1, source_target_pairs={{0,3},{1,2},{2,1},{3,0},{4,7},{5,6},{6,5},{7,4},{8,11},{9,10},{10,... | collective-permute-start | bytes 737288 | tf_op jit(solution)/shard_map/ppermute | solution.py:421
  312.3 10.4 %collective-permute-done.87.refs_13_ = bf16[6,160,128]{2,1,0:T(8,128)(2,1)S(1)} collective-permute-done((bf16[6,160,128]{2,1,0:T(8,128)(2,1)}, bf16[6,160,128]{2,1,0:T(8,128)(2,1)S(1)}, u32[]{:S(2)}, u32[]{:S(2)}) %collective-permute-start.87) | collective-permute-done | bytes 245792 | tf_op jit(solution)/shard_map/ppermute | solution.py:421
  322.8 4.2 %collective-permute-start.59 = (bf16[6,160,128]{2,1,0:T(8,128)(2,1)}, bf16[6,160,128]{2,1,0:T(8,128)(2,1)S(1)}, u32[]{:S(2)}, u32[]{:S(2)}) collective-permute-start(bf16[6,160,128]{2,1,0:T(8,128)(2,1)} %get-tuple-element.294), channel_id=1, source_target_pairs={{0,5},{1,4},{2,7},{3,6},{4,1},{5,0},{6,3},{7,2},{8,13},{9,12},{10,... | collective-permute-start | bytes 737288 | tf_op jit(solution)/shard_map/ppermute | solution.py:421
  326.9 10.6 %collective-permute-done.88.refs_14_ = bf16[6,160,128]{2,1,0:T(8,128)(2,1)} collective-permute-done((bf16[6,160,128]{2,1,0:T(8,128)(2,1)}, bf16[6,160,128]{2,1,0:T(8,128)(2,1)}, u32[]{:S(2)}, u32[]{:S(2)}) %collective-permute-start.88) | collective-permute-done | bytes 245792 | tf_op jit(solution)/shard_map/ppermute | solution.py:421
  337.5 5.8 %collective-permute-done.89.refs_15_ = bf16[6,160,128]{2,1,0:T(8,128)(2,1)} collective-permute-done((bf16[6,160,128]{2,1,0:T(8,128)(2,1)}, bf16[6,160,128]{2,1,0:T(8,128)(2,1)}, u32[]{:S(2)}, u32[]{:S(2)}) %collective-permute-start.89) | collective-permute-done | bytes 245792 | tf_op jit(solution)/shard_map/ppermute | solution.py:421
  344.7 19.4 %inverse.2.refs_9_ = f32[4,12,40,641]{3,2,1,0:T(8,128)} custom-call(s32[11]{0:T(128)} %pad_add_fusion.where_ref, f32[2,2]{1,0:T(2,128)} %gravity_ref.3, f32[2,2]{1,0:T(2,128)} %stability_ref.3, bf16[6,160,128]{2,1,0:T(8,128)(2,1)} %get-tuple-element.314.refs_0_, bf16[6,160,128]{2,1,0:T(8,128)(2,1)} %copy-done.2, bf16[6,160,128]{2,1,0:T(8,128)(2,1)} %copy-done.3, ...), custom_call_target="tpu_custom_call" | custom-call | flops 2520514560 | bytes 20971520 | tf_op jit(solution)/shard_map/inverse/pallas_call | solution.py:480
  365.0 16.1 %inverse.3 = f32[4,12,40,641]{3,2,1,0:T(8,128)} custom-call(s32[11]{0:T(128)} %pad_add_fusion.where_ref, f32[2,2]{1,0:T(2,128)} %gravity_ref.3, f32[2,2]{1,0:T(2,128)} %stability_ref.3, bf16[6,160,128]{2,1,0:T(8,128)(2,1)} %get-tuple-element.289.refs_0_, bf16[6,160,128]{2,1,0:T(8,128)(2,1)} %copy-done, bf16[6,160,128]{2,1,0:T(8,128)(2,1)} %copy-done.1, ...), custom_call_target="tpu_custom_call" | custom-call | flops 1260257280 | bytes 20971520 | tf_op jit(solution)/shard_map/inverse/pallas_call | solution.py:480
  (178 shorter events, 58.9 us)
Async XLA Ops:
  48.5 38.4 %collective-permute-start.62 = (bf16[6,160,128]{2,1,0:T(8,128)(2,1)}, bf16[6,160,128]{2,1,0:T(8,128)(2,1)S(1)}, u32[]{:S(2)}, u32[]{:S(2)}) collective-permute-start(bf16[6,160,128]{2,1,0:T(8,128)(2,1)} %get-tuple-element.299), channel_id=1, source_target_pairs={{0,1},{1,0},{2,3},{3,2},{4,5},{5,4},{6,7},{7,6},{8,9},{9,8},{10,11... | collective-permute-start | bytes 737288 | tf_op jit(solution)/shard_map/ppermute | solution.py:421
  50.0 38.5 %collective-permute-start.63 = (bf16[6,160,128]{2,1,0:T(8,128)(2,1)}, bf16[6,160,128]{2,1,0:T(8,128)(2,1)}, u32[]{:S(2)}, u32[]{:S(2)}) collective-permute-start(bf16[6,160,128]{2,1,0:T(8,128)(2,1)} %get-tuple-element.300), channel_id=1, source_target_pairs={{0,2},{1,3},{2,0},{3,1},{4,6},{5,7},{6,4},{7,5},{8,10},{9,11},{10,... | collective-permute-start | bytes 737288 | tf_op jit(solution)/shard_map/ppermute | solution.py:421
  50.5 59.5 %collective-permute-start.64 = (bf16[6,160,128]{2,1,0:T(8,128)(2,1)}, bf16[6,160,128]{2,1,0:T(8,128)(2,1)}, u32[]{:S(2)}, u32[]{:S(2)}) collective-permute-start(bf16[6,160,128]{2,1,0:T(8,128)(2,1)} %get-tuple-element.301), channel_id=1, source_target_pairs={{0,3},{1,2},{2,1},{3,0},{4,7},{5,6},{6,5},{7,4},{8,11},{9,10},{10,... | collective-permute-start | bytes 737288 | tf_op jit(solution)/shard_map/ppermute | solution.py:421
  52.0 59.5 %collective-permute-start.65 = (bf16[6,160,128]{2,1,0:T(8,128)(2,1)}, bf16[6,160,128]{2,1,0:T(8,128)(2,1)}, u32[]{:S(2)}, u32[]{:S(2)}) collective-permute-start(bf16[6,160,128]{2,1,0:T(8,128)(2,1)} %get-tuple-element.302), channel_id=1, source_target_pairs={{0,4},{1,5},{2,6},{3,7},{4,0},{5,1},{6,2},{7,3},{8,12},{9,13},{10,... | collective-permute-start | bytes 737288 | tf_op jit(solution)/shard_map/ppermute | solution.py:421
  54.6 59.2 %collective-permute-start.66 = (bf16[6,160,128]{2,1,0:T(8,128)(2,1)}, bf16[6,160,128]{2,1,0:T(8,128)(2,1)}, u32[]{:S(2)}, u32[]{:S(2)}) collective-permute-start(bf16[6,160,128]{2,1,0:T(8,128)(2,1)} %get-tuple-element.303), channel_id=1, source_target_pairs={{0,5},{1,4},{2,7},{3,6},{4,1},{5,0},{6,3},{7,2},{8,13},{9,12},{10,... | collective-permute-start | bytes 737288 | tf_op jit(solution)/shard_map/ppermute | solution.py:421
  86.9 26.9 %collective-permute-start.67 = (bf16[6,160,128]{2,1,0:T(8,128)(2,1)}, bf16[6,160,128]{2,1,0:T(8,128)(2,1)}, u32[]{:S(2)}, u32[]{:S(2)}) collective-permute-start(bf16[6,160,128]{2,1,0:T(8,128)(2,1)} %get-tuple-element.304), channel_id=1, source_target_pairs={{0,6},{1,7},{2,4},{3,5},{4,2},{5,3},{6,0},{7,1},{8,14},{9,15},{10,... | collective-permute-start | bytes 737288 | tf_op jit(solution)/shard_map/ppermute | solution.py:421
  88.6 29.3 %collective-permute-start.68 = (bf16[6,160,128]{2,1,0:T(8,128)(2,1)}, bf16[6,160,128]{2,1,0:T(8,128)(2,1)}, u32[]{:S(2)}, u32[]{:S(2)}) collective-permute-start(bf16[6,160,128]{2,1,0:T(8,128)(2,1)} %get-tuple-element.305), channel_id=1, source_target_pairs={{0,7},{1,6},{2,5},{3,4},{4,3},{5,2},{6,1},{7,0},{8,15},{9,14},{10,... | collective-permute-start | bytes 737288 | tf_op jit(solution)/shard_map/ppermute | solution.py:421
  110.0 55.5 %collective-permute-start.48 = (bf16[6,160,128]{2,1,0:T(8,128)(2,1)}, bf16[6,160,128]{2,1,0:T(8,128)(2,1)S(1)}, u32[]{:S(2)}, u32[]{:S(2)}) collective-permute-start(bf16[6,160,128]{2,1,0:T(8,128)(2,1)} %get-tuple-element.282), channel_id=1, source_target_pairs={{0,1},{1,0},{2,3},{3,2},{4,5},{5,4},{6,7},{7,6},{8,9},{9,8},{10,11... | collective-permute-start | bytes 737288 | tf_op jit(solution)/shard_map/ppermute | solution.py:421
  111.6 55.5 %collective-permute-start.49 = (bf16[6,160,128]{2,1,0:T(8,128)(2,1)}, bf16[6,160,128]{2,1,0:T(8,128)(2,1)}, u32[]{:S(2)}, u32[]{:S(2)}) collective-permute-start(bf16[6,160,128]{2,1,0:T(8,128)(2,1)} %get-tuple-element.283), channel_id=1, source_target_pairs={{0,2},{1,3},{2,0},{3,1},{4,6},{5,7},{6,4},{7,5},{8,10},{9,11},{10,... | collective-permute-start | bytes 737288 | tf_op jit(solution)/shard_map/ppermute | solution.py:421
  113.8 53.7 %collective-permute-start.50 = (bf16[6,160,128]{2,1,0:T(8,128)(2,1)}, bf16[6,160,128]{2,1,0:T(8,128)(2,1)}, u32[]{:S(2)}, u32[]{:S(2)}) collective-permute-start(bf16[6,160,128]{2,1,0:T(8,128)(2,1)} %get-tuple-element.284), channel_id=1, source_target_pairs={{0,3},{1,2},{2,1},{3,0},{4,7},{5,6},{6,5},{7,4},{8,11},{9,10},{10,... | collective-permute-start | bytes 737288 | tf_op jit(solution)/shard_map/ppermute | solution.py:421
  113.8 55.2 %collective-permute-start.51 = (bf16[6,160,128]{2,1,0:T(8,128)(2,1)}, bf16[6,160,128]{2,1,0:T(8,128)(2,1)}, u32[]{:S(2)}, u32[]{:S(2)}) collective-permute-start(bf16[6,160,128]{2,1,0:T(8,128)(2,1)} %get-tuple-element.285), channel_id=1, source_target_pairs={{0,4},{1,5},{2,6},{3,7},{4,0},{5,1},{6,2},{7,3},{8,12},{9,13},{10,... | collective-permute-start | bytes 737288 | tf_op jit(solution)/shard_map/ppermute | solution.py:421
  134.1 30.1 %collective-permute-start.33 = (f32[12,40,641]{2,1,0:T(8,128)S(1)}, f32[12,40,641]{2,1,0:T(8,128)}, u32[]{:S(2)}, u32[]{:S(2)}) collective-permute-start(f32[12,40,641]{2,1,0:T(8,128)S(1)} %param.44), channel_id=1, source_target_pairs={{24,0},{25,1},{26,2},{27,3},{28,4},{29,5},{30,6},{31,7}} | collective-permute-start | bytes 3692168 | tf_op jit(solution)/shard_map/cond/branch_12_fun/ppermute | solution.py:317
  165.5 32.0 %collective-permute-start.53 = (bf16[6,160,128]{2,1,0:T(8,128)(2,1)}, bf16[6,160,128]{2,1,0:T(8,128)(2,1)S(1)}, u32[]{:S(2)}, u32[]{:S(2)}) collective-permute-start(bf16[6,160,128]{2,1,0:T(8,128)(2,1)} %get-tuple-element.287), channel_id=1, source_target_pairs={{0,6},{1,7},{2,4},{3,5},{4,2},{5,3},{6,0},{7,1},{8,14},{9,15},{10,... | collective-permute-start | bytes 737288 | tf_op jit(solution)/shard_map/ppermute | solution.py:421
  167.0 38.6 %collective-permute-start.54 = (bf16[6,160,128]{2,1,0:T(8,128)(2,1)}, bf16[6,160,128]{2,1,0:T(8,128)(2,1)S(1)}, u32[]{:S(2)}, u32[]{:S(2)}) collective-permute-start(bf16[6,160,128]{2,1,0:T(8,128)(2,1)} %get-tuple-element.288), channel_id=1, source_target_pairs={{0,7},{1,6},{2,5},{3,4},{4,3},{5,2},{6,1},{7,0},{8,15},{9,14},{10,... | collective-permute-start | bytes 737288 | tf_op jit(solution)/shard_map/ppermute | solution.py:421
  167.5 38.2 %collective-permute-start.76 = (bf16[6,160,128]{2,1,0:T(8,128)(2,1)S(1)}, bf16[6,160,128]{2,1,0:T(8,128)(2,1)S(1)}, u32[]{:S(2)}, u32[]{:S(2)}) collective-permute-start(bf16[6,160,128]{2,1,0:T(8,128)(2,1)S(1)} %copy-done.31), channel_id=1, source_target_pairs={{0,1},{1,0},{2,3},{3,2},{4,5},{5,4},{6,7},{7,6},{8,9},{9,8},{10,11... | collective-permute-start | bytes 737288 | tf_op jit(solution)/shard_map/ppermute | solution.py:421
  169.0 37.2 %collective-permute-start.77 = (bf16[6,160,128]{2,1,0:T(8,128)(2,1)S(1)}, bf16[6,160,128]{2,1,0:T(8,128)(2,1)S(1)}, u32[]{:S(2)}, u32[]{:S(2)}) collective-permute-start(bf16[6,160,128]{2,1,0:T(8,128)(2,1)S(1)} %copy-done.30), channel_id=1, source_target_pairs={{0,2},{1,3},{2,0},{3,1},{4,6},{5,7},{6,4},{7,5},{8,10},{9,11},{10,... | collective-permute-start | bytes 737288 | tf_op jit(solution)/shard_map/ppermute | solution.py:421
  190.8 32.1 %collective-permute-start.78 = (bf16[6,160,128]{2,1,0:T(8,128)(2,1)S(1)}, bf16[6,160,128]{2,1,0:T(8,128)(2,1)S(1)}, u32[]{:S(2)}, u32[]{:S(2)}) collective-permute-start(bf16[6,160,128]{2,1,0:T(8,128)(2,1)S(1)} %copy-done.25), channel_id=1, source_target_pairs={{0,3},{1,2},{2,1},{3,0},{4,7},{5,6},{6,5},{7,4},{8,11},{9,10},{10,... | collective-permute-start | bytes 737288 | tf_op jit(solution)/shard_map/ppermute | solution.py:421
  197.5 30.0 %collective-permute-start.79 = (bf16[6,160,128]{2,1,0:T(8,128)(2,1)S(1)}, bf16[6,160,128]{2,1,0:T(8,128)(2,1)S(1)}, u32[]{:S(2)}, u32[]{:S(2)}) collective-permute-start(bf16[6,160,128]{2,1,0:T(8,128)(2,1)S(1)} %copy-done.23), channel_id=1, source_target_pairs={{0,4},{1,5},{2,6},{3,7},{4,0},{5,1},{6,2},{7,3},{8,12},{9,13},{10,... | collective-permute-start | bytes 737288 | tf_op jit(solution)/shard_map/ppermute | solution.py:421
  205.7 26.9 %collective-permute-start.80 = (bf16[6,160,128]{2,1,0:T(8,128)(2,1)S(1)}, bf16[6,160,128]{2,1,0:T(8,128)(2,1)}, u32[]{:S(2)}, u32[]{:S(2)}) collective-permute-start(bf16[6,160,128]{2,1,0:T(8,128)(2,1)S(1)} %copy-done.21), channel_id=1, source_target_pairs={{0,5},{1,4},{2,7},{3,6},{4,1},{5,0},{6,3},{7,2},{8,13},{9,12},{10,... | collective-permute-start | bytes 737288 | tf_op jit(solution)/shard_map/ppermute | solution.py:421
  205.7 27.1 %collective-permute-start.81 = (bf16[6,160,128]{2,1,0:T(8,128)(2,1)S(1)}, bf16[6,160,128]{2,1,0:T(8,128)(2,1)S(1)}, u32[]{:S(2)}, u32[]{:S(2)}) collective-permute-start(bf16[6,160,128]{2,1,0:T(8,128)(2,1)S(1)} %copy-done.20), channel_id=1, source_target_pairs={{0,6},{1,7},{2,4},{3,5},{4,2},{5,3},{6,0},{7,1},{8,14},{9,15},{10,... | collective-permute-start | bytes 737288 | tf_op jit(solution)/shard_map/ppermute | solution.py:421
  206.2 27.4 %collective-permute-start.82 = (bf16[6,160,128]{2,1,0:T(8,128)(2,1)S(1)}, bf16[6,160,128]{2,1,0:T(8,128)(2,1)S(1)}, u32[]{:S(2)}, u32[]{:S(2)}) collective-permute-start(bf16[6,160,128]{2,1,0:T(8,128)(2,1)S(1)} %copy-done.19), channel_id=1, source_target_pairs={{0,7},{1,6},{2,5},{3,4},{4,3},{5,2},{6,1},{7,0},{8,15},{9,14},{10,... | collective-permute-start | bytes 737288 | tf_op jit(solution)/shard_map/ppermute | solution.py:421
  254.2 38.4 %collective-permute-start.74 = (bf16[6,160,128]{2,1,0:T(8,128)(2,1)S(1)}, bf16[6,160,128]{2,1,0:T(8,128)(2,1)S(1)}, u32[]{:S(2)}, u32[]{:S(2)}) collective-permute-start(bf16[6,160,128]{2,1,0:T(8,128)(2,1)S(1)} %copy-done.24), channel_id=1, source_target_pairs={{0,6},{1,7},{2,4},{3,5},{4,2},{5,3},{6,0},{7,1},{8,14},{9,15},{10,... | collective-permute-start | bytes 737288 | tf_op jit(solution)/shard_map/ppermute | solution.py:421
  256.7 47.9 %collective-permute-start.75 = (bf16[6,160,128]{2,1,0:T(8,128)(2,1)S(1)}, bf16[6,160,128]{2,1,0:T(8,128)(2,1)S(1)}, u32[]{:S(2)}, u32[]{:S(2)}) collective-permute-start(bf16[6,160,128]{2,1,0:T(8,128)(2,1)S(1)} %copy-done.22), channel_id=1, source_target_pairs={{0,7},{1,6},{2,5},{3,4},{4,3},{5,2},{6,1},{7,0},{8,15},{9,14},{10,... | collective-permute-start | bytes 737288 | tf_op jit(solution)/shard_map/ppermute | solution.py:421
  259.5 45.1 %collective-permute-start.83 = (bf16[6,160,128]{2,1,0:T(8,128)(2,1)}, bf16[6,160,128]{2,1,0:T(8,128)(2,1)S(1)}, u32[]{:S(2)}, u32[]{:S(2)}) collective-permute-start(bf16[6,160,128]{2,1,0:T(8,128)(2,1)} %get-tuple-element.341), channel_id=1, source_target_pairs={{0,1},{1,0},{2,3},{3,2},{4,5},{5,4},{6,7},{7,6},{8,9},{9,8},{10,11... | collective-permute-start | bytes 737288 | tf_op jit(solution)/shard_map/ppermute | solution.py:421
  260.0 45.6 %collective-permute-start.84 = (bf16[6,160,128]{2,1,0:T(8,128)(2,1)}, bf16[6,160,128]{2,1,0:T(8,128)(2,1)S(1)}, u32[]{:S(2)}, u32[]{:S(2)}) collective-permute-start(bf16[6,160,128]{2,1,0:T(8,128)(2,1)} %get-tuple-element.342), channel_id=1, source_target_pairs={{0,2},{1,3},{2,0},{3,1},{4,6},{5,7},{6,4},{7,5},{8,10},{9,11},{10,... | collective-permute-start | bytes 737288 | tf_op jit(solution)/shard_map/ppermute | solution.py:421
  277.8 28.3 %collective-permute-start.85 = (bf16[6,160,128]{2,1,0:T(8,128)(2,1)}, bf16[6,160,128]{2,1,0:T(8,128)(2,1)S(1)}, u32[]{:S(2)}, u32[]{:S(2)}) collective-permute-start(bf16[6,160,128]{2,1,0:T(8,128)(2,1)} %get-tuple-element.343), channel_id=1, source_target_pairs={{0,3},{1,2},{2,1},{3,0},{4,7},{5,6},{6,5},{7,4},{8,11},{9,10},{10,... | collective-permute-start | bytes 737288 | tf_op jit(solution)/shard_map/ppermute | solution.py:421
  304.6 32.9 %collective-permute-start.88 = (bf16[6,160,128]{2,1,0:T(8,128)(2,1)}, bf16[6,160,128]{2,1,0:T(8,128)(2,1)}, u32[]{:S(2)}, u32[]{:S(2)}) collective-permute-start(bf16[6,160,128]{2,1,0:T(8,128)(2,1)} %get-tuple-element.346), channel_id=1, source_target_pairs={{0,6},{1,7},{2,4},{3,5},{4,2},{5,3},{6,0},{7,1},{8,14},{9,15},{10,... | collective-permute-start | bytes 737288 | tf_op jit(solution)/shard_map/ppermute | solution.py:421
  305.7 37.6 %collective-permute-start.89 = (bf16[6,160,128]{2,1,0:T(8,128)(2,1)}, bf16[6,160,128]{2,1,0:T(8,128)(2,1)}, u32[]{:S(2)}, u32[]{:S(2)}) collective-permute-start(bf16[6,160,128]{2,1,0:T(8,128)(2,1)} %get-tuple-element.347), channel_id=1, source_target_pairs={{0,7},{1,6},{2,5},{3,4},{4,3},{5,2},{6,1},{7,0},{8,15},{9,14},{10,... | collective-permute-start | bytes 737288 | tf_op jit(solution)/shard_map/ppermute | solution.py:421
  306.1 58.0 %collective-permute-start.57 = (bf16[6,160,128]{2,1,0:T(8,128)(2,1)}, bf16[6,160,128]{2,1,0:T(8,128)(2,1)S(1)}, u32[]{:S(2)}, u32[]{:S(2)}) collective-permute-start(bf16[6,160,128]{2,1,0:T(8,128)(2,1)} %get-tuple-element.292), channel_id=1, source_target_pairs={{0,3},{1,2},{2,1},{3,0},{4,7},{5,6},{6,5},{7,4},{8,11},{9,10},{10,... | collective-permute-start | bytes 737288 | tf_op jit(solution)/shard_map/ppermute | solution.py:421
  311.1 53.0 %collective-permute-start.58 = (bf16[6,160,128]{2,1,0:T(8,128)(2,1)}, bf16[6,160,128]{2,1,0:T(8,128)(2,1)S(1)}, u32[]{:S(2)}, u32[]{:S(2)}) collective-permute-start(bf16[6,160,128]{2,1,0:T(8,128)(2,1)} %get-tuple-element.293), channel_id=1, source_target_pairs={{0,4},{1,5},{2,6},{3,7},{4,0},{5,1},{6,2},{7,3},{8,12},{9,13},{10,... | collective-permute-start | bytes 737288 | tf_op jit(solution)/shard_map/ppermute | solution.py:421
  322.8 41.4 %collective-permute-start.59 = (bf16[6,160,128]{2,1,0:T(8,128)(2,1)}, bf16[6,160,128]{2,1,0:T(8,128)(2,1)S(1)}, u32[]{:S(2)}, u32[]{:S(2)}) collective-permute-start(bf16[6,160,128]{2,1,0:T(8,128)(2,1)} %get-tuple-element.294), channel_id=1, source_target_pairs={{0,5},{1,4},{2,7},{3,6},{4,1},{5,0},{6,3},{7,2},{8,13},{9,12},{10,... | collective-permute-start | bytes 737288 | tf_op jit(solution)/shard_map/ppermute | solution.py:421
  337.5 26.7 %collective-permute-start.60 = (bf16[6,160,128]{2,1,0:T(8,128)(2,1)}, bf16[6,160,128]{2,1,0:T(8,128)(2,1)}, u32[]{:S(2)}, u32[]{:S(2)}) collective-permute-start(bf16[6,160,128]{2,1,0:T(8,128)(2,1)} %get-tuple-element.295), channel_id=1, source_target_pairs={{0,6},{1,7},{2,4},{3,5},{4,2},{5,3},{6,0},{7,1},{8,14},{9,15},{10,... | collective-permute-start | bytes 737288 | tf_op jit(solution)/shard_map/ppermute | solution.py:421
  (58 other events, 1757.3 us)

commit v4 on v3

--- a/solution.py
+++ b/solution.py
@@ -11,8 +11,9 @@
 
 LANES = 128
 SUB = 8
-UNROLL_FORWARD = 2
-UNROLL_INVERSE = 4
+PACKED = 16
+UNROLL_FORWARD = 8
+UNROLL_INVERSE = 8
 LONGITUDES_PER_WAVE = 2
 
 time_step = 0.25
@@ -29,19 +30,19 @@
     return leading, (offset & 1) == 1, order + offset
 
 
-def forward_kernel(where_ref, spec_ref, fresh_ref, leg_ref, *refs, truncation, pairs, keep):
+def forward_kernel(where_ref, spec_ref, leg_ref, *refs, truncation, pairs, keep, count):
     step = pl.program_id(0)
     row_length = truncation + 1
     trajectories, comps, block, _ = spec_ref.shape
     rows = trajectories * comps
     slots = 2 * trajectories
+    fresh_refs, refs = refs[:count], refs[count:]
     out_refs, refs = refs[:slots], refs[slots:]
     if keep:
         keep_ref, refs = refs[0], refs[1:]
     wide, xs, res = refs
     tiles = xs.shape[0]
     padded = tiles * LANES
-    count = fresh_ref.shape[0]
 
     @pl.when(step == 0)
     def _():
@@ -67,7 +68,7 @@
             at = pl.multiple_of(slot * comps * block, SUB)
             for k in range(tiles):
                 width = min(LANES, row_length - k * LANES)
-                fresh = fresh_ref[i, :, :, k * LANES : k * LANES + width].astype(jnp.float32)
+                fresh = fresh_refs[i][:, :, k * LANES : k * LANES + width].astype(jnp.float32)
                 xs[k, pl.ds(at, comps * block), :width] = fresh.reshape(comps * block, width)
 
     first_pair = where_ref[0] + step * block
@@ -76,12 +77,24 @@
         x = jnp.concatenate(
             [xs[k, pl.ds(q, rows, stride=block), :] for k in range(tiles)], axis=1
         )
-        leading, odd, _ = layout_terms(first_pair + q, 1, 0, padded, truncation)
-        lead = jnp.where(leading, x, 0.0)
-        trail = jnp.where(leading, 0.0, x)
-        lhs = jnp.concatenate(
-            [lead, trail, jnp.where(odd, -lead, lead), jnp.where(odd, -trail, trail)], axis=0
-        ).astype(jnp.bfloat16)
+        x = x.astype(jnp.bfloat16)
+        edge = truncation - first_pair - q
+        column = lax.broadcasted_iota(jnp.int32, (PACKED, padded), 1)
+        leading = column < edge
+        odd = (jnp.where(leading, column, column - edge) & 1) == 1
+        sign = jnp.where(odd, -1.0, 1.0)
+        factors = [
+            jnp.where(leading, 1.0, 0.0),
+            jnp.where(leading, 0.0, 1.0),
+            jnp.where(leading, sign, 0.0),
+            jnp.where(leading, 0.0, sign),
+        ]
+        lhs = []
+        for factor in factors:
+            factor = factor.astype(jnp.bfloat16)
+            for at in range(0, rows, PACKED):
+                lhs.append(x[at : at + PACKED] * factor)
+        lhs = jnp.concatenate(lhs, axis=0)
         rhs = wide[pl.ds(q, padded, stride=block), :].astype(jnp.bfloat16)
         if keep:
             keep_ref[q] = rhs
@@ -185,21 +198,21 @@
 
 
 def inverse_kernel(
-    where_ref, gravity_ref, stability_ref, *refs, truncation, pairs, chunks, last, slots
+    where_ref, gravity_ref, stability_ref, *refs, truncation, pairs, chunks, last, slots, count
 ):
     w_refs, refs = refs[: chunks * slots], refs[chunks * slots :]
     leg_refs, refs = refs[:chunks], refs[chunks:]
+    spec_ref, refs = refs[0], refs[1:]
     if last:
-        part_ref, spec_ref, fresh_ref, out_ref, ws, ten = refs
+        out_ref, ws, ten = refs
     else:
-        out_ref, ws, ten, wide = refs
+        fresh_refs, (out_ref, ws, ten, wide) = refs[:count], refs[count:]
     step = pl.program_id(0)
     row_length = truncation + 1
     trajectories, comps, block, _ = out_ref.shape
     rows = trajectories * comps
     tiles = ten.shape[0]
     padded = tiles * LANES
-    count = where_ref.shape[0] - 1 - slots
 
     @pl.when(step == 0)
     def _():
@@ -230,17 +243,18 @@
     first_pair = where_ref[0] + step * block
 
     def one(q, carry):
-        got = None
-        for k in range(chunks):
-            lhs = ws[k, pl.ds(step * block + q, 4 * rows, stride=pairs), :].astype(jnp.bfloat16)
-            if last:
-                rhs = leg_refs[k][q]
-            else:
-                rhs = wide[k, pl.ds(q, padded, stride=block), :].astype(jnp.bfloat16)
-            term = lax.dot_general(
-                lhs, rhs, (((1,), (1,)), ((), ())), preferred_element_type=jnp.float32
+        at = pl.ds(step * block + q, 4 * rows, stride=pairs)
+        lhs = jnp.concatenate([ws[k, at, :].astype(jnp.bfloat16) for k in range(chunks)], axis=1)
+        if last:
+            rhs = jnp.concatenate([leg_refs[k][q] for k in range(chunks)], axis=1)
+        else:
+            at = pl.ds(q, padded, stride=block)
+            rhs = jnp.concatenate(
+                [wide[k, at, :].astype(jnp.bfloat16) for k in range(chunks)], axis=1
             )
-            got = term if got is None else got + term
+        got = lax.dot_general(
+            lhs, rhs, (((1,), (1,)), ((), ())), preferred_element_type=jnp.float32
+        )
         leading, odd, _ = layout_terms(first_pair + q, 1, 0, padded, truncation)
         north = jnp.where(leading, got[:rows], got[rows : 2 * rows])
         south = jnp.where(leading, got[2 * rows : 3 * rows], got[3 * rows :])
@@ -266,13 +280,14 @@
                 at = pl.multiple_of((t * comps + c) * block, SUB)
                 value = ten[k, pl.ds(at, block), :][:, :width]
                 tend.append(value)
+            old = [spec_ref[t, c, :, lanes] for c in range(comps)]
             if last:
-                tend = [tend[c] + part_ref[t, c, :, lanes] for c in range(comps)]
-                old = [spec_ref[t, c, :, lanes] for c in range(comps)]
-                for i in range(fresh_ref.shape[0]):
+                tend = semi_implicit_slabs(old, tend, degree, gm, hm, truncation)
+            else:
+                for i in range(count):
                     mine = where_ref[1 + i] == t
-                    old = [jnp.where(mine, fresh_ref[i, c, :, lanes], old[c]) for c in range(comps)]
-                tend = semi_implicit_slabs(old, tend, degree, gm, hm, truncation)
+                    old = [jnp.where(mine, fresh_refs[i][c, :, lanes], old[c]) for c in range(comps)]
+                tend = [old[c] + time_step * tend[c] for c in range(comps)]
             for c in range(comps):
                 out_ref[t, c, :, lanes] = tend[c]
             return carry
@@ -305,7 +320,7 @@
     index = clones - owner * local
     route = owner[:, 1] * members + owner[:, 0]
     slot = jnp.where(owner[:, 0] == me, index[:, 0], -1)
-    return index[:, 1], route, slot
+    return index[:, 1], owner[:, 1], route, slot
 
 
 def send_clone(row, route):
@@ -318,6 +333,17 @@
 
     branches = [move(a, b) for a in range(members) for b in range(members)]
     return lax.switch(route, branches, row)
+
+
+def share_row(row, owner):
+    members = lax.axis_size("member")
+    differs = jnp.bitwise_xor(owner, lax.axis_index("member").astype(jnp.int32))
+    bit = 1
+    while bit < members:
+        other = lax.ppermute(row, "member", [(m, m ^ bit) for m in range(members)])
+        row = jnp.where(jnp.bitwise_and(differs, bit) != 0, other, row)
+        bit *= 2
+    return row
 
 
 def shards(spectra, legendre, sin_lat, gravity, stability, clones):
@@ -337,18 +363,16 @@
     extra = padded_pairs - pairs
     rows = trajectories * comps
 
-    survivor, route, slot = clone_routes(clones, trajectories)
+    survivor, owner, route, slot = clone_routes(clones, trajectories)
     count = clones.shape[0]
     living = [
         lax.dynamic_index_in_dim(spectra, survivor[i], 0, keepdims=False) for i in range(count)
     ]
-    fresh_narrow = jnp.stack(
-        [send_clone(living[i].astype(jnp.bfloat16), route[i]) for i in range(count)]
-    )
+    fresh_narrow = [send_clone(living[i].astype(jnp.bfloat16), route[i]) for i in range(count)]
     state = spectra
     if extra:
         state = jnp.pad(state, ((0, 0), (0, 0), (0, extra), (0, 0)))
-        fresh_narrow = jnp.pad(fresh_narrow, ((0, 0), (0, 0), (0, extra), (0, 0)))
+        fresh_narrow = [jnp.pad(x, ((0, 0), (0, extra), (0, 0))) for x in fresh_narrow]
     slots = 2 * trajectories
     direct = split == 1
     if direct:
@@ -364,7 +388,7 @@
 
     smem = pl.BlockSpec(memory_space=pltpu.SMEM)
     state_spec = pl.BlockSpec((trajectories, comps, SUB, row_length), lambda i: (0, 0, i, 0))
-    fresh_spec = pl.BlockSpec((count, comps, SUB, row_length), lambda i: (0, 0, i, 0))
+    fresh_spec = pl.BlockSpec((comps, SUB, row_length), lambda i: (0, i, 0))
     kept_spec = pl.BlockSpec((SUB, tiles * LANES, LANES), lambda i: (i, 0, 0))
     part_shape = (fields, 4 * padded_pairs, LANES)
     part_spec = pl.BlockSpec(part_shape, lambda i: (0, 0, 0))
@@ -375,16 +399,16 @@
     mib = 1024 * 1024
 
     def forward(k, where):
-        keep = k == chunk_count - 1
+        keep = k > 0
         kept_shape = jax.ShapeDtypeStruct((padded_pairs, tiles * LANES, LANES), jnp.bfloat16)
         return pl.pallas_call(
             functools.partial(
-                forward_kernel, truncation=truncation, pairs=padded_pairs, keep=keep
+                forward_kernel, truncation=truncation, pairs=padded_pairs, keep=keep, count=count
             ),
             out_shape=[jax.ShapeDtypeStruct(part_shape, jnp.bfloat16)] * slots
             + [kept_shape] * keep,
             grid=(steps,),
-            in_specs=[smem, state_spec, fresh_spec, leg_spec(k)],
+            in_specs=[smem, state_spec, leg_spec(k)] + [fresh_spec] * count,
             out_specs=[part_spec] * slots + [kept_spec] * keep,
             scratch_shapes=[
                 pltpu.VMEM((tiles * LANES * SUB, LANES), jnp.float32),
@@ -398,7 +422,7 @@
                 transcendentals=0,
             ),
             name="forward",
-        )(where, state, fresh_narrow, columns)
+        )(where, state, columns, *fresh_narrow)
 
     def to_wire(x):
         if extra:
@@ -471,12 +495,10 @@
             name="grid",
         )(order, (2.0 * mu)[None], weight[None], synthesis, analysis, *parts)
 
-    def inverse(ws, first, kept, part):
+    def inverse(ws, legs, start, patches):
         chunks = len(ws)
-        last = kept is not None
-        extra_in = [part, state, fresh] if last else []
+        last = not patches
         wide_scratch = pltpu.VMEM((chunks, tiles * LANES * SUB, LANES), jnp.float32)
-        legs = [kept] if last else [columns] * chunks
         return pl.pallas_call(
             functools.partial(
                 inverse_kernel,
@@ -485,13 +507,15 @@
                 chunks=chunks,
                 last=last,
                 slots=slots,
+                count=count,
             ),
             out_shape=jax.ShapeDtypeStruct(state.shape, jnp.float32),
             grid=(steps,),
             in_specs=[smem] * 3
             + [part_spec] * (chunks * slots)
-            + ([kept_spec] if last else [leg_spec(first + k) for k in range(chunks)])
-            + [state_spec, state_spec, fresh_spec][: len(extra_in)],
+            + ([kept_spec] * chunks if last else [leg_spec(k) for k in range(chunks)])
+            + [state_spec]
+            + [fresh_spec] * len(patches),
             out_specs=state_spec,
             scratch_shapes=[
                 pltpu.VMEM((chunks, 4 * rows * padded_pairs, LANES), jnp.float32),
@@ -505,30 +529,26 @@
                 transcendentals=0,
             ),
             name="inverse",
-        )(where, gravity, stability, *[x for w in ws for x in w], *legs, *extra_in)
+        )(where, gravity, stability, *[x for w in ws for x in w], *legs, start, *patches)
 
     made, turn = [], where
     for k in range(chunk_count):
         made.append(list(forward(k, turn)))
         turn, made[-1][0] = lax.optimization_barrier((where, made[-1][0]))
-    kept = made[-1][-1]
+    kept = [x[-1] for x in made[1:]]
     sent = []
     for x in made:
         sent.append(spread(x[:slots]))
+    wide, _ = lax.optimization_barrier((living, made[1][0]))
+    fresh = [share_row(wide[i], owner[i]) for i in range(count)]
+    if extra:
+        fresh = [jnp.pad(x, ((0, 0), (0, extra), (0, 0))) for x in fresh]
     back = []
     for k in range(chunk_count):
-        parts = sent[k]
-        if k == 1:
-            parts, fresh = lax.optimization_barrier((parts, fresh))
-        got = grid(k, parts)
-        if k == 0:
-            wide, got = lax.optimization_barrier((living, got))
-            fresh = jnp.stack([send_clone(wide[i], route[i]) for i in range(count)])
-            if extra:
-                fresh = jnp.pad(fresh, ((0, 0), (0, 0), (0, extra), (0, 0)))
+        got = grid(k, sent[k])
         back.append(collect(got))
-    part = inverse(back[:-1], 0, None, None)
-    out = inverse(back[-1:], chunk_count - 1, kept, part)
+    start = inverse(back[:1], [columns], state, fresh)
+    out = inverse(back[1:], kept, start, [])
     return out[:, :, :pairs] if extra else out
 
 

time: 382 us -> 377 us (0.987)
  Pallas kernels: 121 us -> 112 us
  waiting for transfers between devices: 147 us -> 138 us
  starting transfers between devices: 72.3 us -> 80.4 us
  other arithmetic: 25.7 us -> 32.3 us
    ppermute x4 -> x2, waiting for transfers between devices: 47.9 us -> 11.5 us  [move(): return lambda v: lax.ppermute(v, 'member', [(a, b)])]
    ppermute x42, waiting for transfers between devices: 98.7 us -> 127 us  [swap(): lax.ppermute(x, 'space', [(d, d ^ n) for d in range(space)])]
    ppermute x0 -> x4, starting transfers between devices: none -> 11.6 us  [share_row(): other = lax.ppermute(row, 'member', [(m, m ^ bit) for m in range(members)])]
    select_n x0 -> x4, other arithmetic: none -> 8.46 us  [share_row(): row = jnp.where(jnp.bitwise_and(differs, bit) != 0, other, row)]
    another operation x3 -> x1, other arithmetic: 21.5 us -> 15.8 us
    pallas_call x3, Pallas kernels: 42.4 us -> 37.2 us  [forward(): pl.pallas_call(functools.partial(forward_kernel, truncation=truncation, p...]
    pallas_call x2, Pallas kernels: 35.6 us -> 31.2 us  [inverse(): pl.pallas_call(functools.partial(inverse_kernel, truncation=truncation, p...]
    ppermute x4 -> x2, starting transfers between devices: 6.04 us -> 1.99 us  [move(): return lambda v: lax.ppermute(v, 'member', [(a, b)])]
  transfers between devices with their start and end apart: 46 -> 48, of which waited for: 14 -> 19; matrix products, arithmetic and copies ran while one was open for 7% -> 8% of each run, Pallas kernels for 24% -> 19%
where the time goes in v4:
time: 377 us; the launch traced here: 376 us
  waiting for transfers between devices  138 us (37%)
  Pallas kernels  112 us (30%)
  starting transfers between devices  80.4 us (21%)
  other arithmetic  32.3 us (9%)
  between operations  7 us (2%)
  local copies, waits for them, and re-layouts  6.52 us (2%)
    ppermute x42, waiting for transfers between devices, swap(): lax.ppermute(x, 'space', [(d, d ^ n) for d in range(space)])  127 us
    ppermute x42, starting transfers between devices, swap(): lax.ppermute(x, 'space', [(d, d ^ n) for d in range(space)])  66.8 us
    pallas_call x3, Pallas kernels, grid(): pl.pallas_call(functools.partial(grid_kernel, scale=1.0 / truncation), ou...  43.4 us
    pallas_call x3, Pallas kernels, forward(): pl.pallas_call(functools.partial(forward_kernel, truncation=truncation, p...  37.2 us
    pallas_call x2, Pallas kernels, inverse(): pl.pallas_call(functools.partial(inverse_kernel, truncation=truncation, p...  31.2 us
    another operation x1, other arithmetic  15.8 us
    ppermute x4, starting transfers between devices, share_row(): other = lax.ppermute(row, 'member', [(m, m ^ bit) for m in range(members)])  11.6 us
    ppermute x2, waiting for transfers between devices, move(): return lambda v: lax.ppermute(v, 'member', [(a, b)])  11.5 us
  transfers between devices with their start and end apart: 48, of which 19 were waited for; matrix products, arithmetic and copies ran while one was open for 8% of the time, Pallas kernels for 19%

profile of v4, /device:TPU:8, one launch (start us, length us, event | category | flops | bytes accessed | tf_op | source)
XLA Modules:
  0.0 376.4 jit_solution(15835586745244930199)
XLA Ops:
  7.1 3.8 %fusion.29 = (bf16[12,40,641]{2,1,0:T(8,128)(2,1)S(1)}, f32[12,40,641]{2,1,0:T(8,128)}, bf16[12,40,641]{2,1,0:T(8,128)(2,1)S(1)}, f32[12,40,641]{2,1,0:T(8,128)}) fusion(f32[4,12,40,641]{3,2,1,0:T(8,128)} %refs_9_.1, s32[]{:T(128)S(6)} %select_n.196, s32[]{:T(128)S(6)} %select_n.195), kind=kLoop, calls=%fused_computation.74 | loop fusion | flops 615360 | bytes 6153608 | tf_op jit(solution)/shard_map/convert_element_type | solution.py:371
  10.9 12.8 %conditional.2 = (bf16[12,40,641]{2,1,0:T(8,128)(2,1)S(1)}) conditional(s32[]{:T(128)} %bitcast.5, bf16[12,40,641]{2,1,0:T(8,128)(2,1)S(1)} %get-tuple-element.191, bf16[12,40,641]{2,1,0:T(8,128)(2,1)S(1)} %get-tuple-element.191, bf16[12,40,641]{2,1,0:T(8,128)(2,1)S(1)} %get-tuple-element.191, ...), branch_computations={%region_0.1_spmd, %region_1.2_spmd, %region_2.3_spmd, %region_3.4_... | conditional | bytes 3692208 | solution.py:335
  12.2 11.5 %collective-permute-done.9 = bf16[12,40,641]{2,1,0:T(8,128)(2,1)S(1)} collective-permute-done((bf16[12,40,641]{2,1,0:T(8,128)(2,1)S(1)}, bf16[12,40,641]{2,1,0:T(8,128)(2,1)S(1)}, u32[]{:S(2)}, u32[]{:S(2)}) %collective-permute-start.9) | collective-permute-done | bytes 615392 | tf_op jit(solution)/shard_map/cond/branch_12_fun/ppermute | solution.py:332
  25.4 11.3 %forward.3 = (bf16[6,160,128]{2,1,0:T(8,128)(2,1)}, bf16[6,160,128]{2,1,0:T(8,128)(2,1)}, bf16[6,160,128]{2,1,0:T(8,128)(2,1)}, bf16[6,160,128]{2,1,0:T(8,128)(2...) custom-call(s32[11]{0:T(128)} %pad_add_fusion.where_ref, ...), custom_call_target="tpu_custom_call" | custom-call | flops 1260257280 | bytes 16777216 | tf_op jit(solution)/shard_map/forward/pallas_call | solution.py:404
  36.7 13.0 %forward.4 = (bf16[6,160,128]{2,1,0:T(8,128)(2,1)}, bf16[6,160,128]{2,1,0:T(8,128)(2,1)}, bf16[6,160,128]{2,1,0:T(8,128)(2,1)}, bf16[6,160,128]{2,1,0:T(8,128)(2...) custom-call(s32[11]{0:T(128)} %pad_add_fusion.where_ref, ...), custom_call_target="tpu_custom_call" | custom-call | flops 1260257280 | bytes 16777216 | tf_op jit(solution)/shard_map/forward/pallas_call | solution.py:404
  58.8 15.8 %fusion.7 = (bf16[1280,640]{1,0:T(8,128)(2,1)}, bf16[1280,640]{1,0:T(8,128)(2,1)}) fusion(s32[1280]{0:T(1024)S(1)} %get-tuple-element.217, s32[1280]{0:T(1024)S(1)} %get-tuple-element.216, pred[1280]{0:T(1024)(128)(4,1)S(1)} %fusion.22), kind=kLoop, calls=%fused_computation.11 | loop fusion | flops 11468800 | bytes 3288320 | tf_op jit(solution)/shard_map/convert
  74.6 12.9 %forward.5 = (bf16[6,160,128]{2,1,0:T(8,128)(2,1)}, bf16[6,160,128]{2,1,0:T(8,128)(2,1)}, bf16[6,160,128]{2,1,0:T(8,128)(2,1)}, bf16[6,160,128]{2,1,0:T(8,128)(2...) custom-call(s32[11]{0:T(128)} %pad_add_fusion.where_ref, ...), custom_call_target="tpu_custom_call" | custom-call | flops 1260257280 | bytes 16777216 | tf_op jit(solution)/shard_map/forward/pallas_call | solution.py:404
  91.8 9.9 %collective-permute-start.66 = (f32[12,40,641]{2,1,0:T(8,128)}, f32[12,40,641]{2,1,0:T(8,128)}, u32[]{:S(2)}, u32[]{:S(2)}) collective-permute-start(f32[12,40,641]{2,1,0:T(8,128)} %get-tuple-element.183), channel_id=1, source_target_pairs={{0,8},{8,0},{16,24},{24,16},{1,9},{9,1},{17,25},{25,17},{2,10},{10... | collective-permute-start | bytes 3692168 | tf_op jit(solution)/shard_map/ppermute | solution.py:343
  110.3 3.4 copy.7.syn_ref
  115.6 13.7 %collective-permute-done.41.refs_4_ = bf16[6,160,128]{2,1,0:T(8,128)(2,1)} collective-permute-done((bf16[6,160,128]{2,1,0:T(8,128)(2,1)}, bf16[6,160,128]{2,1,0:T(8,128)(2,1)}, u32[]{:S(2)}, u32[]{:S(2)}) %collective-permute-start.41) | collective-permute-done | bytes 245792 | tf_op jit(solution)/shard_map/ppermute | solution.py:445
  129.3 10.4 %collective-permute-done.42.refs_5_ = bf16[6,160,128]{2,1,0:T(8,128)(2,1)} collective-permute-done((bf16[6,160,128]{2,1,0:T(8,128)(2,1)}, bf16[6,160,128]{2,1,0:T(8,128)(2,1)}, u32[]{:S(2)}, u32[]{:S(2)}) %collective-permute-start.42) | collective-permute-done | bytes 245792 | tf_op jit(solution)/shard_map/ppermute | solution.py:445
  139.7 5.6 %collective-permute-done.43.refs_6_ = bf16[6,160,128]{2,1,0:T(8,128)(2,1)} collective-permute-done((bf16[6,160,128]{2,1,0:T(8,128)(2,1)}, bf16[6,160,128]{2,1,0:T(8,128)(2,1)}, u32[]{:S(2)}, u32[]{:S(2)}) %collective-permute-start.43) | collective-permute-done | bytes 245792 | tf_op jit(solution)/shard_map/ppermute | solution.py:445
  145.3 14.6 %grid.3 = (bf16[6,160,128]{2,1,0:T(8,128)(2,1)}, bf16[6,160,128]{2,1,0:T(8,128)(2,1)}, bf16[6,160,128]{2,1,0:T(8,128)(2,1)}, bf16[6,160,128]{2,1,0:T(8,128)(2,1)...) custom-call(s32[8]{0:T(128)} %copy-done.18, ...), custom_call_target="tpu_custom_call" | custom-call | flops 5033164800 | bytes 12582912 | tf_op jit(solution)/shard_map/grid/pallas_call | solution.py:480
  174.5 16.8 %collective-permute-done.55.refs_4_ = bf16[6,160,128]{2,1,0:T(8,128)(2,1)S(1)} collective-permute-done((bf16[6,160,128]{2,1,0:T(8,128)(2,1)S(1)}, bf16[6,160,128]{2,1,0:T(8,128)(2,1)S(1)}, u32[]{:S(2)}, u32[]{:S(2)}) %collective-permute-start.55) | collective-permute-done | bytes 245792 | tf_op jit(solution)/shard_map/ppermute | solution.py:445
  192.8 3.8 %collective-permute-done.56.refs_5_ = bf16[6,160,128]{2,1,0:T(8,128)(2,1)S(1)} collective-permute-done((bf16[6,160,128]{2,1,0:T(8,128)(2,1)S(1)}, bf16[6,160,128]{2,1,0:T(8,128)(2,1)S(1)}, u32[]{:S(2)}, u32[]{:S(2)}) %collective-permute-start.56) | collective-permute-done | bytes 245792 | tf_op jit(solution)/shard_map/ppermute | solution.py:445
  196.6 3.3 collective-permute-start.32
  204.5 6.1 %collective-permute-done.58.refs_7_ = bf16[6,160,128]{2,1,0:T(8,128)(2,1)S(1)} collective-permute-done((bf16[6,160,128]{2,1,0:T(8,128)(2,1)S(1)}, bf16[6,160,128]{2,1,0:T(8,128)(2,1)S(1)}, u32[]{:S(2)}, u32[]{:S(2)}) %collective-permute-start.58) | collective-permute-done | bytes 245792 | tf_op jit(solution)/shard_map/ppermute | solution.py:445
  210.7 3.9 %collective-permute-start.35 = (bf16[6,160,128]{2,1,0:T(8,128)(2,1)}, bf16[6,160,128]{2,1,0:T(8,128)(2,1)S(1)}, u32[]{:S(2)}, u32[]{:S(2)}) collective-permute-start(bf16[6,160,128]{2,1,0:T(8,128)(2,1)} %get-tuple-element.144), channel_id=1, source_target_pairs={{0,5},{1,4},{2,7},{3,6},{4,1},{5,0},{6,3},{7,2},{8,13},{9,12},{10,... | collective-permute-start | bytes 737288 | tf_op jit(solution)/shard_map/ppermute | solution.py:445
  215.2 14.4 %grid.4 = (bf16[6,160,128]{2,1,0:T(8,128)(2,1)}, bf16[6,160,128]{2,1,0:T(8,128)(2,1)}, bf16[6,160,128]{2,1,0:T(8,128)(2,1)}, bf16[6,160,128]{2,1,0:T(8,128)(2,1)...) custom-call(s32[8]{0:T(128)} %copy-done.18, ...), custom_call_target="tpu_custom_call" | custom-call | flops 5033164800 | bytes 12582912 | tf_op jit(solution)/shard_map/grid/pallas_call | solution.py:480
  234.6 8.3 %collective-permute-done.35.refs_5_ = bf16[6,160,128]{2,1,0:T(8,128)(2,1)S(1)} collective-permute-done((bf16[6,160,128]{2,1,0:T(8,128)(2,1)}, bf16[6,160,128]{2,1,0:T(8,128)(2,1)S(1)}, u32[]{:S(2)}, u32[]{:S(2)}) %collective-permute-start.35) | collective-permute-done | bytes 245792 | tf_op jit(solution)/shard_map/ppermute | solution.py:445
  244.0 5.9 %collective-permute-done.36.refs_6_ = bf16[6,160,128]{2,1,0:T(8,128)(2,1)} collective-permute-done((bf16[6,160,128]{2,1,0:T(8,128)(2,1)}, bf16[6,160,128]{2,1,0:T(8,128)(2,1)}, u32[]{:S(2)}, u32[]{:S(2)}) %collective-permute-start.36) | collective-permute-done | bytes 245792 | tf_op jit(solution)/shard_map/ppermute | solution.py:445
  249.9 14.4 %grid.5 = (bf16[6,160,128]{2,1,0:T(8,128)(2,1)}, bf16[6,160,128]{2,1,0:T(8,128)(2,1)}, bf16[6,160,128]{2,1,0:T(8,128)(2,1)}, bf16[6,160,128]{2,1,0:T(8,128)(2,1)...) custom-call(s32[8]{0:T(128)} %copy-done.18, ...), custom_call_target="tpu_custom_call" | custom-call | flops 5033164800 | bytes 12582912 | tf_op jit(solution)/shard_map/grid/pallas_call | solution.py:480
  267.9 4.2 %collective-permute-done.59.refs_1_ = bf16[6,160,128]{2,1,0:T(8,128)(2,1)} collective-permute-done((bf16[6,160,128]{2,1,0:T(8,128)(2,1)}, bf16[6,160,128]{2,1,0:T(8,128)(2,1)}, u32[]{:S(2)}, u32[]{:S(2)}) %collective-permute-start.59) | collective-permute-done | bytes 245792 | tf_op jit(solution)/shard_map/ppermute | solution.py:445
  272.1 3.6 collective-permute-start.62
  285.0 17.2 %collective-permute-done.62.refs_4_ = bf16[6,160,128]{2,1,0:T(8,128)(2,1)S(1)} collective-permute-done((bf16[6,160,128]{2,1,0:T(8,128)(2,1)}, bf16[6,160,128]{2,1,0:T(8,128)(2,1)S(1)}, u32[]{:S(2)}, u32[]{:S(2)}) %collective-permute-start.62) | collective-permute-done | bytes 245792 | tf_op jit(solution)/shard_map/ppermute | solution.py:445
  303.2 4.3 %collective-permute-done.63.refs_5_ = bf16[6,160,128]{2,1,0:T(8,128)(2,1)S(1)} collective-permute-done((bf16[6,160,128]{2,1,0:T(8,128)(2,1)}, bf16[6,160,128]{2,1,0:T(8,128)(2,1)S(1)}, u32[]{:S(2)}, u32[]{:S(2)}) %collective-permute-start.63) | collective-permute-done | bytes 245792 | tf_op jit(solution)/shard_map/ppermute | solution.py:445
  308.1 3.8 %collective-permute-start.48 = (bf16[6,160,128]{2,1,0:T(8,128)(2,1)}, bf16[6,160,128]{2,1,0:T(8,128)(2,1)S(1)}, u32[]{:S(2)}, u32[]{:S(2)}) collective-permute-start(bf16[6,160,128]{2,1,0:T(8,128)(2,1)} %get-tuple-element.161), channel_id=1, source_target_pairs={{0,4},{1,5},{2,6},{3,7},{4,0},{5,1},{6,2},{7,3},{8,12},{9,13},{10,... | collective-permute-start | bytes 737288 | tf_op jit(solution)/shard_map/ppermute | solution.py:445
  312.0 13.3 %collective-permute-done.64.refs_6_ = bf16[6,160,128]{2,1,0:T(8,128)(2,1)S(1)} collective-permute-done((bf16[6,160,128]{2,1,0:T(8,128)(2,1)}, bf16[6,160,128]{2,1,0:T(8,128)(2,1)S(1)}, u32[]{:S(2)}, u32[]{:S(2)}) %collective-permute-start.64) | collective-permute-done | bytes 245792 | tf_op jit(solution)/shard_map/ppermute | solution.py:445
  325.2 5.4 %collective-permute-done.65.refs_7_ = bf16[6,160,128]{2,1,0:T(8,128)(2,1)S(1)} collective-permute-done((bf16[6,160,128]{2,1,0:T(8,128)(2,1)}, bf16[6,160,128]{2,1,0:T(8,128)(2,1)S(1)}, u32[]{:S(2)}, u32[]{:S(2)}) %collective-permute-start.65) | collective-permute-done | bytes 245792 | tf_op jit(solution)/shard_map/ppermute | solution.py:445
  330.7 9.3 %collective-permute-start.50 = (bf16[6,160,128]{2,1,0:T(8,128)(2,1)}, bf16[6,160,128]{2,1,0:T(8,128)(2,1)S(1)}, u32[]{:S(2)}, u32[]{:S(2)}) collective-permute-start(bf16[6,160,128]{2,1,0:T(8,128)(2,1)} %get-tuple-element.163), channel_id=1, source_target_pairs={{0,6},{1,7},{2,4},{3,5},{4,2},{5,3},{6,0},{7,1},{8,14},{9,15},{10,... | collective-permute-start | bytes 737288 | tf_op jit(solution)/shard_map/ppermute | solution.py:445
  344.0 14.5 %inverse.2.refs_18_ = f32[4,12,40,641]{3,2,1,0:T(8,128)} custom-call(s32[11]{0:T(128)} %pad_add_fusion.where_ref, f32[2,2]{1,0:T(2,128)} %gravity_ref.3, f32[2,2]{1,0:T(2,128)} %stability_ref.3, bf16[6,160,128]{2,1,0:T(8,128)(2,1)} %get-tuple-element.175.refs_0_, bf16[6,160,128]{2,1,0:T(8,128)(2,1)} %collective-permute-done.59.refs_1_, ...), custom_call_target="tpu_custom_call" | custom-call | flops 1260257280 | bytes 20971520 | tf_op jit(solution)/shard_map/inverse/pallas_call | solution.py:502
  359.5 16.7 %inverse.3 = f32[4,12,40,641]{3,2,1,0:T(8,128)} custom-call(s32[11]{0:T(128)} %pad_add_fusion.where_ref, f32[2,2]{1,0:T(2,128)} %gravity_ref.3, f32[2,2]{1,0:T(2,128)} %stability_ref.3, bf16[6,160,128]{2,1,0:T(8,128)(2,1)} %get-tuple-element.139.refs_0_, bf16[6,160,128]{2,1,0:T(8,128)(2,1)} %copy-done.2, bf16[6,160,128]{2,1,0:T(8,128)(2,1)} %copy-done.3, ...), custom_call_target="tpu_custom_call" | custom-call | flops 2520514560 | bytes 20971520 | tf_op jit(solution)/shard_map/inverse/pallas_call | solution.py:502
  (176 shorter events, 75.3 us)
Async XLA Ops:
  51.2 36.3 %collective-permute-start.25 = (bf16[6,160,128]{2,1,0:T(8,128)(2,1)}, bf16[6,160,128]{2,1,0:T(8,128)(2,1)S(1)}, u32[]{:S(2)}, u32[]{:S(2)}) collective-permute-start(bf16[6,160,128]{2,1,0:T(8,128)(2,1)} %get-tuple-element.133), channel_id=1, source_target_pairs={{0,2},{1,3},{2,0},{3,1},{4,6},{5,7},{6,4},{7,5},{8,10},{9,11},{10,... | collective-permute-start | bytes 737288 | tf_op jit(solution)/shard_map/ppermute | solution.py:445
  51.7 36.3 %collective-permute-start.26 = (bf16[6,160,128]{2,1,0:T(8,128)(2,1)}, bf16[6,160,128]{2,1,0:T(8,128)(2,1)S(1)}, u32[]{:S(2)}, u32[]{:S(2)}) collective-permute-start(bf16[6,160,128]{2,1,0:T(8,128)(2,1)} %get-tuple-element.134), channel_id=1, source_target_pairs={{0,3},{1,2},{2,1},{3,0},{4,7},{5,6},{6,5},{7,4},{8,11},{9,10},{10,... | collective-permute-start | bytes 737288 | tf_op jit(solution)/shard_map/ppermute | solution.py:445
  53.2 36.3 %collective-permute-start.27 = (bf16[6,160,128]{2,1,0:T(8,128)(2,1)}, bf16[6,160,128]{2,1,0:T(8,128)(2,1)S(1)}, u32[]{:S(2)}, u32[]{:S(2)}) collective-permute-start(bf16[6,160,128]{2,1,0:T(8,128)(2,1)} %get-tuple-element.135), channel_id=1, source_target_pairs={{0,4},{1,5},{2,6},{3,7},{4,0},{5,1},{6,2},{7,3},{8,12},{9,13},{10,... | collective-permute-start | bytes 737288 | tf_op jit(solution)/shard_map/ppermute | solution.py:445
  55.8 36.0 %collective-permute-start.28 = (bf16[6,160,128]{2,1,0:T(8,128)(2,1)}, bf16[6,160,128]{2,1,0:T(8,128)(2,1)S(1)}, u32[]{:S(2)}, u32[]{:S(2)}) collective-permute-start(bf16[6,160,128]{2,1,0:T(8,128)(2,1)} %get-tuple-element.136), channel_id=1, source_target_pairs={{0,5},{1,4},{2,7},{3,6},{4,1},{5,0},{6,3},{7,2},{8,13},{9,12},{10,... | collective-permute-start | bytes 737288 | tf_op jit(solution)/shard_map/ppermute | solution.py:445
  57.2 34.7 %collective-permute-start.29 = (bf16[6,160,128]{2,1,0:T(8,128)(2,1)}, bf16[6,160,128]{2,1,0:T(8,128)(2,1)S(1)}, u32[]{:S(2)}, u32[]{:S(2)}) collective-permute-start(bf16[6,160,128]{2,1,0:T(8,128)(2,1)} %get-tuple-element.137), channel_id=1, source_target_pairs={{0,6},{1,7},{2,4},{3,5},{4,2},{5,3},{6,0},{7,1},{8,14},{9,15},{10,... | collective-permute-start | bytes 737288 | tf_op jit(solution)/shard_map/ppermute | solution.py:445
  91.8 74.3 %collective-permute-start.66 = (f32[12,40,641]{2,1,0:T(8,128)}, f32[12,40,641]{2,1,0:T(8,128)}, u32[]{:S(2)}, u32[]{:S(2)}) collective-permute-start(f32[12,40,641]{2,1,0:T(8,128)} %get-tuple-element.183), channel_id=1, source_target_pairs={{0,8},{8,0},{16,24},{24,16},{1,9},{9,1},{17,25},{25,17},{2,10},{10... | collective-permute-start | bytes 3692168 | tf_op jit(solution)/shard_map/ppermute | solution.py:343
  103.9 25.4 %collective-permute-start.41 = (bf16[6,160,128]{2,1,0:T(8,128)(2,1)}, bf16[6,160,128]{2,1,0:T(8,128)(2,1)}, u32[]{:S(2)}, u32[]{:S(2)}) collective-permute-start(bf16[6,160,128]{2,1,0:T(8,128)(2,1)} %get-tuple-element.153), channel_id=1, source_target_pairs={{0,4},{1,5},{2,6},{3,7},{4,0},{5,1},{6,2},{7,3},{8,12},{9,13},{10,... | collective-permute-start | bytes 737288 | tf_op jit(solution)/shard_map/ppermute | solution.py:445
  106.9 32.7 %collective-permute-start.42 = (bf16[6,160,128]{2,1,0:T(8,128)(2,1)}, bf16[6,160,128]{2,1,0:T(8,128)(2,1)}, u32[]{:S(2)}, u32[]{:S(2)}) collective-permute-start(bf16[6,160,128]{2,1,0:T(8,128)(2,1)} %get-tuple-element.154), channel_id=1, source_target_pairs={{0,5},{1,4},{2,7},{3,6},{4,1},{5,0},{6,3},{7,2},{8,13},{9,12},{10,... | collective-permute-start | bytes 737288 | tf_op jit(solution)/shard_map/ppermute | solution.py:445
  107.0 38.4 %collective-permute-start.43 = (bf16[6,160,128]{2,1,0:T(8,128)(2,1)}, bf16[6,160,128]{2,1,0:T(8,128)(2,1)}, u32[]{:S(2)}, u32[]{:S(2)}) collective-permute-start(bf16[6,160,128]{2,1,0:T(8,128)(2,1)} %get-tuple-element.155), channel_id=1, source_target_pairs={{0,6},{1,7},{2,4},{3,5},{4,2},{5,3},{6,0},{7,1},{8,14},{9,15},{10,... | collective-permute-start | bytes 737288 | tf_op jit(solution)/shard_map/ppermute | solution.py:445
  108.8 94.0 %collective-permute-start.68 = (f32[12,40,641]{2,1,0:T(8,128)}, f32[12,40,641]{2,1,0:T(8,128)}, u32[]{:S(2)}, u32[]{:S(2)}) collective-permute-start(f32[12,40,641]{2,1,0:T(8,128)} %get-tuple-element.184), channel_id=1, source_target_pairs={{0,8},{8,0},{16,24},{24,16},{1,9},{9,1},{17,25},{25,17},{2,10},{10... | collective-permute-start | bytes 3692168 | tf_op jit(solution)/shard_map/ppermute | solution.py:343
  129.3 30.7 %collective-permute-start.44 = (bf16[6,160,128]{2,1,0:T(8,128)(2,1)}, bf16[6,160,128]{2,1,0:T(8,128)(2,1)S(1)}, u32[]{:S(2)}, u32[]{:S(2)}) collective-permute-start(bf16[6,160,128]{2,1,0:T(8,128)(2,1)} %get-tuple-element.156), channel_id=1, source_target_pairs={{0,7},{1,6},{2,5},{3,4},{4,3},{5,2},{6,1},{7,0},{8,15},{9,14},{10,... | collective-permute-start | bytes 737288 | tf_op jit(solution)/shard_map/ppermute | solution.py:445
  139.7 22.1 %collective-permute-start.52 = (bf16[6,160,128]{2,1,0:T(8,128)(2,1)}, bf16[6,160,128]{2,1,0:T(8,128)(2,1)S(1)}, u32[]{:S(2)}, u32[]{:S(2)}) collective-permute-start(bf16[6,160,128]{2,1,0:T(8,128)(2,1)} %get-tuple-element.168), channel_id=1, source_target_pairs={{0,1},{1,0},{2,3},{3,2},{4,5},{5,4},{6,7},{7,6},{8,9},{9,8},{10,11... | collective-permute-start | bytes 737288 | tf_op jit(solution)/shard_map/ppermute | solution.py:445
  161.8 29.5 %collective-permute-start.55 = (bf16[6,160,128]{2,1,0:T(8,128)(2,1)S(1)}, bf16[6,160,128]{2,1,0:T(8,128)(2,1)S(1)}, u32[]{:S(2)}, u32[]{:S(2)}) collective-permute-start(bf16[6,160,128]{2,1,0:T(8,128)(2,1)S(1)} %copy-done.22), channel_id=1, source_target_pairs={{0,4},{1,5},{2,6},{3,7},{4,0},{5,1},{6,2},{7,3},{8,12},{9,13},{10,... | collective-permute-start | bytes 737288 | tf_op jit(solution)/shard_map/ppermute | solution.py:445
  163.9 32.7 %collective-permute-start.56 = (bf16[6,160,128]{2,1,0:T(8,128)(2,1)S(1)}, bf16[6,160,128]{2,1,0:T(8,128)(2,1)S(1)}, u32[]{:S(2)}, u32[]{:S(2)}) collective-permute-start(bf16[6,160,128]{2,1,0:T(8,128)(2,1)S(1)} %copy-done.21), channel_id=1, source_target_pairs={{0,5},{1,4},{2,7},{3,6},{4,1},{5,0},{6,3},{7,2},{8,13},{9,12},{10,... | collective-permute-start | bytes 737288 | tf_op jit(solution)/shard_map/ppermute | solution.py:445
  166.1 36.7 %collective-permute-start.57 = (bf16[6,160,128]{2,1,0:T(8,128)(2,1)S(1)}, bf16[6,160,128]{2,1,0:T(8,128)(2,1)S(1)}, u32[]{:S(2)}, u32[]{:S(2)}) collective-permute-start(bf16[6,160,128]{2,1,0:T(8,128)(2,1)S(1)} %copy-done.20), channel_id=1, source_target_pairs={{0,6},{1,7},{2,4},{3,5},{4,2},{5,3},{6,0},{7,1},{8,14},{9,15},{10,... | collective-permute-start | bytes 737288 | tf_op jit(solution)/shard_map/ppermute | solution.py:445
  172.1 38.5 %collective-permute-start.58 = (bf16[6,160,128]{2,1,0:T(8,128)(2,1)S(1)}, bf16[6,160,128]{2,1,0:T(8,128)(2,1)S(1)}, u32[]{:S(2)}, u32[]{:S(2)}) collective-permute-start(bf16[6,160,128]{2,1,0:T(8,128)(2,1)S(1)} %copy-done.19), channel_id=1, source_target_pairs={{0,7},{1,6},{2,5},{3,4},{4,3},{5,2},{6,1},{7,0},{8,15},{9,14},{10,... | collective-permute-start | bytes 737288 | tf_op jit(solution)/shard_map/ppermute | solution.py:445
  191.4 19.3 %collective-permute-start.31 = (bf16[6,160,128]{2,1,0:T(8,128)(2,1)S(1)}, bf16[6,160,128]{2,1,0:T(8,128)(2,1)S(1)}, u32[]{:S(2)}, u32[]{:S(2)}) collective-permute-start(bf16[6,160,128]{2,1,0:T(8,128)(2,1)S(1)} %copy-done.40), channel_id=1, source_target_pairs={{0,1},{1,0},{2,3},{3,2},{4,5},{5,4},{6,7},{7,6},{8,9},{9,8},{10,11... | collective-permute-start | bytes 737288 | tf_op jit(solution)/shard_map/ppermute | solution.py:445
  202.9 78.2 %collective-permute-start.67 = (f32[12,40,641]{2,1,0:T(8,128)S(1)}, f32[12,40,641]{2,1,0:T(8,128)}, u32[]{:S(2)}, u32[]{:S(2)}) collective-permute-start(f32[12,40,641]{2,1,0:T(8,128)S(1)} %broadcast_select_fusion.2), channel_id=1, source_target_pairs={{0,16},{8,24},{16,0},{24,8},{1,17},{9,25},{17,1},{25,9},{2,18},{10... | collective-permute-start | bytes 3692168 | tf_op jit(solution)/shard_map/ppermute | solution.py:343
  210.6 21.7 %collective-permute-start.34 = (bf16[6,160,128]{2,1,0:T(8,128)(2,1)}, bf16[6,160,128]{2,1,0:T(8,128)(2,1)S(1)}, u32[]{:S(2)}, u32[]{:S(2)}) collective-permute-start(bf16[6,160,128]{2,1,0:T(8,128)(2,1)} %get-tuple-element.143), channel_id=1, source_target_pairs={{0,4},{1,5},{2,6},{3,7},{4,0},{5,1},{6,2},{7,3},{8,12},{9,13},{10,... | collective-permute-start | bytes 737288 | tf_op jit(solution)/shard_map/ppermute | solution.py:445
  210.7 32.2 %collective-permute-start.35 = (bf16[6,160,128]{2,1,0:T(8,128)(2,1)}, bf16[6,160,128]{2,1,0:T(8,128)(2,1)S(1)}, u32[]{:S(2)}, u32[]{:S(2)}) collective-permute-start(bf16[6,160,128]{2,1,0:T(8,128)(2,1)} %get-tuple-element.144), channel_id=1, source_target_pairs={{0,5},{1,4},{2,7},{3,6},{4,1},{5,0},{6,3},{7,2},{8,13},{9,12},{10,... | collective-permute-start | bytes 737288 | tf_op jit(solution)/shard_map/ppermute | solution.py:445
  214.5 35.3 %collective-permute-start.36 = (bf16[6,160,128]{2,1,0:T(8,128)(2,1)}, bf16[6,160,128]{2,1,0:T(8,128)(2,1)}, u32[]{:S(2)}, u32[]{:S(2)}) collective-permute-start(bf16[6,160,128]{2,1,0:T(8,128)(2,1)} %get-tuple-element.145), channel_id=1, source_target_pairs={{0,6},{1,7},{2,4},{3,5},{4,2},{5,3},{6,0},{7,1},{8,14},{9,15},{10,... | collective-permute-start | bytes 737288 | tf_op jit(solution)/shard_map/ppermute | solution.py:445
  215.1 124.8 %collective-permute-start.69 = (f32[12,40,641]{2,1,0:T(8,128)S(1)}, f32[12,40,641]{2,1,0:T(8,128)}, u32[]{:S(2)}, u32[]{:S(2)}) collective-permute-start(f32[12,40,641]{2,1,0:T(8,128)S(1)} %broadcast_select_fusion), channel_id=1, source_target_pairs={{0,16},{8,24},{16,0},{24,8},{1,17},{9,25},{17,1},{25,9},{2,18},{10... | collective-permute-start | bytes 3692168 | tf_op jit(solution)/shard_map/ppermute | solution.py:343
  232.3 31.9 %collective-permute-start.37 = (bf16[6,160,128]{2,1,0:T(8,128)(2,1)}, bf16[6,160,128]{2,1,0:T(8,128)(2,1)S(1)}, u32[]{:S(2)}, u32[]{:S(2)}) collective-permute-start(bf16[6,160,128]{2,1,0:T(8,128)(2,1)} %get-tuple-element.146), channel_id=1, source_target_pairs={{0,7},{1,6},{2,5},{3,4},{4,3},{5,2},{6,1},{7,0},{8,15},{9,14},{10,... | collective-permute-start | bytes 737288 | tf_op jit(solution)/shard_map/ppermute | solution.py:445
  242.9 22.6 %collective-permute-start.45 = (bf16[6,160,128]{2,1,0:T(8,128)(2,1)}, bf16[6,160,128]{2,1,0:T(8,128)(2,1)S(1)}, u32[]{:S(2)}, u32[]{:S(2)}) collective-permute-start(bf16[6,160,128]{2,1,0:T(8,128)(2,1)} %get-tuple-element.158), channel_id=1, source_target_pairs={{0,1},{1,0},{2,3},{3,2},{4,5},{5,4},{6,7},{7,6},{8,9},{9,8},{10,11... | collective-permute-start | bytes 737288 | tf_op jit(solution)/shard_map/ppermute | solution.py:445
  272.1 30.1 %collective-permute-start.62 = (bf16[6,160,128]{2,1,0:T(8,128)(2,1)}, bf16[6,160,128]{2,1,0:T(8,128)(2,1)S(1)}, u32[]{:S(2)}, u32[]{:S(2)}) collective-permute-start(bf16[6,160,128]{2,1,0:T(8,128)(2,1)} %get-tuple-element.179), channel_id=1, source_target_pairs={{0,4},{1,5},{2,6},{3,7},{4,0},{5,1},{6,2},{7,3},{8,12},{9,13},{10,... | collective-permute-start | bytes 737288 | tf_op jit(solution)/shard_map/ppermute | solution.py:445
  277.0 30.5 %collective-permute-start.63 = (bf16[6,160,128]{2,1,0:T(8,128)(2,1)}, bf16[6,160,128]{2,1,0:T(8,128)(2,1)S(1)}, u32[]{:S(2)}, u32[]{:S(2)}) collective-permute-start(bf16[6,160,128]{2,1,0:T(8,128)(2,1)} %get-tuple-element.180), channel_id=1, source_target_pairs={{0,5},{1,4},{2,7},{3,6},{4,1},{5,0},{6,3},{7,2},{8,13},{9,12},{10,... | collective-permute-start | bytes 737288 | tf_op jit(solution)/shard_map/ppermute | solution.py:445
  280.2 45.1 %collective-permute-start.64 = (bf16[6,160,128]{2,1,0:T(8,128)(2,1)}, bf16[6,160,128]{2,1,0:T(8,128)(2,1)S(1)}, u32[]{:S(2)}, u32[]{:S(2)}) collective-permute-start(bf16[6,160,128]{2,1,0:T(8,128)(2,1)} %get-tuple-element.181), channel_id=1, source_target_pairs={{0,6},{1,7},{2,4},{3,5},{4,2},{5,3},{6,0},{7,1},{8,14},{9,15},{10,... | collective-permute-start | bytes 737288 | tf_op jit(solution)/shard_map/ppermute | solution.py:445
  281.0 49.6 %collective-permute-start.65 = (bf16[6,160,128]{2,1,0:T(8,128)(2,1)}, bf16[6,160,128]{2,1,0:T(8,128)(2,1)S(1)}, u32[]{:S(2)}, u32[]{:S(2)}) collective-permute-start(bf16[6,160,128]{2,1,0:T(8,128)(2,1)} %get-tuple-element.182), channel_id=1, source_target_pairs={{0,7},{1,6},{2,5},{3,4},{4,3},{5,2},{6,1},{7,0},{8,15},{9,14},{10,... | collective-permute-start | bytes 737288 | tf_op jit(solution)/shard_map/ppermute | solution.py:445
  302.2 56.3 %collective-permute-start.47 = (bf16[6,160,128]{2,1,0:T(8,128)(2,1)}, bf16[6,160,128]{2,1,0:T(8,128)(2,1)S(1)}, u32[]{:S(2)}, u32[]{:S(2)}) collective-permute-start(bf16[6,160,128]{2,1,0:T(8,128)(2,1)} %get-tuple-element.160), channel_id=1, source_target_pairs={{0,3},{1,2},{2,1},{3,0},{4,7},{5,6},{6,5},{7,4},{8,11},{9,10},{10,... | collective-permute-start | bytes 737288 | tf_op jit(solution)/shard_map/ppermute | solution.py:445
  308.1 50.4 %collective-permute-start.48 = (bf16[6,160,128]{2,1,0:T(8,128)(2,1)}, bf16[6,160,128]{2,1,0:T(8,128)(2,1)S(1)}, u32[]{:S(2)}, u32[]{:S(2)}) collective-permute-start(bf16[6,160,128]{2,1,0:T(8,128)(2,1)} %get-tuple-element.161), channel_id=1, source_target_pairs={{0,4},{1,5},{2,6},{3,7},{4,0},{5,1},{6,2},{7,3},{8,12},{9,13},{10,... | collective-permute-start | bytes 737288 | tf_op jit(solution)/shard_map/ppermute | solution.py:445
  325.2 33.3 %collective-permute-start.49 = (bf16[6,160,128]{2,1,0:T(8,128)(2,1)}, bf16[6,160,128]{2,1,0:T(8,128)(2,1)S(1)}, u32[]{:S(2)}, u32[]{:S(2)}) collective-permute-start(bf16[6,160,128]{2,1,0:T(8,128)(2,1)} %get-tuple-element.162), channel_id=1, source_target_pairs={{0,5},{1,4},{2,7},{3,6},{4,1},{5,0},{6,3},{7,2},{8,13},{9,12},{10,... | collective-permute-start | bytes 737288 | tf_op jit(solution)/shard_map/ppermute | solution.py:445
  330.7 27.9 %collective-permute-start.50 = (bf16[6,160,128]{2,1,0:T(8,128)(2,1)}, bf16[6,160,128]{2,1,0:T(8,128)(2,1)S(1)}, u32[]{:S(2)}, u32[]{:S(2)}) collective-permute-start(bf16[6,160,128]{2,1,0:T(8,128)(2,1)} %get-tuple-element.163), channel_id=1, source_target_pairs={{0,6},{1,7},{2,4},{3,5},{4,2},{5,3},{6,0},{7,1},{8,14},{9,15},{10,... | collective-permute-start | bytes 737288 | tf_op jit(solution)/shard_map/ppermute | solution.py:445
  (57 other events, 1099.3 us)

commit v5 on v4

--- a/solution.py
+++ b/solution.py
@@ -167,33 +167,34 @@
             out_refs[n][f] = modes[pl.ds(at, rows), f * lanes : (f + 1) * lanes]
 
 
-def semi_implicit_slabs(old, tend, degree, gm, hm, truncation):
+def step_terms(degree, gm, hm, truncation):
     eig = wave_scale * (degree * (degree + 1)).astype(jnp.float32) / float(truncation * truncation)
     damping = 1.0 / (1.0 + diffusion * eig * eig)
     coupling = time_step * time_step * eig
     pm = [[gm[a][0] * hm[0][b] + gm[a][1] * hm[1][b] for b in range(2)] for a in range(2)]
-    diag_one = 1.0 + coupling * pm[0][0]
-    diag_two = 1.0 + coupling * pm[1][1]
-    cross_one = coupling * pm[0][1]
-    cross_two = coupling * pm[1][0]
-    inverse = 1.0 / (diag_one * diag_two - cross_one * cross_two)
+    diag = [1.0 + coupling * pm[a][a] for a in range(2)]
+    cross = [coupling * pm[0][1], coupling * pm[1][0]]
+    inverse = 1.0 / (diag[0] * diag[1] - cross[0] * cross[1])
+    solve = [
+        [diag[1] * inverse, -cross[0] * inverse],
+        [-cross[1] * inverse, diag[0] * inverse],
+    ]
+    push = [[time_step * eig * gm[a][b] for b in range(2)] for a in range(2)]
+    return damping, solve, push
+
+
+def semi_implicit_slabs(old, tend, terms, hm):
+    damping, solve, push = terms
     out = [None] * 12
     for r in range(2):
         star = [old[c * 2 + r] + time_step * tend[c * 2 + r] for c in range(6)]
-        right = [
-            star[2 + a] + time_step * eig * (gm[a][0] * star[4] + gm[a][1] * star[5])
-            for a in range(2)
-        ]
-        div = [
-            (diag_two * right[0] - cross_one * right[1]) * inverse,
-            (diag_one * right[1] - cross_two * right[0]) * inverse,
-        ]
+        right = [star[2 + a] + push[a][0] * star[4] + push[a][1] * star[5] for a in range(2)]
+        div = [solve[a][0] * right[0] + solve[a][1] * right[1] for a in range(2)]
         for a in range(2):
+            heat = (time_step * hm[a][0]) * div[0] + (time_step * hm[a][1]) * div[1]
             out[a * 2 + r] = damping * star[a]
             out[(2 + a) * 2 + r] = damping * div[a]
-            out[(4 + a) * 2 + r] = damping * (
-                star[4 + a] - time_step * (hm[a][0] * div[0] + hm[a][1] * div[1])
-            )
+            out[(4 + a) * 2 + r] = damping * (star[4 + a] - heat)
     return out
 
 
@@ -273,6 +274,7 @@
         lanes = slice(k * LANES, k * LANES + width)
         if last:
             _, _, degree = layout_terms(first_pair, block, k * LANES, width, truncation)
+            terms = step_terms(degree, gm, hm, truncation)
 
         def body(t, carry):
             tend = []
@@ -282,7 +284,7 @@
                 tend.append(value)
             old = [spec_ref[t, c, :, lanes] for c in range(comps)]
             if last:
-                tend = semi_implicit_slabs(old, tend, degree, gm, hm, truncation)
+                tend = semi_implicit_slabs(old, tend, terms, hm)
             else:
                 for i in range(count):
                     mine = where_ref[1 + i] == t
@@ -313,14 +315,42 @@
     return jnp.concatenate([first, second], axis=1).astype(jnp.bfloat16)
 
 
-def clone_routes(clones, local):
-    members = lax.axis_size("member")
+def pick_kernel(clones_ref, me_ref, spec_ref, row_ref, route_ref, slot_ref, *, members):
+    i = pl.program_id(0)
+    local = me_ref[1]
+    row_ref[...] = spec_ref[...].astype(jnp.bfloat16)
+    source = lax.div(clones_ref[i, 1], local)
+    target = lax.div(clones_ref[i, 0], local)
+    route_ref[i] = source * members + target
+    slot_ref[i] = jnp.where(target == me_ref[0], clones_ref[i, 0] - target * local, -1)
+
+
+def pick_clones(spectra, clones):
+    local, comps, pairs, row_length = spectra.shape
+    count = clones.shape[0]
     me = lax.axis_index("member").astype(jnp.int32)
-    owner = lax.div(clones, jnp.full_like(clones, local))
-    index = clones - owner * local
-    route = owner[:, 1] * members + owner[:, 0]
-    slot = jnp.where(owner[:, 0] == me, index[:, 0], -1)
-    return index[:, 1], owner[:, 1], route, slot
+    smem = pl.BlockSpec(memory_space=pltpu.SMEM)
+    block = (1, comps, pairs, row_length)
+    return pl.pallas_call(
+        functools.partial(pick_kernel, members=lax.axis_size("member")),
+        out_shape=[
+            jax.ShapeDtypeStruct((count,) + block[1:], jnp.bfloat16),
+            jax.ShapeDtypeStruct((count,), jnp.int32),
+            jax.ShapeDtypeStruct((count,), jnp.int32),
+        ],
+        grid_spec=pltpu.PrefetchScalarGridSpec(
+            num_scalar_prefetch=2,
+            grid=(count,),
+            in_specs=[
+                pl.BlockSpec(block, lambda i, c, m: (lax.rem(c[i, 1], m[1]), 0, 0, 0)),
+            ],
+            out_specs=[pl.BlockSpec(block, lambda i, c, m: (i, 0, 0, 0)), smem, smem],
+        ),
+        cost_estimate=pl.CostEstimate(
+            flops=0, bytes_accessed=6 * 1024 * 1024, transcendentals=0
+        ),
+        name="pick",
+    )(clones, jnp.stack([me, jnp.int32(local)]), spectra)
 
 
 def send_clone(row, route):
@@ -363,12 +393,9 @@
     extra = padded_pairs - pairs
     rows = trajectories * comps
 
-    survivor, owner, route, slot = clone_routes(clones, trajectories)
     count = clones.shape[0]
-    living = [
-        lax.dynamic_index_in_dim(spectra, survivor[i], 0, keepdims=False) for i in range(count)
-    ]
-    fresh_narrow = [send_clone(living[i].astype(jnp.bfloat16), route[i]) for i in range(count)]
+    picked, route, slot = pick_clones(spectra, clones)
+    fresh_narrow = [send_clone(picked[i], route[i]) for i in range(count)]
     state = spectra
     if extra:
         state = jnp.pad(state, ((0, 0), (0, 0), (0, extra), (0, 0)))
@@ -441,10 +468,10 @@
         return lax.all_to_all(x, "space", split_axis=0, concat_axis=0, tiled=True)
 
     def swap(parts):
-        return [
-            lax.ppermute(x, "space", [(d, d ^ n) for d in range(space)]) if n else x
-            for n, x in enumerate(parts)
-        ]
+        got = list(parts)
+        for n in reversed(range(1, space)):
+            got[n] = lax.ppermute(parts[n], "space", [(d, d ^ n) for d in range(space)])
+        return got
 
     def spread(parts):
         if direct:
@@ -539,8 +566,14 @@
     sent = []
     for x in made:
         sent.append(spread(x[:slots]))
-    wide, _ = lax.optimization_barrier((living, made[1][0]))
-    fresh = [share_row(wide[i], owner[i]) for i in range(count)]
+    later, _ = lax.optimization_barrier((clones[:, 1], made[1][0]))
+    fresh = [
+        share_row(
+            lax.dynamic_index_in_dim(spectra, lax.rem(later[i], trajectories), 0, keepdims=False),
+            lax.div(later[i], trajectories),
+        )
+        for i in range(count)
+    ]
     if extra:
         fresh = [jnp.pad(x, ((0, 0), (0, extra), (0, 0))) for x in fresh]
     back = []

time: 377 us -> 381 us (1.011)
  the two profiles are of different devices: /device:TPU:8 before, /device:TPU:16 now
where the time goes in v5:
time: 381 us; the launch traced here: 380 us
  waiting for transfers between devices  130 us (34%)
  Pallas kernels  115 us (30%)
  starting transfers between devices  89.9 us (24%)
  other arithmetic  26.6 us (7%)
  local copies, waits for them, and re-layouts  13.1 us (3%)
  between operations  5.62 us (1%)
    ppermute x42, waiting for transfers between devices, swap(): got[n] = lax.ppermute(parts[n], 'space', [(d, d ^ n) for d in range(space)])  118 us
    ppermute x42, starting transfers between devices, swap(): got[n] = lax.ppermute(parts[n], 'space', [(d, d ^ n) for d in range(space)])  72.6 us
    pallas_call x3, Pallas kernels, grid(): pl.pallas_call(functools.partial(grid_kernel, scale=1.0 / truncation), ou...  43.3 us
    pallas_call x3, Pallas kernels, forward(): pl.pallas_call(functools.partial(forward_kernel, truncation=truncation, p...  37.2 us
    pallas_call x2, Pallas kernels, inverse(): pl.pallas_call(functools.partial(inverse_kernel, truncation=truncation, p...  31 us
    another operation x1, other arithmetic  15.9 us
    ppermute x4, starting transfers between devices, share_row(): other = lax.ppermute(row, 'member', [(m, m ^ bit) for m in range(members)])  15.3 us
    ppermute x2, waiting for transfers between devices, move(): return lambda v: lax.ppermute(v, 'member', [(a, b)])  11.5 us
  transfers between devices with their start and end apart: 48, of which 18 were waited for; matrix products, arithmetic and copies ran while one was open for 9% of the time, Pallas kernels for 19%

profile of v5, /device:TPU:16, one launch (start us, length us, event | category | flops | bytes accessed | tf_op | source)
XLA Modules:
  0.0 380.1 jit_solution(6749398006994088581)
XLA Ops:
  0.7 3.5 pick.1
  8.3 12.9 %conditional.2 = (bf16[12,40,641]{2,1,0:T(8,128)(2,1)S(1)}) conditional(s32[]{:T(128)} %bitcast.6, bf16[12,40,641]{2,1,0:T(8,128)(2,1)S(1)} %get-tuple-element.194, bf16[12,40,641]{2,1,0:T(8,128)(2,1)S(1)} %get-tuple-element.194, bf16[12,40,641]{2,1,0:T(8,128)(2,1)S(1)} %get-tuple-element.194, ...), branch_computations={%region_0.0_spmd, %region_1.0_spmd, %region_2.0_spmd, %region_3.0_... | conditional | bytes 3692208 | solution.py:365
  9.6 11.5 %collective-permute-done.9 = bf16[12,40,641]{2,1,0:T(8,128)(2,1)S(1)} collective-permute-done((bf16[12,40,641]{2,1,0:T(8,128)(2,1)S(1)}, bf16[12,40,641]{2,1,0:T(8,128)(2,1)S(1)}, u32[]{:S(2)}, u32[]{:S(2)}) %collective-permute-start.9) | collective-permute-done | bytes 615392 | tf_op jit(solution)/shard_map/cond/branch_12_fun/ppermute | solution.py:362
  22.8 11.2 %forward.3 = (bf16[6,160,128]{2,1,0:T(8,128)(2,1)}, bf16[6,160,128]{2,1,0:T(8,128)(2,1)}, bf16[6,160,128]{2,1,0:T(8,128)(2,1)}, bf16[6,160,128]{2,1,0:T(8,128)(2...) custom-call(s32[11]{0:T(128)} %pad_add_fusion.1.where_ref, ...), custom_call_target="tpu_custom_call" | custom-call | flops 1260257280 | bytes 16777216 | tf_op jit(solution)/shard_map/forward/pallas_call | solution.py:431
  34.1 12.9 %forward.4 = (bf16[6,160,128]{2,1,0:T(8,128)(2,1)}, bf16[6,160,128]{2,1,0:T(8,128)(2,1)}, bf16[6,160,128]{2,1,0:T(8,128)(2,1)}, bf16[6,160,128]{2,1,0:T(8,128)(2...) custom-call(s32[11]{0:T(128)} %pad_add_fusion.1.where_ref, ...), custom_call_target="tpu_custom_call" | custom-call | flops 1260257280 | bytes 16777216 | tf_op jit(solution)/shard_map/forward/pallas_call | solution.py:431
  50.5 3.9 %collective-permute-start.28 = (bf16[6,160,128]{2,1,0:T(8,128)(2,1)}, bf16[6,160,128]{2,1,0:T(8,128)(2,1)S(1)}, u32[]{:S(2)}, u32[]{:S(2)}) collective-permute-start(bf16[6,160,128]{2,1,0:T(8,128)(2,1)} %get-tuple-element.141), channel_id=1, source_target_pairs={{0,5},{1,4},{2,7},{3,6},{4,1},{5,0},{6,3},{7,2},{8,13},{9,12},{10,... | collective-permute-start | bytes 737288 | tf_op jit(solution)/shard_map/ppermute | solution.py:473
  54.5 15.9 %fusion.7 = (bf16[1280,640]{1,0:T(8,128)(2,1)}, bf16[1280,640]{1,0:T(8,128)(2,1)}) fusion(s32[1280]{0:T(1024)S(1)} %get-tuple-element.211, s32[1280]{0:T(1024)S(1)} %get-tuple-element.210, pred[1280]{0:T(1024)(128)(4,1)S(1)} %fusion.22), kind=kLoop, calls=%fused_computation.11 | loop fusion | flops 11468800 | bytes 3288320 | tf_op jit(solution)/shard_map/convert
  70.6 13.0 %forward.5 = (bf16[6,160,128]{2,1,0:T(8,128)(2,1)}, bf16[6,160,128]{2,1,0:T(8,128)(2,1)}, bf16[6,160,128]{2,1,0:T(8,128)(2,1)}, bf16[6,160,128]{2,1,0:T(8,128)(2...) custom-call(s32[11]{0:T(128)} %pad_add_fusion.1.where_ref, ...), custom_call_target="tpu_custom_call" | custom-call | flops 1260257280 | bytes 16777216 | tf_op jit(solution)/shard_map/forward/pallas_call | solution.py:431
  88.4 3.8 %dynamic-slice_bitcast_fusion = (f32[12,40,641]{2,1,0:T(8,128)}, f32[12,40,641]{2,1,0:T(8,128)}) fusion(f32[4,12,40,641]{3,2,1,0:T(8,128)} %refs_9_.1, s32[]{:T(128)S(6)} %select_n.193, s32[]{:T(128)S(6)} %select_n.188), kind=kLoop, calls=%fused_computation.12 | loop fusion | bytes 4922888 | tf_op jit(solution)/shard_map/jit(dynamic_index_in_dim)/squeeze | solution.py:572
  98.6 6.3 %collective-permute-start.66 = (f32[12,40,641]{2,1,0:T(8,128)}, f32[12,40,641]{2,1,0:T(8,128)}, u32[]{:S(2)}, u32[]{:S(2)}) collective-permute-start(f32[12,40,641]{2,1,0:T(8,128)} %get-tuple-element.192), channel_id=1, source_target_pairs={{0,8},{8,0},{16,24},{24,16},{1,9},{9,1},{17,25},{25,17},{2,10},{10... | collective-permute-start | bytes 3692168 | tf_op jit(solution)/shard_map/ppermute | solution.py:373
  106.3 6.6 %collective-permute-start.42 = (bf16[6,160,128]{2,1,0:T(8,128)(2,1)}, bf16[6,160,128]{2,1,0:T(8,128)(2,1)}, u32[]{:S(2)}, u32[]{:S(2)}) collective-permute-start(bf16[6,160,128]{2,1,0:T(8,128)(2,1)} %get-tuple-element.159), channel_id=1, source_target_pairs={{0,5},{1,4},{2,7},{3,6},{4,1},{5,0},{6,3},{7,2},{8,13},{9,12},{10,... | collective-permute-start | bytes 737288 | tf_op jit(solution)/shard_map/ppermute | solution.py:473
  112.9 7.6 %collective-permute-start.68 = (f32[12,40,641]{2,1,0:T(8,128)}, f32[12,40,641]{2,1,0:T(8,128)}, u32[]{:S(2)}, u32[]{:S(2)}) collective-permute-start(f32[12,40,641]{2,1,0:T(8,128)} %get-tuple-element.191), channel_id=1, source_target_pairs={{0,8},{8,0},{16,24},{24,16},{1,9},{9,1},{17,25},{25,17},{2,10},{10... | collective-permute-start | bytes 3692168 | tf_op jit(solution)/shard_map/ppermute | solution.py:373
  124.5 8.7 %collective-permute-done.42.refs_5_ = bf16[6,160,128]{2,1,0:T(8,128)(2,1)} collective-permute-done((bf16[6,160,128]{2,1,0:T(8,128)(2,1)}, bf16[6,160,128]{2,1,0:T(8,128)(2,1)}, u32[]{:S(2)}, u32[]{:S(2)}) %collective-permute-start.42) | collective-permute-done | bytes 245792 | tf_op jit(solution)/shard_map/ppermute | solution.py:473
  133.2 8.8 %collective-permute-start.52 = (bf16[6,160,128]{2,1,0:T(8,128)(2,1)}, bf16[6,160,128]{2,1,0:T(8,128)(2,1)S(1)}, u32[]{:S(2)}, u32[]{:S(2)}) collective-permute-start(bf16[6,160,128]{2,1,0:T(8,128)(2,1)} %get-tuple-element.173), channel_id=1, source_target_pairs={{0,1},{1,0},{2,3},{3,2},{4,5},{5,4},{6,7},{7,6},{8,9},{9,8},{10,11... | collective-permute-start | bytes 737288 | tf_op jit(solution)/shard_map/ppermute | solution.py:473
  145.5 14.6 %grid.3 = (bf16[6,160,128]{2,1,0:T(8,128)(2,1)}, bf16[6,160,128]{2,1,0:T(8,128)(2,1)}, bf16[6,160,128]{2,1,0:T(8,128)(2,1)}, bf16[6,160,128]{2,1,0:T(8,128)(2,1)...) custom-call(s32[8]{0:T(128)} %copy-done.21, ...), custom_call_target="tpu_custom_call" | custom-call | flops 5033164800 | bytes 12582912 | tf_op jit(solution)/shard_map/grid/pallas_call | solution.py:507
  172.7 19.5 %collective-permute-done.55.refs_4_ = bf16[6,160,128]{2,1,0:T(8,128)(2,1)S(1)} collective-permute-done((bf16[6,160,128]{2,1,0:T(8,128)(2,1)S(1)}, bf16[6,160,128]{2,1,0:T(8,128)(2,1)S(1)}, u32[]{:S(2)}, u32[]{:S(2)}) %collective-permute-start.55) | collective-permute-done | bytes 245792 | tf_op jit(solution)/shard_map/ppermute | solution.py:473
  193.7 3.8 %collective-permute-done.56.refs_5_ = bf16[6,160,128]{2,1,0:T(8,128)(2,1)S(1)} collective-permute-done((bf16[6,160,128]{2,1,0:T(8,128)(2,1)S(1)}, bf16[6,160,128]{2,1,0:T(8,128)(2,1)S(1)}, u32[]{:S(2)}, u32[]{:S(2)}) %collective-permute-start.56) | collective-permute-done | bytes 245792 | tf_op jit(solution)/shard_map/ppermute | solution.py:473
  199.0 4.0 %collective-permute-done.57.refs_6_ = bf16[6,160,128]{2,1,0:T(8,128)(2,1)S(1)} collective-permute-done((bf16[6,160,128]{2,1,0:T(8,128)(2,1)S(1)}, bf16[6,160,128]{2,1,0:T(8,128)(2,1)S(1)}, u32[]{:S(2)}, u32[]{:S(2)}) %collective-permute-start.57) | collective-permute-done | bytes 245792 | tf_op jit(solution)/shard_map/ppermute | solution.py:473
  208.6 5.2 %collective-permute-start.35 = (bf16[6,160,128]{2,1,0:T(8,128)(2,1)}, bf16[6,160,128]{2,1,0:T(8,128)(2,1)S(1)}, u32[]{:S(2)}, u32[]{:S(2)}) collective-permute-start(bf16[6,160,128]{2,1,0:T(8,128)(2,1)} %get-tuple-element.149), channel_id=1, source_target_pairs={{0,5},{1,4},{2,7},{3,6},{4,1},{5,0},{6,3},{7,2},{8,13},{9,12},{10,... | collective-permute-start | bytes 737288 | tf_op jit(solution)/shard_map/ppermute | solution.py:473
  216.0 14.4 %grid.4 = (bf16[6,160,128]{2,1,0:T(8,128)(2,1)}, bf16[6,160,128]{2,1,0:T(8,128)(2,1)}, bf16[6,160,128]{2,1,0:T(8,128)(2,1)}, bf16[6,160,128]{2,1,0:T(8,128)(2,1)...) custom-call(s32[8]{0:T(128)} %copy-done.21, ...), custom_call_target="tpu_custom_call" | custom-call | flops 5033164800 | bytes 12582912 | tf_op jit(solution)/shard_map/grid/pallas_call | solution.py:507
  230.4 4.7 %collective-permute-start.37 = (bf16[6,160,128]{2,1,0:T(8,128)(2,1)}, bf16[6,160,128]{2,1,0:T(8,128)(2,1)S(1)}, u32[]{:S(2)}, u32[]{:S(2)}) collective-permute-start(bf16[6,160,128]{2,1,0:T(8,128)(2,1)} %get-tuple-element.151), channel_id=1, source_target_pairs={{0,7},{1,6},{2,5},{3,4},{4,3},{5,2},{6,1},{7,0},{8,15},{9,14},{10,... | collective-permute-start | bytes 737288 | tf_op jit(solution)/shard_map/ppermute | solution.py:473
  237.4 13.0 %collective-permute-done.36.refs_6_ = bf16[6,160,128]{2,1,0:T(8,128)(2,1)} collective-permute-done((bf16[6,160,128]{2,1,0:T(8,128)(2,1)}, bf16[6,160,128]{2,1,0:T(8,128)(2,1)}, u32[]{:S(2)}, u32[]{:S(2)}) %collective-permute-start.36) | collective-permute-done | bytes 245792 | tf_op jit(solution)/shard_map/ppermute | solution.py:473
  250.4 14.3 %grid.5 = (bf16[6,160,128]{2,1,0:T(8,128)(2,1)}, bf16[6,160,128]{2,1,0:T(8,128)(2,1)}, bf16[6,160,128]{2,1,0:T(8,128)(2,1)}, bf16[6,160,128]{2,1,0:T(8,128)(2,1)...) custom-call(s32[8]{0:T(128)} %copy-done.21, ...), custom_call_target="tpu_custom_call" | custom-call | flops 5033164800 | bytes 12582912 | tf_op jit(solution)/shard_map/grid/pallas_call | solution.py:507
  268.4 5.2 %collective-permute-done.59.refs_1_ = bf16[6,160,128]{2,1,0:T(8,128)(2,1)} collective-permute-done((bf16[6,160,128]{2,1,0:T(8,128)(2,1)}, bf16[6,160,128]{2,1,0:T(8,128)(2,1)}, u32[]{:S(2)}, u32[]{:S(2)}) %collective-permute-start.59) | collective-permute-done | bytes 245792 | tf_op jit(solution)/shard_map/ppermute | solution.py:473
  277.8 4.5 %collective-permute-done.61.refs_3_ = bf16[6,160,128]{2,1,0:T(8,128)(2,1)} collective-permute-done((bf16[6,160,128]{2,1,0:T(8,128)(2,1)}, bf16[6,160,128]{2,1,0:T(8,128)(2,1)}, u32[]{:S(2)}, u32[]{:S(2)}) %collective-permute-start.61) | collective-permute-done | bytes 245792 | tf_op jit(solution)/shard_map/ppermute | solution.py:473
  286.4 14.5 %collective-permute-done.62.refs_4_ = bf16[6,160,128]{2,1,0:T(8,128)(2,1)S(1)} collective-permute-done((bf16[6,160,128]{2,1,0:T(8,128)(2,1)}, bf16[6,160,128]{2,1,0:T(8,128)(2,1)S(1)}, u32[]{:S(2)}, u32[]{:S(2)}) %collective-permute-start.62) | collective-permute-done | bytes 245792 | tf_op jit(solution)/shard_map/ppermute | solution.py:473
  300.8 6.6 %collective-permute-start.47 = (bf16[6,160,128]{2,1,0:T(8,128)(2,1)}, bf16[6,160,128]{2,1,0:T(8,128)(2,1)S(1)}, u32[]{:S(2)}, u32[]{:S(2)}) collective-permute-start(bf16[6,160,128]{2,1,0:T(8,128)(2,1)} %get-tuple-element.165), channel_id=1, source_target_pairs={{0,3},{1,2},{2,1},{3,0},{4,7},{5,6},{6,5},{7,4},{8,11},{9,10},{10,... | collective-permute-start | bytes 737288 | tf_op jit(solution)/shard_map/ppermute | solution.py:473
  308.1 3.8 collective-permute-start.48
  311.9 8.7 %collective-permute-done.64.refs_6_ = bf16[6,160,128]{2,1,0:T(8,128)(2,1)S(1)} collective-permute-done((bf16[6,160,128]{2,1,0:T(8,128)(2,1)}, bf16[6,160,128]{2,1,0:T(8,128)(2,1)S(1)}, u32[]{:S(2)}, u32[]{:S(2)}) %collective-permute-start.64) | collective-permute-done | bytes 245792 | tf_op jit(solution)/shard_map/ppermute | solution.py:473
  320.6 22.3 %collective-permute-done.65.refs_7_ = bf16[6,160,128]{2,1,0:T(8,128)(2,1)S(1)} collective-permute-done((bf16[6,160,128]{2,1,0:T(8,128)(2,1)}, bf16[6,160,128]{2,1,0:T(8,128)(2,1)S(1)}, u32[]{:S(2)}, u32[]{:S(2)}) %collective-permute-start.65) | collective-permute-done | bytes 245792 | tf_op jit(solution)/shard_map/ppermute | solution.py:473
  347.3 14.6 %inverse.2.refs_18_ = f32[4,12,40,641]{3,2,1,0:T(8,128)} custom-call(s32[11]{0:T(128)} %pad_add_fusion.1.where_ref, f32[2,2]{1,0:T(2,128)} %gravity_ref.3, f32[2,2]{1,0:T(2,128)} %stability_ref.3, bf16[6,160,128]{2,1,0:T(8,128)(2,1)} %get-tuple-element.180.refs_0_, bf16[6,160,128]{2,1,0:T(8,128)(2,1)} %collective-permute-done.59.refs_1_, ...), custom_call_target="tpu_custom_call" | custom-call | flops 1260257280 | bytes 20971520 | tf_op jit(solution)/shard_map/inverse/pallas_call | solution.py:529
  363.6 16.4 %inverse.3 = f32[4,12,40,641]{3,2,1,0:T(8,128)} custom-call(s32[11]{0:T(128)} %pad_add_fusion.1.where_ref, f32[2,2]{1,0:T(2,128)} %gravity_ref.3, f32[2,2]{1,0:T(2,128)} %stability_ref.3, bf16[6,160,128]{2,1,0:T(8,128)(2,1)} %get-tuple-element.144.refs_0_, bf16[6,160,128]{2,1,0:T(8,128)(2,1)} %copy-done.4, bf16[6,160,128]{2,1,0:T(8,128)(2,1)} %copy-done.5, ...), custom_call_target="tpu_custom_call" | custom-call | flops 2520514560 | bytes 20971520 | tf_op jit(solution)/shard_map/inverse/pallas_call | solution.py:529
  (192 shorter events, 71.4 us)
Async XLA Ops:
  47.0 36.6 %collective-permute-start.24 = (bf16[6,160,128]{2,1,0:T(8,128)(2,1)}, bf16[6,160,128]{2,1,0:T(8,128)(2,1)S(1)}, u32[]{:S(2)}, u32[]{:S(2)}) collective-permute-start(bf16[6,160,128]{2,1,0:T(8,128)(2,1)} %get-tuple-element.137), channel_id=1, source_target_pairs={{0,1},{1,0},{2,3},{3,2},{4,5},{5,4},{6,7},{7,6},{8,9},{9,8},{10,11... | collective-permute-start | bytes 737288 | tf_op jit(solution)/shard_map/ppermute | solution.py:473
  48.5 43.6 %collective-permute-start.25 = (bf16[6,160,128]{2,1,0:T(8,128)(2,1)}, bf16[6,160,128]{2,1,0:T(8,128)(2,1)S(1)}, u32[]{:S(2)}, u32[]{:S(2)}) collective-permute-start(bf16[6,160,128]{2,1,0:T(8,128)(2,1)} %get-tuple-element.138), channel_id=1, source_target_pairs={{0,2},{1,3},{2,0},{3,1},{4,6},{5,7},{6,4},{7,5},{8,10},{9,11},{10,... | collective-permute-start | bytes 737288 | tf_op jit(solution)/shard_map/ppermute | solution.py:473
  50.1 43.6 %collective-permute-start.26 = (bf16[6,160,128]{2,1,0:T(8,128)(2,1)}, bf16[6,160,128]{2,1,0:T(8,128)(2,1)S(1)}, u32[]{:S(2)}, u32[]{:S(2)}) collective-permute-start(bf16[6,160,128]{2,1,0:T(8,128)(2,1)} %get-tuple-element.139), channel_id=1, source_target_pairs={{0,3},{1,2},{2,1},{3,0},{4,7},{5,6},{6,5},{7,4},{8,11},{9,10},{10,... | collective-permute-start | bytes 737288 | tf_op jit(solution)/shard_map/ppermute | solution.py:473
  50.5 44.7 %collective-permute-start.27 = (bf16[6,160,128]{2,1,0:T(8,128)(2,1)}, bf16[6,160,128]{2,1,0:T(8,128)(2,1)S(1)}, u32[]{:S(2)}, u32[]{:S(2)}) collective-permute-start(bf16[6,160,128]{2,1,0:T(8,128)(2,1)} %get-tuple-element.140), channel_id=1, source_target_pairs={{0,4},{1,5},{2,6},{3,7},{4,0},{5,1},{6,2},{7,3},{8,12},{9,13},{10,... | collective-permute-start | bytes 737288 | tf_op jit(solution)/shard_map/ppermute | solution.py:473
  50.5 48.1 %collective-permute-start.28 = (bf16[6,160,128]{2,1,0:T(8,128)(2,1)}, bf16[6,160,128]{2,1,0:T(8,128)(2,1)S(1)}, u32[]{:S(2)}, u32[]{:S(2)}) collective-permute-start(bf16[6,160,128]{2,1,0:T(8,128)(2,1)} %get-tuple-element.141), channel_id=1, source_target_pairs={{0,5},{1,4},{2,7},{3,6},{4,1},{5,0},{6,3},{7,2},{8,13},{9,12},{10,... | collective-permute-start | bytes 737288 | tf_op jit(solution)/shard_map/ppermute | solution.py:473
  98.6 67.5 %collective-permute-start.66 = (f32[12,40,641]{2,1,0:T(8,128)}, f32[12,40,641]{2,1,0:T(8,128)}, u32[]{:S(2)}, u32[]{:S(2)}) collective-permute-start(f32[12,40,641]{2,1,0:T(8,128)} %get-tuple-element.192), channel_id=1, source_target_pairs={{0,8},{8,0},{16,24},{24,16},{1,9},{9,1},{17,25},{25,17},{2,10},{10... | collective-permute-start | bytes 3692168 | tf_op jit(solution)/shard_map/ppermute | solution.py:373
  106.3 26.9 %collective-permute-start.42 = (bf16[6,160,128]{2,1,0:T(8,128)(2,1)}, bf16[6,160,128]{2,1,0:T(8,128)(2,1)}, u32[]{:S(2)}, u32[]{:S(2)}) collective-permute-start(bf16[6,160,128]{2,1,0:T(8,128)(2,1)} %get-tuple-element.159), channel_id=1, source_target_pairs={{0,5},{1,4},{2,7},{3,6},{4,1},{5,0},{6,3},{7,2},{8,13},{9,12},{10,... | collective-permute-start | bytes 737288 | tf_op jit(solution)/shard_map/ppermute | solution.py:473
  112.9 32.5 %collective-permute-start.43 = (bf16[6,160,128]{2,1,0:T(8,128)(2,1)}, bf16[6,160,128]{2,1,0:T(8,128)(2,1)}, u32[]{:S(2)}, u32[]{:S(2)}) collective-permute-start(bf16[6,160,128]{2,1,0:T(8,128)(2,1)} %get-tuple-element.160), channel_id=1, source_target_pairs={{0,6},{1,7},{2,4},{3,5},{4,2},{5,3},{6,0},{7,1},{8,14},{9,15},{10,... | collective-permute-start | bytes 737288 | tf_op jit(solution)/shard_map/ppermute | solution.py:473
  112.9 90.2 %collective-permute-start.68 = (f32[12,40,641]{2,1,0:T(8,128)}, f32[12,40,641]{2,1,0:T(8,128)}, u32[]{:S(2)}, u32[]{:S(2)}) collective-permute-start(f32[12,40,641]{2,1,0:T(8,128)} %get-tuple-element.191), channel_id=1, source_target_pairs={{0,8},{8,0},{16,24},{24,16},{1,9},{9,1},{17,25},{25,17},{2,10},{10... | collective-permute-start | bytes 3692168 | tf_op jit(solution)/shard_map/ppermute | solution.py:373
  124.5 35.6 %collective-permute-start.44 = (bf16[6,160,128]{2,1,0:T(8,128)(2,1)}, bf16[6,160,128]{2,1,0:T(8,128)(2,1)S(1)}, u32[]{:S(2)}, u32[]{:S(2)}) collective-permute-start(bf16[6,160,128]{2,1,0:T(8,128)(2,1)} %get-tuple-element.161), channel_id=1, source_target_pairs={{0,7},{1,6},{2,5},{3,4},{4,3},{5,2},{6,1},{7,0},{8,15},{9,14},{10,... | collective-permute-start | bytes 737288 | tf_op jit(solution)/shard_map/ppermute | solution.py:473
  133.2 30.2 %collective-permute-start.52 = (bf16[6,160,128]{2,1,0:T(8,128)(2,1)}, bf16[6,160,128]{2,1,0:T(8,128)(2,1)S(1)}, u32[]{:S(2)}, u32[]{:S(2)}) collective-permute-start(bf16[6,160,128]{2,1,0:T(8,128)(2,1)} %get-tuple-element.173), channel_id=1, source_target_pairs={{0,1},{1,0},{2,3},{3,2},{4,5},{5,4},{6,7},{7,6},{8,9},{9,8},{10,11... | collective-permute-start | bytes 737288 | tf_op jit(solution)/shard_map/ppermute | solution.py:473
  145.4 20.0 %collective-permute-start.53 = (bf16[6,160,128]{2,1,0:T(8,128)(2,1)S(1)}, bf16[6,160,128]{2,1,0:T(8,128)(2,1)S(1)}, u32[]{:S(2)}, u32[]{:S(2)}) collective-permute-start(bf16[6,160,128]{2,1,0:T(8,128)(2,1)S(1)} %copy-done.28), channel_id=1, source_target_pairs={{0,2},{1,3},{2,0},{3,1},{4,6},{5,7},{6,4},{7,5},{8,10},{9,11},{10,... | collective-permute-start | bytes 737288 | tf_op jit(solution)/shard_map/ppermute | solution.py:473
  163.4 28.8 %collective-permute-start.55 = (bf16[6,160,128]{2,1,0:T(8,128)(2,1)S(1)}, bf16[6,160,128]{2,1,0:T(8,128)(2,1)S(1)}, u32[]{:S(2)}, u32[]{:S(2)}) collective-permute-start(bf16[6,160,128]{2,1,0:T(8,128)(2,1)S(1)} %copy-done.26), channel_id=1, source_target_pairs={{0,4},{1,5},{2,6},{3,7},{4,0},{5,1},{6,2},{7,3},{8,12},{9,13},{10,... | collective-permute-start | bytes 737288 | tf_op jit(solution)/shard_map/ppermute | solution.py:473
  165.4 32.1 %collective-permute-start.56 = (bf16[6,160,128]{2,1,0:T(8,128)(2,1)S(1)}, bf16[6,160,128]{2,1,0:T(8,128)(2,1)S(1)}, u32[]{:S(2)}, u32[]{:S(2)}) collective-permute-start(bf16[6,160,128]{2,1,0:T(8,128)(2,1)S(1)} %copy-done.25), channel_id=1, source_target_pairs={{0,5},{1,4},{2,7},{3,6},{4,1},{5,0},{6,3},{7,2},{8,13},{9,12},{10,... | collective-permute-start | bytes 737288 | tf_op jit(solution)/shard_map/ppermute | solution.py:473
  166.2 36.9 %collective-permute-start.57 = (bf16[6,160,128]{2,1,0:T(8,128)(2,1)S(1)}, bf16[6,160,128]{2,1,0:T(8,128)(2,1)S(1)}, u32[]{:S(2)}, u32[]{:S(2)}) collective-permute-start(bf16[6,160,128]{2,1,0:T(8,128)(2,1)S(1)} %copy-done.24), channel_id=1, source_target_pairs={{0,6},{1,7},{2,4},{3,5},{4,2},{5,3},{6,0},{7,1},{8,14},{9,15},{10,... | collective-permute-start | bytes 737288 | tf_op jit(solution)/shard_map/ppermute | solution.py:473
  172.0 36.6 %collective-permute-start.58 = (bf16[6,160,128]{2,1,0:T(8,128)(2,1)S(1)}, bf16[6,160,128]{2,1,0:T(8,128)(2,1)S(1)}, u32[]{:S(2)}, u32[]{:S(2)}) collective-permute-start(bf16[6,160,128]{2,1,0:T(8,128)(2,1)S(1)} %copy-done.23), channel_id=1, source_target_pairs={{0,7},{1,6},{2,5},{3,4},{4,3},{5,2},{6,1},{7,0},{8,15},{9,14},{10,... | collective-permute-start | bytes 737288 | tf_op jit(solution)/shard_map/ppermute | solution.py:473
  203.1 79.8 %collective-permute-start.67 = (f32[12,40,641]{2,1,0:T(8,128)S(1)}, f32[12,40,641]{2,1,0:T(8,128)}, u32[]{:S(2)}, u32[]{:S(2)}) collective-permute-start(f32[12,40,641]{2,1,0:T(8,128)S(1)} %broadcast_select_fusion.2), channel_id=1, source_target_pairs={{0,16},{8,24},{16,0},{24,8},{1,17},{9,25},{17,1},{25,9},{2,18},{10... | collective-permute-start | bytes 3692168 | tf_op jit(solution)/shard_map/ppermute | solution.py:373
  208.6 21.8 %collective-permute-start.34 = (bf16[6,160,128]{2,1,0:T(8,128)(2,1)}, bf16[6,160,128]{2,1,0:T(8,128)(2,1)S(1)}, u32[]{:S(2)}, u32[]{:S(2)}) collective-permute-start(bf16[6,160,128]{2,1,0:T(8,128)(2,1)} %get-tuple-element.148), channel_id=1, source_target_pairs={{0,4},{1,5},{2,6},{3,7},{4,0},{5,1},{6,2},{7,3},{8,12},{9,13},{10,... | collective-permute-start | bytes 737288 | tf_op jit(solution)/shard_map/ppermute | solution.py:473
  208.6 27.1 %collective-permute-start.35 = (bf16[6,160,128]{2,1,0:T(8,128)(2,1)}, bf16[6,160,128]{2,1,0:T(8,128)(2,1)S(1)}, u32[]{:S(2)}, u32[]{:S(2)}) collective-permute-start(bf16[6,160,128]{2,1,0:T(8,128)(2,1)} %get-tuple-element.149), channel_id=1, source_target_pairs={{0,5},{1,4},{2,7},{3,6},{4,1},{5,0},{6,3},{7,2},{8,13},{9,12},{10,... | collective-permute-start | bytes 737288 | tf_op jit(solution)/shard_map/ppermute | solution.py:473
  213.9 36.6 %collective-permute-start.36 = (bf16[6,160,128]{2,1,0:T(8,128)(2,1)}, bf16[6,160,128]{2,1,0:T(8,128)(2,1)}, u32[]{:S(2)}, u32[]{:S(2)}) collective-permute-start(bf16[6,160,128]{2,1,0:T(8,128)(2,1)} %get-tuple-element.150), channel_id=1, source_target_pairs={{0,6},{1,7},{2,4},{3,5},{4,2},{5,3},{6,0},{7,1},{8,14},{9,15},{10,... | collective-permute-start | bytes 737288 | tf_op jit(solution)/shard_map/ppermute | solution.py:473
  215.9 126.9 %collective-permute-start.69 = (f32[12,40,641]{2,1,0:T(8,128)S(1)}, f32[12,40,641]{2,1,0:T(8,128)}, u32[]{:S(2)}, u32[]{:S(2)}) collective-permute-start(f32[12,40,641]{2,1,0:T(8,128)S(1)} %broadcast_select_fusion), channel_id=1, source_target_pairs={{0,16},{8,24},{16,0},{24,8},{1,17},{9,25},{17,1},{25,9},{2,18},{10... | collective-permute-start | bytes 3692168 | tf_op jit(solution)/shard_map/ppermute | solution.py:373
  230.4 34.4 %collective-permute-start.37 = (bf16[6,160,128]{2,1,0:T(8,128)(2,1)}, bf16[6,160,128]{2,1,0:T(8,128)(2,1)S(1)}, u32[]{:S(2)}, u32[]{:S(2)}) collective-permute-start(bf16[6,160,128]{2,1,0:T(8,128)(2,1)} %get-tuple-element.151), channel_id=1, source_target_pairs={{0,7},{1,6},{2,5},{3,4},{4,3},{5,2},{6,1},{7,0},{8,15},{9,14},{10,... | collective-permute-start | bytes 737288 | tf_op jit(solution)/shard_map/ppermute | solution.py:473
  235.8 30.6 %collective-permute-start.45 = (bf16[6,160,128]{2,1,0:T(8,128)(2,1)}, bf16[6,160,128]{2,1,0:T(8,128)(2,1)S(1)}, u32[]{:S(2)}, u32[]{:S(2)}) collective-permute-start(bf16[6,160,128]{2,1,0:T(8,128)(2,1)} %get-tuple-element.163), channel_id=1, source_target_pairs={{0,1},{1,0},{2,3},{3,2},{4,5},{5,4},{6,7},{7,6},{8,9},{9,8},{10,11... | collective-permute-start | bytes 737288 | tf_op jit(solution)/shard_map/ppermute | solution.py:473
  273.7 27.2 %collective-permute-start.62 = (bf16[6,160,128]{2,1,0:T(8,128)(2,1)}, bf16[6,160,128]{2,1,0:T(8,128)(2,1)S(1)}, u32[]{:S(2)}, u32[]{:S(2)}) collective-permute-start(bf16[6,160,128]{2,1,0:T(8,128)(2,1)} %get-tuple-element.184), channel_id=1, source_target_pairs={{0,4},{1,5},{2,6},{3,7},{4,0},{5,1},{6,2},{7,3},{8,12},{9,13},{10,... | collective-permute-start | bytes 737288 | tf_op jit(solution)/shard_map/ppermute | solution.py:473
  275.5 31.9 %collective-permute-start.63 = (bf16[6,160,128]{2,1,0:T(8,128)(2,1)}, bf16[6,160,128]{2,1,0:T(8,128)(2,1)S(1)}, u32[]{:S(2)}, u32[]{:S(2)}) collective-permute-start(bf16[6,160,128]{2,1,0:T(8,128)(2,1)} %get-tuple-element.185), channel_id=1, source_target_pairs={{0,5},{1,4},{2,7},{3,6},{4,1},{5,0},{6,3},{7,2},{8,13},{9,12},{10,... | collective-permute-start | bytes 737288 | tf_op jit(solution)/shard_map/ppermute | solution.py:473
  282.3 38.3 %collective-permute-start.64 = (bf16[6,160,128]{2,1,0:T(8,128)(2,1)}, bf16[6,160,128]{2,1,0:T(8,128)(2,1)S(1)}, u32[]{:S(2)}, u32[]{:S(2)}) collective-permute-start(bf16[6,160,128]{2,1,0:T(8,128)(2,1)} %get-tuple-element.186), channel_id=1, source_target_pairs={{0,6},{1,7},{2,4},{3,5},{4,2},{5,3},{6,0},{7,1},{8,14},{9,15},{10,... | collective-permute-start | bytes 737288 | tf_op jit(solution)/shard_map/ppermute | solution.py:473
  282.9 60.0 %collective-permute-start.65 = (bf16[6,160,128]{2,1,0:T(8,128)(2,1)}, bf16[6,160,128]{2,1,0:T(8,128)(2,1)S(1)}, u32[]{:S(2)}, u32[]{:S(2)}) collective-permute-start(bf16[6,160,128]{2,1,0:T(8,128)(2,1)} %get-tuple-element.187), channel_id=1, source_target_pairs={{0,7},{1,6},{2,5},{3,4},{4,3},{5,2},{6,1},{7,0},{8,15},{9,14},{10,... | collective-permute-start | bytes 737288 | tf_op jit(solution)/shard_map/ppermute | solution.py:473
  300.8 61.0 %collective-permute-start.47 = (bf16[6,160,128]{2,1,0:T(8,128)(2,1)}, bf16[6,160,128]{2,1,0:T(8,128)(2,1)S(1)}, u32[]{:S(2)}, u32[]{:S(2)}) collective-permute-start(bf16[6,160,128]{2,1,0:T(8,128)(2,1)} %get-tuple-element.165), channel_id=1, source_target_pairs={{0,3},{1,2},{2,1},{3,0},{4,7},{5,6},{6,5},{7,4},{8,11},{9,10},{10,... | collective-permute-start | bytes 737288 | tf_op jit(solution)/shard_map/ppermute | solution.py:473
  308.1 53.8 %collective-permute-start.48 = (bf16[6,160,128]{2,1,0:T(8,128)(2,1)}, bf16[6,160,128]{2,1,0:T(8,128)(2,1)S(1)}, u32[]{:S(2)}, u32[]{:S(2)}) collective-permute-start(bf16[6,160,128]{2,1,0:T(8,128)(2,1)} %get-tuple-element.166), channel_id=1, source_target_pairs={{0,4},{1,5},{2,6},{3,7},{4,0},{5,1},{6,2},{7,3},{8,12},{9,13},{10,... | collective-permute-start | bytes 737288 | tf_op jit(solution)/shard_map/ppermute | solution.py:473
  320.6 41.3 %collective-permute-start.49 = (bf16[6,160,128]{2,1,0:T(8,128)(2,1)}, bf16[6,160,128]{2,1,0:T(8,128)(2,1)S(1)}, u32[]{:S(2)}, u32[]{:S(2)}) collective-permute-start(bf16[6,160,128]{2,1,0:T(8,128)(2,1)} %get-tuple-element.167), channel_id=1, source_target_pairs={{0,5},{1,4},{2,7},{3,6},{4,1},{5,0},{6,3},{7,2},{8,13},{9,12},{10,... | collective-permute-start | bytes 737288 | tf_op jit(solution)/shard_map/ppermute | solution.py:473
  342.9 19.1 %collective-permute-start.50 = (bf16[6,160,128]{2,1,0:T(8,128)(2,1)}, bf16[6,160,128]{2,1,0:T(8,128)(2,1)S(1)}, u32[]{:S(2)}, u32[]{:S(2)}) collective-permute-start(bf16[6,160,128]{2,1,0:T(8,128)(2,1)} %get-tuple-element.168), channel_id=1, source_target_pairs={{0,6},{1,7},{2,4},{3,5},{4,2},{5,3},{6,0},{7,1},{8,14},{9,15},{10,... | collective-permute-start | bytes 737288 | tf_op jit(solution)/shard_map/ppermute | solution.py:473
  342.9 20.0 %collective-permute-start.51 = (bf16[6,160,128]{2,1,0:T(8,128)(2,1)}, bf16[6,160,128]{2,1,0:T(8,128)(2,1)S(1)}, u32[]{:S(2)}, u32[]{:S(2)}) collective-permute-start(bf16[6,160,128]{2,1,0:T(8,128)(2,1)} %get-tuple-element.169), channel_id=1, source_target_pairs={{0,7},{1,6},{2,5},{3,4},{4,3},{5,2},{6,1},{7,0},{8,15},{9,14},{10,... | collective-permute-start | bytes 737288 | tf_op jit(solution)/shard_map/ppermute | solution.py:473
  (64 other events, 924.4 us)

commit v6 on v5

--- a/solution.py
+++ b/solution.py
@@ -30,19 +30,22 @@
     return leading, (offset & 1) == 1, order + offset
 
 
-def forward_kernel(where_ref, spec_ref, leg_ref, *refs, truncation, pairs, keep, count):
+def forward_kernel(
+    where_ref, spec_ref, leg_ref, *refs, truncation, pairs, keep, count, made, span
+):
     step = pl.program_id(0)
     row_length = truncation + 1
-    trajectories, comps, block, _ = spec_ref.shape
-    rows = trajectories * comps
-    slots = 2 * trajectories
+    _, comps, block, _ = spec_ref.shape
+    rows = span * comps
     fresh_refs, refs = refs[:count], refs[count:]
-    out_refs, refs = refs[:slots], refs[slots:]
+    out_refs, refs = refs[: len(made)], refs[len(made) :]
     if keep:
         keep_ref, refs = refs[0], refs[1:]
     wide, xs, res = refs
     tiles = xs.shape[0]
     padded = tiles * LANES
+    first_place = lax.div(where_ref[1 + count + made[0]], 2)
+    t0 = lax.div(first_place, span) * span
 
     @pl.when(step == 0)
     def _():
@@ -58,12 +61,12 @@
         lanes = slice(k * LANES, k * LANES + width)
         if width < LANES:
             xs[k] = jnp.zeros((rows * block, LANES), jnp.float32)
-        xs[k, :, :width] = spec_ref[:, :, :, lanes].reshape(rows * block, width)
+        xs[k, :, :width] = spec_ref[pl.ds(t0, span), :, :, lanes].reshape(rows * block, width)
 
     for i in range(count):
-        slot = where_ref[1 + i]
-
-        @pl.when(slot >= 0)
+        slot = where_ref[1 + i] - t0
+
+        @pl.when(jnp.logical_and(slot >= 0, slot < span))
         def _():
             at = pl.multiple_of(slot * comps * block, SUB)
             for k in range(tiles):
@@ -77,24 +80,26 @@
         x = jnp.concatenate(
             [xs[k, pl.ds(q, rows, stride=block), :] for k in range(tiles)], axis=1
         )
-        x = x.astype(jnp.bfloat16)
         edge = truncation - first_pair - q
-        column = lax.broadcasted_iota(jnp.int32, (PACKED, padded), 1)
+        group = PACKED if rows % PACKED == 0 else SUB
+        column = lax.broadcasted_iota(jnp.int32, (group, padded), 1)
         leading = column < edge
         odd = (jnp.where(leading, column, column - edge) & 1) == 1
         sign = jnp.where(odd, -1.0, 1.0)
+        kind = jnp.bfloat16 if group == PACKED else jnp.float32
         factors = [
             jnp.where(leading, 1.0, 0.0),
             jnp.where(leading, 0.0, 1.0),
             jnp.where(leading, sign, 0.0),
             jnp.where(leading, 0.0, sign),
         ]
+        x = x.astype(kind)
         lhs = []
         for factor in factors:
-            factor = factor.astype(jnp.bfloat16)
-            for at in range(0, rows, PACKED):
-                lhs.append(x[at : at + PACKED] * factor)
-        lhs = jnp.concatenate(lhs, axis=0)
+            factor = factor.astype(kind)
+            for at in range(0, rows, group):
+                lhs.append(x[at : at + group] * factor)
+        lhs = jnp.concatenate(lhs, axis=0).astype(jnp.bfloat16)
         rhs = wide[pl.ds(q, padded, stride=block), :].astype(jnp.bfloat16)
         if keep:
             keep_ref[q] = rhs
@@ -106,9 +111,9 @@
 
     @pl.when(step == pl.num_programs(0) - 1)
     def _():
-        for n in range(slots):
-            place = where_ref[1 + count + n]
-            t, s = lax.div(place, 2), lax.rem(place, 2)
+        for n, slot in enumerate(made):
+            place = where_ref[1 + count + slot]
+            t, s = lax.div(place, 2) - t0, lax.rem(place, 2)
             base = pl.multiple_of((s * (2 * rows) + t * comps) * pairs, SUB)
             for f in range(comps // 2):
                 parts = []
@@ -199,15 +204,16 @@
 
 
 def inverse_kernel(
-    where_ref, gravity_ref, stability_ref, *refs, truncation, pairs, chunks, last, slots, count
+    where_ref, gravity_ref, stability_ref, *refs, truncation, pairs, chunks, last, stored, slots, count
 ):
     w_refs, refs = refs[: chunks * slots], refs[chunks * slots :]
     leg_refs, refs = refs[:chunks], refs[chunks:]
     spec_ref, refs = refs[0], refs[1:]
-    if last:
-        out_ref, ws, ten = refs
-    else:
-        fresh_refs, (out_ref, ws, ten, wide) = refs[:count], refs[count:]
+    patches = count if stored else 0
+    fresh_refs, refs = refs[:patches], refs[patches:]
+    out_ref, ws, ten = refs[:3]
+    if stored:
+        wide = refs[3]
     step = pl.program_id(0)
     row_length = truncation + 1
     trajectories, comps, block, _ = out_ref.shape
@@ -217,7 +223,7 @@
 
     @pl.when(step == 0)
     def _():
-        if not last:
+        if stored:
             for k in range(chunks):
                 wide[k, row_length * block :, :] = jnp.zeros(
                     (wide.shape[1] - row_length * block, LANES), jnp.float32
@@ -236,7 +242,7 @@
                                 at : at + pairs, :
                             ]
 
-    if not last:
+    if stored:
         for k in range(chunks):
             wide[k, : row_length * block, :] = (
                 leg_refs[k][...].astype(jnp.float32).reshape(row_length * block, LANES)
@@ -246,7 +252,7 @@
     def one(q, carry):
         at = pl.ds(step * block + q, 4 * rows, stride=pairs)
         lhs = jnp.concatenate([ws[k, at, :].astype(jnp.bfloat16) for k in range(chunks)], axis=1)
-        if last:
+        if not stored:
             rhs = jnp.concatenate([leg_refs[k][q] for k in range(chunks)], axis=1)
         else:
             at = pl.ds(q, padded, stride=block)
@@ -286,7 +292,7 @@
             if last:
                 tend = semi_implicit_slabs(old, tend, terms, hm)
             else:
-                for i in range(count):
+                for i in range(patches):
                     mine = where_ref[1 + i] == t
                     old = [jnp.where(mine, fresh_refs[i][c, :, lanes], old[c]) for c in range(comps)]
                 tend = [old[c] + time_step * tend[c] for c in range(comps)]
@@ -315,42 +321,45 @@
     return jnp.concatenate([first, second], axis=1).astype(jnp.bfloat16)
 
 
-def pick_kernel(clones_ref, me_ref, spec_ref, row_ref, route_ref, slot_ref, *, members):
-    i = pl.program_id(0)
-    local = me_ref[1]
+def pick_kernel(clones_ref, spec_ref, row_ref, where_ref, *route_refs, local, pairs, slots, direct):
     row_ref[...] = spec_ref[...].astype(jnp.bfloat16)
-    source = lax.div(clones_ref[i, 1], local)
-    target = lax.div(clones_ref[i, 0], local)
-    route_ref[i] = source * members + target
-    slot_ref[i] = jnp.where(target == me_ref[0], clones_ref[i, 0] - target * local, -1)
-
-
-def pick_clones(spectra, clones):
+    members, member = lax.axis_size("member"), lax.axis_index("member")
+    position = lax.axis_index("space")
+    count = len(route_refs)
+    where_ref[0] = position * pairs
+    for i in range(count):
+        source = lax.div(clones_ref[i, 1], local)
+        target = lax.div(clones_ref[i, 0], local)
+        route_refs[i][0] = source * members + target
+        where_ref[1 + i] = jnp.where(target == member, clones_ref[i, 0] - target * local, -1)
+    for n in range(slots):
+        where_ref[1 + count + n] = jnp.bitwise_xor(position, n) if direct else n
+
+
+def pick_clones(spectra, clones, slots, direct):
     local, comps, pairs, row_length = spectra.shape
     count = clones.shape[0]
-    me = lax.axis_index("member").astype(jnp.int32)
     smem = pl.BlockSpec(memory_space=pltpu.SMEM)
     block = (1, comps, pairs, row_length)
-    return pl.pallas_call(
-        functools.partial(pick_kernel, members=lax.axis_size("member")),
+    got = pl.pallas_call(
+        functools.partial(pick_kernel, local=local, pairs=pairs, slots=slots, direct=direct),
         out_shape=[
             jax.ShapeDtypeStruct((count,) + block[1:], jnp.bfloat16),
-            jax.ShapeDtypeStruct((count,), jnp.int32),
-            jax.ShapeDtypeStruct((count,), jnp.int32),
-        ],
+            jax.ShapeDtypeStruct((1 + count + slots,), jnp.int32),
+        ]
+        + [jax.ShapeDtypeStruct((1,), jnp.int32)] * count,
         grid_spec=pltpu.PrefetchScalarGridSpec(
-            num_scalar_prefetch=2,
+            num_scalar_prefetch=1,
             grid=(count,),
-            in_specs=[
-                pl.BlockSpec(block, lambda i, c, m: (lax.rem(c[i, 1], m[1]), 0, 0, 0)),
-            ],
-            out_specs=[pl.BlockSpec(block, lambda i, c, m: (i, 0, 0, 0)), smem, smem],
+            in_specs=[pl.BlockSpec(block, lambda i, c: (lax.rem(c[i, 1], local), 0, 0, 0))],
+            out_specs=[pl.BlockSpec(block, lambda i, c: (i, 0, 0, 0))] + [smem] * (1 + count),
         ),
         cost_estimate=pl.CostEstimate(
             flops=0, bytes_accessed=6 * 1024 * 1024, transcendentals=0
         ),
         name="pick",
-    )(clones, jnp.stack([me, jnp.int32(local)]), spectra)
+    )(clones, spectra)
+    return got[0], got[1], [r.reshape(()) for r in got[2:]]
 
 
 def send_clone(row, route):
@@ -394,21 +403,17 @@
     rows = trajectories * comps
 
     count = clones.shape[0]
-    picked, route, slot = pick_clones(spectra, clones)
+    slots = 2 * trajectories
+    direct = split == 1
+    picked, where, route = pick_clones(spectra, clones, slots, direct)
     fresh_narrow = [send_clone(picked[i], route[i]) for i in range(count)]
     state = spectra
     if extra:
         state = jnp.pad(state, ((0, 0), (0, 0), (0, extra), (0, 0)))
         fresh_narrow = [jnp.pad(x, ((0, 0), (0, extra), (0, 0))) for x in fresh_narrow]
-    slots = 2 * trajectories
-    direct = split == 1
+    order = jnp.arange(space, dtype=jnp.int32)
     if direct:
-        order = jnp.bitwise_xor(position.astype(jnp.int32), jnp.arange(space, dtype=jnp.int32))
-        slot_order = order
-    else:
-        order = jnp.arange(space, dtype=jnp.int32)
-        slot_order = jnp.arange(slots, dtype=jnp.int32)
-    where = jnp.concatenate([(position * pairs).astype(jnp.int32).reshape(1), slot, slot_order])
+        order = jnp.bitwise_xor(position.astype(jnp.int32), order)
     columns = jnp.transpose(legendre, (1, 0, 2))
     if extra:
         columns = jnp.pad(columns, ((0, 0), (0, extra), (0, 0)))
@@ -425,26 +430,26 @@
 
     mib = 1024 * 1024
 
-    def forward(k, where):
+    def forward(k, where, made, span):
         keep = k > 0
         kept_shape = jax.ShapeDtypeStruct((padded_pairs, tiles * LANES, LANES), jnp.bfloat16)
         return pl.pallas_call(
             functools.partial(
-                forward_kernel, truncation=truncation, pairs=padded_pairs, keep=keep, count=count
+                forward_kernel, truncation=truncation, pairs=padded_pairs, keep=keep, count=count, made=made, span=span
             ),
-            out_shape=[jax.ShapeDtypeStruct(part_shape, jnp.bfloat16)] * slots
+            out_shape=[jax.ShapeDtypeStruct(part_shape, jnp.bfloat16)] * len(made)
             + [kept_shape] * keep,
             grid=(steps,),
             in_specs=[smem, state_spec, leg_spec(k)] + [fresh_spec] * count,
-            out_specs=[part_spec] * slots + [kept_spec] * keep,
+            out_specs=[part_spec] * len(made) + [kept_spec] * keep,
             scratch_shapes=[
                 pltpu.VMEM((tiles * LANES * SUB, LANES), jnp.float32),
-                pltpu.VMEM((tiles, rows * SUB, LANES), jnp.float32),
-                pltpu.VMEM((4 * rows * padded_pairs, LANES), jnp.float32),
+                pltpu.VMEM((tiles, span * comps * SUB, LANES), jnp.float32),
+                pltpu.VMEM((4 * span * comps * padded_pairs, LANES), jnp.float32),
             ],
             compiler_params=pltpu.CompilerParams(vmem_limit_bytes=60 * mib),
             cost_estimate=pl.CostEstimate(
-                flops=8 * rows * padded_pairs * row_length * LANES,
+                flops=8 * span * comps * padded_pairs * row_length * LANES,
                 bytes_accessed=16 * 1024 * 1024,
                 transcendentals=0,
             ),
@@ -522,9 +527,9 @@
             name="grid",
         )(order, (2.0 * mu)[None], weight[None], synthesis, analysis, *parts)
 
-    def inverse(ws, legs, start, patches):
+    def inverse(ws, legs, start, patches, last):
         chunks = len(ws)
-        last = not patches
+        stored = bool(patches)
         wide_scratch = pltpu.VMEM((chunks, tiles * LANES * SUB, LANES), jnp.float32)
         return pl.pallas_call(
             functools.partial(
@@ -533,6 +538,7 @@
                 pairs=padded_pairs,
                 chunks=chunks,
                 last=last,
+                stored=stored,
                 slots=slots,
                 count=count,
             ),
@@ -540,7 +546,7 @@
             grid=(steps,),
             in_specs=[smem] * 3
             + [part_spec] * (chunks * slots)
-            + ([kept_spec] * chunks if last else [leg_spec(k) for k in range(chunks)])
+            + ([leg_spec(k) for k in range(chunks)] if stored else [kept_spec] * chunks)
             + [state_spec]
             + [fresh_spec] * len(patches),
             out_specs=state_spec,
@@ -548,7 +554,7 @@
                 pltpu.VMEM((chunks, 4 * rows * padded_pairs, LANES), jnp.float32),
                 pltpu.VMEM((tiles, rows * SUB, LANES), jnp.float32),
             ]
-            + ([] if last else [wide_scratch]),
+            + ([wide_scratch] if stored else []),
             compiler_params=pltpu.CompilerParams(vmem_limit_bytes=60 * mib),
             cost_estimate=pl.CostEstimate(
                 flops=8 * rows * padded_pairs * row_length * LANES * chunks,
@@ -559,8 +565,18 @@
         )(where, gravity, stability, *[x for w in ws for x in w], *legs, start, *patches)
 
     made, turn = [], where
+    everything = tuple(range(slots))
+    halved = direct and trajectories % 2 == 0
     for k in range(chunk_count):
-        made.append(list(forward(k, turn)))
+        if k == 0 and halved:
+            near = everything[: slots // 2]
+            far = everything[slots // 2 :]
+            first = list(forward(k, turn, far, trajectories // 2))
+            turn, first[0] = lax.optimization_barrier((where, first[0]))
+            second = list(forward(k, turn, near, trajectories // 2))
+            made.append(second + first)
+        else:
+            made.append(list(forward(k, turn, everything, trajectories)))
         turn, made[-1][0] = lax.optimization_barrier((where, made[-1][0]))
     kept = [x[-1] for x in made[1:]]
     sent = []
@@ -580,8 +596,10 @@
     for k in range(chunk_count):
         got = grid(k, sent[k])
         back.append(collect(got))
-    start = inverse(back[:1], [columns], state, fresh)
-    out = inverse(back[1:], kept, start, [])
+    start = inverse(back[:1], [columns], state, fresh, False)
+    for k in range(1, chunk_count - 1):
+        start = inverse(back[k : k + 1], kept[k - 1 : k], start, [], False)
+    out = inverse(back[-1:], kept[-1:], start, [], True)
     return out[:, :, :pairs] if extra else out
 
 

time: 381 us -> 370 us (0.971)
  the two profiles are of different devices: /device:TPU:16 before, /device:TPU:0 now
where the time goes in v6:
time: 370 us; the launch traced here: 362 us
  Pallas kernels  131 us (35%)
  starting transfers between devices  96.2 us (26%)
  waiting for transfers between devices  88 us (24%)
  other arithmetic  27.3 us (7%)
  local copies, waits for them, and re-layouts  13.5 us (4%)
  between operations  5.62 us (2%)
    ppermute x42, starting transfers between devices, swap(): got[n] = lax.ppermute(parts[n], 'space', [(d, d ^ n) for d in range(space)])  93 us
    ppermute x42, waiting for transfers between devices, swap(): got[n] = lax.ppermute(parts[n], 'space', [(d, d ^ n) for d in range(space)])  67.5 us
    pallas_call x4, Pallas kernels, forward(): pl.pallas_call(functools.partial(forward_kernel, truncation=truncation, p...  46.3 us
    pallas_call x3, Pallas kernels, grid(): pl.pallas_call(functools.partial(grid_kernel, scale=1.0 / truncation), ou...  43.3 us
    pallas_call x3, Pallas kernels, inverse(): pl.pallas_call(functools.partial(inverse_kernel, truncation=truncation, p...  38.4 us
    ppermute x2, waiting for transfers between devices, move(): return lambda v: lax.ppermute(v, 'member', [(a, b)])  20.5 us
    another operation x1, other arithmetic  15.9 us
    select_n x4, other arithmetic, share_row(): row = jnp.where(jnp.bitwise_and(differs, bit) != 0, other, row)  8.32 us
  transfers between devices with their start and end apart: 48, of which 13 were waited for; matrix products, arithmetic and copies ran while one was open for 10% of the time, Pallas kernels for 29%

profile of v6, /device:TPU:0, one launch (start us, length us, event | category | flops | bytes accessed | tf_op | source)
XLA Modules:
  0.0 362.5 jit_solution(16083224934130089296)
XLA Ops:
  6.9 22.1 %conditional.2 = (bf16[12,40,641]{2,1,0:T(8,128)(2,1)S(1)}) conditional(s32[]{:T(128)} %bitcast.4, bf16[12,40,641]{2,1,0:T(8,128)(2,1)S(1)} %get-tuple-element.200, bf16[12,40,641]{2,1,0:T(8,128)(2,1)S(1)} %get-tuple-element.200, bf16[12,40,641]{2,1,0:T(8,128)(2,1)S(1)} %get-tuple-element.200, ...), branch_computations={%region_0.0_spmd, %region_1.0_spmd, %region_2.0_spmd, %region_3.0_... | conditional | bytes 3692208 | solution.py:374
  8.3 20.5 %collective-permute-done.9 = bf16[12,40,641]{2,1,0:T(8,128)(2,1)S(1)} collective-permute-done((bf16[12,40,641]{2,1,0:T(8,128)(2,1)S(1)}, bf16[12,40,641]{2,1,0:T(8,128)(2,1)S(1)}, u32[]{:S(2)}, u32[]{:S(2)}) %collective-permute-start.9) | collective-permute-done | bytes 615392 | tf_op jit(solution)/shard_map/cond/branch_12_fun/ppermute | solution.py:371
  29.1 10.1 %forward.4 = (bf16[6,160,128]{2,1,0:T(8,128)(2,1)}, bf16[6,160,128]{2,1,0:T(8,128)(2,1)}, bf16[6,160,128]{2,1,0:T(8,128)(2,1)}, bf16[6,160,128]{2,1,0:T(8,128)(2,1)}) custom-call(s32[11]{0:T(128)} %get-tuple-element.142.where_ref, f32[4,12,40,641]{3,2,1,0:T(8,128)} %refs_9_.1, bf16[641,40,384]{2,1,0:T(8,128)(2,1)} %bitcast.26, ...), custom_call_target="tpu_custom_call" | custom-call | flops 630128640 | bytes 16777216 | tf_op jit(solution)/shard_map/forward/pallas_call | solution.py:436
  47.5 10.2 %forward.5 = (bf16[6,160,128]{2,1,0:T(8,128)(2,1)}, bf16[6,160,128]{2,1,0:T(8,128)(2,1)}, bf16[6,160,128]{2,1,0:T(8,128)(2,1)}, bf16[6,160,128]{2,1,0:T(8,128)(2,1)}) custom-call(s32[11]{0:T(128)} %get-tuple-element.142.where_ref, f32[4,12,40,641]{3,2,1,0:T(8,128)} %refs_9_.1, bf16[641,40,384]{2,1,0:T(8,128)(2,1)} %bitcast.27, ...), custom_call_target="tpu_custom_call" | custom-call | flops 630128640 | bytes 16777216 | tf_op jit(solution)/shard_map/forward/pallas_call | solution.py:436
  59.6 13.0 %forward.6 = (bf16[6,160,128]{2,1,0:T(8,128)(2,1)}, bf16[6,160,128]{2,1,0:T(8,128)(2,1)}, bf16[6,160,128]{2,1,0:T(8,128)(2,1)}, bf16[6,160,128]{2,1,0:T(8,128)(2...) custom-call(s32[11]{0:T(128)} %get-tuple-element.142.where_ref, ...), custom_call_target="tpu_custom_call" | custom-call | flops 1260257280 | bytes 16777216 | tf_op jit(solution)/shard_map/forward/pallas_call | solution.py:436
  72.6 15.9 %fusion.7 = (bf16[1280,640]{1,0:T(8,128)(2,1)S(1)}, bf16[1280,640]{1,0:T(8,128)(2,1)}) fusion(s32[1280]{0:T(1024)S(1)} %get-tuple-element.215, s32[1280]{0:T(1024)S(1)} %get-tuple-element.214, pred[1280]{0:T(1024)(128)(4,1)S(1)} %fusion.22), kind=kLoop, calls=%fused_computation.11 | loop fusion | flops 11468800 | bytes 3288320 | tf_op jit(solution)/shard_map/convert
  93.1 3.8 %dynamic-slice_bitcast_fusion = (f32[12,40,641]{2,1,0:T(8,128)}, f32[12,40,641]{2,1,0:T(8,128)}) fusion(f32[4,12,40,641]{3,2,1,0:T(8,128)} %refs_9_.1, s32[]{:T(128)S(6)} %select_n.193, s32[]{:T(128)S(6)} %select_n.188), kind=kLoop, calls=%fused_computation.12 | loop fusion | bytes 4922888 | tf_op jit(solution)/shard_map/jit(dynamic_index_in_dim)/squeeze | solution.py:588
  106.4 13.0 %forward.7 = (bf16[6,160,128]{2,1,0:T(8,128)(2,1)}, bf16[6,160,128]{2,1,0:T(8,128)(2,1)}, bf16[6,160,128]{2,1,0:T(8,128)(2,1)}, bf16[6,160,128]{2,1,0:T(8,128)(2...) custom-call(s32[11]{0:T(128)} %get-tuple-element.142.where_ref, ...), custom_call_target="tpu_custom_call" | custom-call | flops 1260257280 | bytes 16777216 | tf_op jit(solution)/shard_map/forward/pallas_call | solution.py:436
  127.6 5.7 %copy.7.syn_ref = bf16[1280,1280]{1,0:T(8,128)(2,1)} copy(bf16[1280,1280]{0,1:T(8,128)(2,1)} %bitcast.31) | data formatting | bytes 6553600 | tf_op jit(solution)/shard_map/transpose | solution.py:497
  133.9 11.1 %collective-permute-done.41.refs_4_ = bf16[6,160,128]{2,1,0:T(8,128)(2,1)S(1)} collective-permute-done((bf16[6,160,128]{2,1,0:T(8,128)(2,1)S(1)}, bf16[6,160,128]{2,1,0:T(8,128)(2,1)S(1)}, u32[]{:S(2)}, u32[]{:S(2)}) %collective-permute-start.41) | collective-permute-done | bytes 245792 | tf_op jit(solution)/shard_map/ppermute | solution.py:478
  148.3 8.3 %collective-permute-done.42.refs_5_ = bf16[6,160,128]{2,1,0:T(8,128)(2,1)S(1)} collective-permute-done((bf16[6,160,128]{2,1,0:T(8,128)(2,1)S(1)}, bf16[6,160,128]{2,1,0:T(8,128)(2,1)S(1)}, u32[]{:S(2)}, u32[]{:S(2)}) %collective-permute-start.42) | collective-permute-done | bytes 245792 | tf_op jit(solution)/shard_map/ppermute | solution.py:478
  157.0 4.4 %collective-permute-start.25 = (bf16[6,160,128]{2,1,0:T(8,128)(2,1)S(1)}, bf16[6,160,128]{2,1,0:T(8,128)(2,1)S(1)}, u32[]{:S(2)}, u32[]{:S(2)}) collective-permute-start(bf16[6,160,128]{2,1,0:T(8,128)(2,1)S(1)} %copy-done.41), channel_id=1, source_target_pairs={{0,2},{1,3},{2,0},{3,1},{4,6},{5,7},{6,4},{7,5},{8,10},{9,11},{10,... | collective-permute-start | bytes 737288 | tf_op jit(solution)/shard_map/ppermute | solution.py:478
  161.4 14.6 %grid.5 = (bf16[6,160,128]{2,1,0:T(8,128)(2,1)}, bf16[6,160,128]{2,1,0:T(8,128)(2,1)}, bf16[6,160,128]{2,1,0:T(8,128)(2,1)}, bf16[6,160,128]{2,1,0:T(8,128)(2,1)...) custom-call(s32[8]{0:T(128)} %iota_xor_fusion.order_ref, ...), custom_call_target="tpu_custom_call" | custom-call | flops 5033164800 | bytes 12582912 | tf_op jit(solution)/shard_map/grid/pallas_call | solution.py:512
  185.4 4.5 %collective-permute-done.26.refs_3_ = bf16[6,160,128]{2,1,0:T(8,128)(2,1)S(1)} collective-permute-done((bf16[6,160,128]{2,1,0:T(8,128)(2,1)S(1)}, bf16[6,160,128]{2,1,0:T(8,128)(2,1)S(1)}, u32[]{:S(2)}, u32[]{:S(2)}) %collective-permute-start.26) | collective-permute-done | bytes 245792 | tf_op jit(solution)/shard_map/ppermute | solution.py:478
  191.1 17.7 %collective-permute-done.27.refs_4_ = bf16[6,160,128]{2,1,0:T(8,128)(2,1)S(1)} collective-permute-done((bf16[6,160,128]{2,1,0:T(8,128)(2,1)S(1)}, bf16[6,160,128]{2,1,0:T(8,128)(2,1)S(1)}, u32[]{:S(2)}, u32[]{:S(2)}) %collective-permute-start.27) | collective-permute-done | bytes 245792 | tf_op jit(solution)/shard_map/ppermute | solution.py:478
  209.2 4.7 %collective-permute-done.28.refs_5_ = bf16[6,160,128]{2,1,0:T(8,128)(2,1)S(1)} collective-permute-done((bf16[6,160,128]{2,1,0:T(8,128)(2,1)S(1)}, bf16[6,160,128]{2,1,0:T(8,128)(2,1)S(1)}, u32[]{:S(2)}, u32[]{:S(2)}) %collective-permute-start.28) | collective-permute-done | bytes 245792 | tf_op jit(solution)/shard_map/ppermute | solution.py:478
  214.0 5.8 %collective-permute-start.61 = (bf16[6,160,128]{2,1,0:T(8,128)(2,1)S(1)}, bf16[6,160,128]{2,1,0:T(8,128)(2,1)}, u32[]{:S(2)}, u32[]{:S(2)}) collective-permute-start(bf16[6,160,128]{2,1,0:T(8,128)(2,1)S(1)} %copy-done.43), channel_id=1, source_target_pairs={{0,3},{1,2},{2,1},{3,0},{4,7},{5,6},{6,5},{7,4},{8,11},{9,10},{10,... | collective-permute-start | bytes 737288 | tf_op jit(solution)/shard_map/ppermute | solution.py:478
  222.5 6.3 %collective-permute-start.62 = (bf16[6,160,128]{2,1,0:T(8,128)(2,1)}, bf16[6,160,128]{2,1,0:T(8,128)(2,1)S(1)}, u32[]{:S(2)}, u32[]{:S(2)}) collective-permute-start(bf16[6,160,128]{2,1,0:T(8,128)(2,1)} %get-tuple-element.190), channel_id=1, source_target_pairs={{0,4},{1,5},{2,6},{3,7},{4,0},{5,1},{6,2},{7,3},{8,12},{9,13},{10,... | collective-permute-start | bytes 737288 | tf_op jit(solution)/shard_map/ppermute | solution.py:478
  230.8 14.4 %grid.4 = (bf16[6,160,128]{2,1,0:T(8,128)(2,1)}, bf16[6,160,128]{2,1,0:T(8,128)(2,1)}, bf16[6,160,128]{2,1,0:T(8,128)(2,1)}, bf16[6,160,128]{2,1,0:T(8,128)(2,1)...) custom-call(s32[8]{0:T(128)} %iota_xor_fusion.order_ref, ...), custom_call_target="tpu_custom_call" | custom-call | flops 5033164800 | bytes 12582912 | tf_op jit(solution)/shard_map/grid/pallas_call | solution.py:512
  245.2 4.9 %collective-permute-done.62.refs_4_ = bf16[6,160,128]{2,1,0:T(8,128)(2,1)S(1)} collective-permute-done((bf16[6,160,128]{2,1,0:T(8,128)(2,1)}, bf16[6,160,128]{2,1,0:T(8,128)(2,1)S(1)}, u32[]{:S(2)}, u32[]{:S(2)}) %collective-permute-start.62) | collective-permute-done | bytes 245792 | tf_op jit(solution)/shard_map/ppermute | solution.py:478
  252.7 7.7 %collective-permute-done.63.refs_5_ = bf16[6,160,128]{2,1,0:T(8,128)(2,1)} collective-permute-done((bf16[6,160,128]{2,1,0:T(8,128)(2,1)}, bf16[6,160,128]{2,1,0:T(8,128)(2,1)}, u32[]{:S(2)}, u32[]{:S(2)}) %collective-permute-start.63) | collective-permute-done | bytes 245792 | tf_op jit(solution)/shard_map/ppermute | solution.py:478
  262.2 4.4 %collective-permute-start.46 = (bf16[6,160,128]{2,1,0:T(8,128)(2,1)}, bf16[6,160,128]{2,1,0:T(8,128)(2,1)}, u32[]{:S(2)}, u32[]{:S(2)}) collective-permute-start(bf16[6,160,128]{2,1,0:T(8,128)(2,1)} %get-tuple-element.171), channel_id=1, source_target_pairs={{0,2},{1,3},{2,0},{3,1},{4,6},{5,7},{6,4},{7,5},{8,10},{9,11},{10,... | collective-permute-start | bytes 737288 | tf_op jit(solution)/shard_map/ppermute | solution.py:478
  266.5 4.5 %collective-permute-start.47 = (bf16[6,160,128]{2,1,0:T(8,128)(2,1)}, bf16[6,160,128]{2,1,0:T(8,128)(2,1)S(1)}, u32[]{:S(2)}, u32[]{:S(2)}) collective-permute-start(bf16[6,160,128]{2,1,0:T(8,128)(2,1)} %get-tuple-element.172), channel_id=1, source_target_pairs={{0,3},{1,2},{2,1},{3,0},{4,7},{5,6},{6,5},{7,4},{8,11},{9,10},{10,... | collective-permute-start | bytes 737288 | tf_op jit(solution)/shard_map/ppermute | solution.py:478
  272.5 7.0 %collective-permute-start.49 = (bf16[6,160,128]{2,1,0:T(8,128)(2,1)}, bf16[6,160,128]{2,1,0:T(8,128)(2,1)}, u32[]{:S(2)}, u32[]{:S(2)}) collective-permute-start(bf16[6,160,128]{2,1,0:T(8,128)(2,1)} %get-tuple-element.174), channel_id=1, source_target_pairs={{0,5},{1,4},{2,7},{3,6},{4,1},{5,0},{6,3},{7,2},{8,13},{9,12},{10,... | collective-permute-start | bytes 737288 | tf_op jit(solution)/shard_map/ppermute | solution.py:478
  279.5 14.3 %grid.3 = (bf16[6,160,128]{2,1,0:T(8,128)(2,1)}, bf16[6,160,128]{2,1,0:T(8,128)(2,1)}, bf16[6,160,128]{2,1,0:T(8,128)(2,1)}, bf16[6,160,128]{2,1,0:T(8,128)(2,1)...) custom-call(s32[8]{0:T(128)} %iota_xor_fusion.order_ref, ...), custom_call_target="tpu_custom_call" | custom-call | flops 5033164800 | bytes 12582912 | tf_op jit(solution)/shard_map/grid/pallas_call | solution.py:512
  299.1 3.7 %collective-permute-done.49.refs_5_ = bf16[6,160,128]{2,1,0:T(8,128)(2,1)} collective-permute-done((bf16[6,160,128]{2,1,0:T(8,128)(2,1)}, bf16[6,160,128]{2,1,0:T(8,128)(2,1)}, u32[]{:S(2)}, u32[]{:S(2)}) %collective-permute-start.49) | collective-permute-done | bytes 245792 | tf_op jit(solution)/shard_map/ppermute | solution.py:478
  309.0 3.9 %collective-permute-start.33 = (bf16[6,160,128]{2,1,0:T(8,128)(2,1)}, bf16[6,160,128]{2,1,0:T(8,128)(2,1)S(1)}, u32[]{:S(2)}, u32[]{:S(2)}) collective-permute-start(bf16[6,160,128]{2,1,0:T(8,128)(2,1)} %get-tuple-element.155), channel_id=1, source_target_pairs={{0,3},{1,2},{2,1},{3,0},{4,7},{5,6},{6,5},{7,4},{8,11},{9,10},{10,... | collective-permute-start | bytes 737288 | tf_op jit(solution)/shard_map/ppermute | solution.py:478
  312.8 3.9 %collective-permute-start.34 = (bf16[6,160,128]{2,1,0:T(8,128)(2,1)}, bf16[6,160,128]{2,1,0:T(8,128)(2,1)S(1)}, u32[]{:S(2)}, u32[]{:S(2)}) collective-permute-start(bf16[6,160,128]{2,1,0:T(8,128)(2,1)} %get-tuple-element.156), channel_id=1, source_target_pairs={{0,4},{1,5},{2,6},{3,7},{4,0},{5,1},{6,2},{7,3},{8,12},{9,13},{10,... | collective-permute-start | bytes 737288 | tf_op jit(solution)/shard_map/ppermute | solution.py:478
  316.7 4.7 %collective-permute-start.36 = (bf16[6,160,128]{2,1,0:T(8,128)(2,1)}, bf16[6,160,128]{2,1,0:T(8,128)(2,1)S(1)}, u32[]{:S(2)}, u32[]{:S(2)}) collective-permute-start(bf16[6,160,128]{2,1,0:T(8,128)(2,1)} %get-tuple-element.158), channel_id=1, source_target_pairs={{0,6},{1,7},{2,4},{3,5},{4,2},{5,3},{6,0},{7,1},{8,14},{9,15},{10,... | collective-permute-start | bytes 737288 | tf_op jit(solution)/shard_map/ppermute | solution.py:478
  322.9 14.5 %inverse.3.refs_9_ = f32[4,12,40,641]{3,2,1,0:T(8,128)} custom-call(s32[11]{0:T(128)} %get-tuple-element.142.where_ref, f32[2,2]{1,0:T(2,128)} %gravity_ref.5, f32[2,2]{1,0:T(2,128)} %stability_ref.5, bf16[6,160,128]{2,1,0:T(8,128)(2,1)} %get-tuple-element.186.refs_0_, bf16[6,160,128]{2,1,0:T(8,128)(2,1)} %copy-done.2, bf16[6,160,128]{2,1,0:T(8,128)(2,1)} %copy-done.3, ...), custom_call_target="tpu_custom_call" | custom-call | flops 1260257280 | bytes 20971520 | tf_op jit(solution)/shard_map/inverse/pallas_call | solution.py:534
  337.4 11.7 %inverse.4.refs_9_ = f32[4,12,40,641]{3,2,1,0:T(8,128)} custom-call(s32[11]{0:T(128)} %get-tuple-element.142.where_ref, f32[2,2]{1,0:T(2,128)} %gravity_ref.5, f32[2,2]{1,0:T(2,128)} %stability_ref.5, bf16[6,160,128]{2,1,0:T(8,128)(2,1)} %get-tuple-element.169.refs_0_, bf16[6,160,128]{2,1,0:T(8,128)(2,1)} %copy-done.6, ...), custom_call_target="tpu_custom_call" | custom-call | flops 1260257280 | bytes 20971520 | tf_op jit(solution)/shard_map/inverse/pallas_call | solution.py:534
  350.2 12.3 %inverse.5 = f32[4,12,40,641]{3,2,1,0:T(8,128)} custom-call(s32[11]{0:T(128)} %get-tuple-element.142.where_ref, f32[2,2]{1,0:T(2,128)} %gravity_ref.5, f32[2,2]{1,0:T(2,128)} %stability_ref.5, bf16[6,160,128]{2,1,0:T(8,128)(2,1)} %get-tuple-element.152.refs_0_, bf16[6,160,128]{2,1,0:T(8,128)(2,1)} %copy-done.9, bf16[6,160,128]{2,1,0:T(8,128)(2,1)} %copy-done.10, ...), custom_call_target="tpu_custom_call" | custom-call | flops 1260257280 | bytes 20971520 | tf_op jit(solution)/shard_map/inverse/pallas_call | solution.py:534
  (187 shorter events, 76.3 us)
Async XLA Ops:
  7.0 21.8 %collective-permute-start.9 = (bf16[12,40,641]{2,1,0:T(8,128)(2,1)S(1)}, bf16[12,40,641]{2,1,0:T(8,128)(2,1)S(1)}, u32[]{:S(2)}, u32[]{:S(2)}) collective-permute-start(bf16[12,40,641]{2,1,0:T(8,128)(2,1)S(1)} %param.12), channel_id=1, source_target_pairs={{24,0},{25,1},{26,2},{27,3},{28,4},{29,5},{30,6},{31,7}} | collective-permute-start | bytes 1846088 | tf_op jit(solution)/shard_map/cond/branch_12_fun/ppermute | solution.py:371
  39.2 57.7 %collective-permute-start.55 = (bf16[6,160,128]{2,1,0:T(8,128)(2,1)}, bf16[6,160,128]{2,1,0:T(8,128)(2,1)S(1)}, u32[]{:S(2)}, u32[]{:S(2)}) collective-permute-start(bf16[6,160,128]{2,1,0:T(8,128)(2,1)} %get-tuple-element.182), channel_id=1, source_target_pairs={{0,4},{1,5},{2,6},{3,7},{4,0},{5,1},{6,2},{7,3},{8,12},{9,13},{10,... | collective-permute-start | bytes 737288 | tf_op jit(solution)/shard_map/ppermute | solution.py:478
  42.6 54.2 %collective-permute-start.56 = (bf16[6,160,128]{2,1,0:T(8,128)(2,1)}, bf16[6,160,128]{2,1,0:T(8,128)(2,1)}, u32[]{:S(2)}, u32[]{:S(2)}) collective-permute-start(bf16[6,160,128]{2,1,0:T(8,128)(2,1)} %get-tuple-element.183), channel_id=1, source_target_pairs={{0,5},{1,4},{2,7},{3,6},{4,1},{5,0},{6,3},{7,2},{8,13},{9,12},{10,... | collective-permute-start | bytes 737288 | tf_op jit(solution)/shard_map/ppermute | solution.py:478
  43.9 54.9 %collective-permute-start.57 = (bf16[6,160,128]{2,1,0:T(8,128)(2,1)}, bf16[6,160,128]{2,1,0:T(8,128)(2,1)}, u32[]{:S(2)}, u32[]{:S(2)}) collective-permute-start(bf16[6,160,128]{2,1,0:T(8,128)(2,1)} %get-tuple-element.184), channel_id=1, source_target_pairs={{0,6},{1,7},{2,4},{3,5},{4,2},{5,3},{6,0},{7,1},{8,14},{9,15},{10,... | collective-permute-start | bytes 737288 | tf_op jit(solution)/shard_map/ppermute | solution.py:478
  47.5 53.2 %collective-permute-start.58 = (bf16[6,160,128]{2,1,0:T(8,128)(2,1)}, bf16[6,160,128]{2,1,0:T(8,128)(2,1)}, u32[]{:S(2)}, u32[]{:S(2)}) collective-permute-start(bf16[6,160,128]{2,1,0:T(8,128)(2,1)} %get-tuple-element.185), channel_id=1, source_target_pairs={{0,7},{1,6},{2,5},{3,4},{4,3},{5,2},{6,1},{7,0},{8,15},{9,14},{10,... | collective-permute-start | bytes 737288 | tf_op jit(solution)/shard_map/ppermute | solution.py:478
  57.7 44.6 %collective-permute-start.52 = (bf16[6,160,128]{2,1,0:T(8,128)(2,1)}, bf16[6,160,128]{2,1,0:T(8,128)(2,1)}, u32[]{:S(2)}, u32[]{:S(2)}) collective-permute-start(bf16[6,160,128]{2,1,0:T(8,128)(2,1)} %get-tuple-element.179), channel_id=1, source_target_pairs={{0,1},{1,0},{2,3},{3,2},{4,5},{5,4},{6,7},{7,6},{8,9},{9,8},{10,11... | collective-permute-start | bytes 737288 | tf_op jit(solution)/shard_map/ppermute | solution.py:478
  98.7 82.1 %collective-permute-start.68 = (f32[12,40,641]{2,1,0:T(8,128)}, f32[12,40,641]{2,1,0:T(8,128)}, u32[]{:S(2)}, u32[]{:S(2)}) collective-permute-start(f32[12,40,641]{2,1,0:T(8,128)} %get-tuple-element.197), channel_id=1, source_target_pairs={{0,8},{8,0},{16,24},{24,16},{1,9},{9,1},{17,25},{25,17},{2,10},{10... | collective-permute-start | bytes 3692168 | tf_op jit(solution)/shard_map/ppermute | solution.py:382
  103.4 20.1 %collective-permute-start.40 = (bf16[6,160,128]{2,1,0:T(8,128)(2,1)}, bf16[6,160,128]{2,1,0:T(8,128)(2,1)}, u32[]{:S(2)}, u32[]{:S(2)}) collective-permute-start(bf16[6,160,128]{2,1,0:T(8,128)(2,1)} %get-tuple-element.164), channel_id=1, source_target_pairs={{0,3},{1,2},{2,1},{3,0},{4,7},{5,6},{6,5},{7,4},{8,11},{9,10},{10,... | collective-permute-start | bytes 737288 | tf_op jit(solution)/shard_map/ppermute | solution.py:478
  106.4 113.3 %collective-permute-start.66 = (f32[12,40,641]{2,1,0:T(8,128)}, f32[12,40,641]{2,1,0:T(8,128)}, u32[]{:S(2)}, u32[]{:S(2)}) collective-permute-start(f32[12,40,641]{2,1,0:T(8,128)} %get-tuple-element.198), channel_id=1, source_target_pairs={{0,8},{8,0},{16,24},{24,16},{1,9},{9,1},{17,25},{25,17},{2,10},{10... | collective-permute-start | bytes 3692168 | tf_op jit(solution)/shard_map/ppermute | solution.py:382
  119.4 25.6 %collective-permute-start.41 = (bf16[6,160,128]{2,1,0:T(8,128)(2,1)S(1)}, bf16[6,160,128]{2,1,0:T(8,128)(2,1)S(1)}, u32[]{:S(2)}, u32[]{:S(2)}) collective-permute-start(bf16[6,160,128]{2,1,0:T(8,128)(2,1)S(1)} %copy-done.24), channel_id=1, source_target_pairs={{0,4},{1,5},{2,6},{3,7},{4,0},{5,1},{6,2},{7,3},{8,12},{9,13},{10,... | collective-permute-start | bytes 737288 | tf_op jit(solution)/shard_map/ppermute | solution.py:478
  122.2 34.4 %collective-permute-start.42 = (bf16[6,160,128]{2,1,0:T(8,128)(2,1)S(1)}, bf16[6,160,128]{2,1,0:T(8,128)(2,1)S(1)}, u32[]{:S(2)}, u32[]{:S(2)}) collective-permute-start(bf16[6,160,128]{2,1,0:T(8,128)(2,1)S(1)} %copy-done.23), channel_id=1, source_target_pairs={{0,5},{1,4},{2,7},{3,6},{4,1},{5,0},{6,3},{7,2},{8,13},{9,12},{10,... | collective-permute-start | bytes 737288 | tf_op jit(solution)/shard_map/ppermute | solution.py:478
  123.5 33.5 %collective-permute-start.43 = (bf16[6,160,128]{2,1,0:T(8,128)(2,1)S(1)}, bf16[6,160,128]{2,1,0:T(8,128)(2,1)S(1)}, u32[]{:S(2)}, u32[]{:S(2)}) collective-permute-start(bf16[6,160,128]{2,1,0:T(8,128)(2,1)S(1)} %copy-done.22), channel_id=1, source_target_pairs={{0,6},{1,7},{2,4},{3,5},{4,2},{5,3},{6,0},{7,1},{8,14},{9,15},{10,... | collective-permute-start | bytes 737288 | tf_op jit(solution)/shard_map/ppermute | solution.py:478
  145.0 31.1 %collective-permute-start.44 = (bf16[6,160,128]{2,1,0:T(8,128)(2,1)S(1)}, bf16[6,160,128]{2,1,0:T(8,128)(2,1)S(1)}, u32[]{:S(2)}, u32[]{:S(2)}) collective-permute-start(bf16[6,160,128]{2,1,0:T(8,128)(2,1)S(1)} %copy-done.21), channel_id=1, source_target_pairs={{0,7},{1,6},{2,5},{3,4},{4,3},{5,2},{6,1},{7,0},{8,15},{9,14},{10,... | collective-permute-start | bytes 737288 | tf_op jit(solution)/shard_map/ppermute | solution.py:478
  156.6 21.3 %collective-permute-start.24 = (bf16[6,160,128]{2,1,0:T(8,128)(2,1)S(1)}, bf16[6,160,128]{2,1,0:T(8,128)(2,1)S(1)}, u32[]{:S(2)}, u32[]{:S(2)}) collective-permute-start(bf16[6,160,128]{2,1,0:T(8,128)(2,1)S(1)} %copy-done.42), channel_id=1, source_target_pairs={{0,1},{1,0},{2,3},{3,2},{4,5},{5,4},{6,7},{7,6},{8,9},{9,8},{10,11... | collective-permute-start | bytes 737288 | tf_op jit(solution)/shard_map/ppermute | solution.py:478
  157.0 23.1 %collective-permute-start.25 = (bf16[6,160,128]{2,1,0:T(8,128)(2,1)S(1)}, bf16[6,160,128]{2,1,0:T(8,128)(2,1)S(1)}, u32[]{:S(2)}, u32[]{:S(2)}) collective-permute-start(bf16[6,160,128]{2,1,0:T(8,128)(2,1)S(1)} %copy-done.41), channel_id=1, source_target_pairs={{0,2},{1,3},{2,0},{3,1},{4,6},{5,7},{6,4},{7,5},{8,10},{9,11},{10,... | collective-permute-start | bytes 737288 | tf_op jit(solution)/shard_map/ppermute | solution.py:478
  177.9 30.9 %collective-permute-start.27 = (bf16[6,160,128]{2,1,0:T(8,128)(2,1)S(1)}, bf16[6,160,128]{2,1,0:T(8,128)(2,1)S(1)}, u32[]{:S(2)}, u32[]{:S(2)}) collective-permute-start(bf16[6,160,128]{2,1,0:T(8,128)(2,1)S(1)} %copy-done.38), channel_id=1, source_target_pairs={{0,4},{1,5},{2,6},{3,7},{4,0},{5,1},{6,2},{7,3},{8,12},{9,13},{10,... | collective-permute-start | bytes 737288 | tf_op jit(solution)/shard_map/ppermute | solution.py:478
  180.1 33.8 %collective-permute-start.28 = (bf16[6,160,128]{2,1,0:T(8,128)(2,1)S(1)}, bf16[6,160,128]{2,1,0:T(8,128)(2,1)S(1)}, u32[]{:S(2)}, u32[]{:S(2)}) collective-permute-start(bf16[6,160,128]{2,1,0:T(8,128)(2,1)S(1)} %copy-done.36), channel_id=1, source_target_pairs={{0,5},{1,4},{2,7},{3,6},{4,1},{5,0},{6,3},{7,2},{8,13},{9,12},{10,... | collective-permute-start | bytes 737288 | tf_op jit(solution)/shard_map/ppermute | solution.py:478
  180.9 33.0 %collective-permute-start.29 = (bf16[6,160,128]{2,1,0:T(8,128)(2,1)S(1)}, bf16[6,160,128]{2,1,0:T(8,128)(2,1)S(1)}, u32[]{:S(2)}, u32[]{:S(2)}) collective-permute-start(bf16[6,160,128]{2,1,0:T(8,128)(2,1)S(1)} %copy-done.34), channel_id=1, source_target_pairs={{0,6},{1,7},{2,4},{3,5},{4,2},{5,3},{6,0},{7,1},{8,14},{9,15},{10,... | collective-permute-start | bytes 737288 | tf_op jit(solution)/shard_map/ppermute | solution.py:478
  190.0 32.5 %collective-permute-start.30 = (bf16[6,160,128]{2,1,0:T(8,128)(2,1)S(1)}, bf16[6,160,128]{2,1,0:T(8,128)(2,1)S(1)}, u32[]{:S(2)}, u32[]{:S(2)}) collective-permute-start(bf16[6,160,128]{2,1,0:T(8,128)(2,1)S(1)} %copy-done.31), channel_id=1, source_target_pairs={{0,7},{1,6},{2,5},{3,4},{4,3},{5,2},{6,1},{7,0},{8,15},{9,14},{10,... | collective-permute-start | bytes 737288 | tf_op jit(solution)/shard_map/ppermute | solution.py:478
  219.8 86.5 %collective-permute-start.69 = (f32[12,40,641]{2,1,0:T(8,128)S(1)}, f32[12,40,641]{2,1,0:T(8,128)}, u32[]{:S(2)}, u32[]{:S(2)}) collective-permute-start(f32[12,40,641]{2,1,0:T(8,128)S(1)} %broadcast_select_fusion), channel_id=1, source_target_pairs={{0,16},{8,24},{16,0},{24,8},{1,17},{9,25},{17,1},{25,9},{2,18},{10... | collective-permute-start | bytes 3692168 | tf_op jit(solution)/shard_map/ppermute | solution.py:382
  222.5 27.5 %collective-permute-start.62 = (bf16[6,160,128]{2,1,0:T(8,128)(2,1)}, bf16[6,160,128]{2,1,0:T(8,128)(2,1)S(1)}, u32[]{:S(2)}, u32[]{:S(2)}) collective-permute-start(bf16[6,160,128]{2,1,0:T(8,128)(2,1)} %get-tuple-element.190), channel_id=1, source_target_pairs={{0,4},{1,5},{2,6},{3,7},{4,0},{5,1},{6,2},{7,3},{8,12},{9,13},{10,... | collective-permute-start | bytes 737288 | tf_op jit(solution)/shard_map/ppermute | solution.py:478
  228.8 31.5 %collective-permute-start.63 = (bf16[6,160,128]{2,1,0:T(8,128)(2,1)}, bf16[6,160,128]{2,1,0:T(8,128)(2,1)}, u32[]{:S(2)}, u32[]{:S(2)}) collective-permute-start(bf16[6,160,128]{2,1,0:T(8,128)(2,1)} %get-tuple-element.191), channel_id=1, source_target_pairs={{0,5},{1,4},{2,7},{3,6},{4,1},{5,0},{6,3},{7,2},{8,13},{9,12},{10,... | collective-permute-start | bytes 737288 | tf_op jit(solution)/shard_map/ppermute | solution.py:478
  228.8 33.3 %collective-permute-start.64 = (bf16[6,160,128]{2,1,0:T(8,128)(2,1)}, bf16[6,160,128]{2,1,0:T(8,128)(2,1)}, u32[]{:S(2)}, u32[]{:S(2)}) collective-permute-start(bf16[6,160,128]{2,1,0:T(8,128)(2,1)} %get-tuple-element.192), channel_id=1, source_target_pairs={{0,6},{1,7},{2,4},{3,5},{4,2},{5,3},{6,0},{7,1},{8,14},{9,15},{10,... | collective-permute-start | bytes 737288 | tf_op jit(solution)/shard_map/ppermute | solution.py:478
  229.6 91.9 %collective-permute-start.67 = (f32[12,40,641]{2,1,0:T(8,128)}, f32[12,40,641]{2,1,0:T(8,128)S(1)}, u32[]{:S(2)}, u32[]{:S(2)}) collective-permute-start(f32[12,40,641]{2,1,0:T(8,128)} %broadcast_select_fusion.2), channel_id=1, source_target_pairs={{0,16},{8,24},{16,0},{24,8},{1,17},{9,25},{17,1},{25,9},{2,18},{10... | collective-permute-start | bytes 3692168 | tf_op jit(solution)/shard_map/ppermute | solution.py:382
  266.5 27.3 %collective-permute-start.47 = (bf16[6,160,128]{2,1,0:T(8,128)(2,1)}, bf16[6,160,128]{2,1,0:T(8,128)(2,1)S(1)}, u32[]{:S(2)}, u32[]{:S(2)}) collective-permute-start(bf16[6,160,128]{2,1,0:T(8,128)(2,1)} %get-tuple-element.172), channel_id=1, source_target_pairs={{0,3},{1,2},{2,1},{3,0},{4,7},{5,6},{6,5},{7,4},{8,11},{9,10},{10,... | collective-permute-start | bytes 737288 | tf_op jit(solution)/shard_map/ppermute | solution.py:478
  271.0 25.7 %collective-permute-start.48 = (bf16[6,160,128]{2,1,0:T(8,128)(2,1)}, bf16[6,160,128]{2,1,0:T(8,128)(2,1)S(1)}, u32[]{:S(2)}, u32[]{:S(2)}) collective-permute-start(bf16[6,160,128]{2,1,0:T(8,128)(2,1)} %get-tuple-element.173), channel_id=1, source_target_pairs={{0,4},{1,5},{2,6},{3,7},{4,0},{5,1},{6,2},{7,3},{8,12},{9,13},{10,... | collective-permute-start | bytes 737288 | tf_op jit(solution)/shard_map/ppermute | solution.py:478
  272.5 30.3 %collective-permute-start.49 = (bf16[6,160,128]{2,1,0:T(8,128)(2,1)}, bf16[6,160,128]{2,1,0:T(8,128)(2,1)}, u32[]{:S(2)}, u32[]{:S(2)}) collective-permute-start(bf16[6,160,128]{2,1,0:T(8,128)(2,1)} %get-tuple-element.174), channel_id=1, source_target_pairs={{0,5},{1,4},{2,7},{3,6},{4,1},{5,0},{6,3},{7,2},{8,13},{9,12},{10,... | collective-permute-start | bytes 737288 | tf_op jit(solution)/shard_map/ppermute | solution.py:478
  309.0 40.1 %collective-permute-start.33 = (bf16[6,160,128]{2,1,0:T(8,128)(2,1)}, bf16[6,160,128]{2,1,0:T(8,128)(2,1)S(1)}, u32[]{:S(2)}, u32[]{:S(2)}) collective-permute-start(bf16[6,160,128]{2,1,0:T(8,128)(2,1)} %get-tuple-element.155), channel_id=1, source_target_pairs={{0,3},{1,2},{2,1},{3,0},{4,7},{5,6},{6,5},{7,4},{8,11},{9,10},{10,... | collective-permute-start | bytes 737288 | tf_op jit(solution)/shard_map/ppermute | solution.py:478
  312.8 36.3 %collective-permute-start.34 = (bf16[6,160,128]{2,1,0:T(8,128)(2,1)}, bf16[6,160,128]{2,1,0:T(8,128)(2,1)S(1)}, u32[]{:S(2)}, u32[]{:S(2)}) collective-permute-start(bf16[6,160,128]{2,1,0:T(8,128)(2,1)} %get-tuple-element.156), channel_id=1, source_target_pairs={{0,4},{1,5},{2,6},{3,7},{4,0},{5,1},{6,2},{7,3},{8,12},{9,13},{10,... | collective-permute-start | bytes 737288 | tf_op jit(solution)/shard_map/ppermute | solution.py:478
  316.7 32.6 %collective-permute-start.35 = (bf16[6,160,128]{2,1,0:T(8,128)(2,1)}, bf16[6,160,128]{2,1,0:T(8,128)(2,1)S(1)}, u32[]{:S(2)}, u32[]{:S(2)}) collective-permute-start(bf16[6,160,128]{2,1,0:T(8,128)(2,1)} %get-tuple-element.157), channel_id=1, source_target_pairs={{0,5},{1,4},{2,7},{3,6},{4,1},{5,0},{6,3},{7,2},{8,13},{9,12},{10,... | collective-permute-start | bytes 737288 | tf_op jit(solution)/shard_map/ppermute | solution.py:478
  316.7 32.6 %collective-permute-start.36 = (bf16[6,160,128]{2,1,0:T(8,128)(2,1)}, bf16[6,160,128]{2,1,0:T(8,128)(2,1)S(1)}, u32[]{:S(2)}, u32[]{:S(2)}) collective-permute-start(bf16[6,160,128]{2,1,0:T(8,128)(2,1)} %get-tuple-element.158), channel_id=1, source_target_pairs={{0,6},{1,7},{2,4},{3,5},{4,2},{5,3},{6,0},{7,1},{8,14},{9,15},{10,... | collective-permute-start | bytes 737288 | tf_op jit(solution)/shard_map/ppermute | solution.py:478
  321.4 27.9 %collective-permute-start.37 = (bf16[6,160,128]{2,1,0:T(8,128)(2,1)}, bf16[6,160,128]{2,1,0:T(8,128)(2,1)S(1)}, u32[]{:S(2)}, u32[]{:S(2)}) collective-permute-start(bf16[6,160,128]{2,1,0:T(8,128)(2,1)} %get-tuple-element.159), channel_id=1, source_target_pairs={{0,7},{1,6},{2,5},{3,4},{4,3},{5,2},{6,1},{7,0},{8,15},{9,14},{10,... | collective-permute-start | bytes 737288 | tf_op jit(solution)/shard_map/ppermute | solution.py:478
  (62 other events, 1018.2 us)
